TPU v7x, 32 devices: a whole 2x2x4 slice. The times are simulated.
32 devices in a mesh: fsdp: 16 (over z, y, core), seq: 2 (over x).
Axes of the slice: x: 2, y: 2, z: 4, core: 2. Of those that a mesh axis runs over, the one named last changes fastest.
Arguments:
- inputs: bfloat16 [16, 2048, 1024], P('fsdp', 'seq'), may hold values from -6 to 6
- cotangent: bfloat16 [16, 2048, 1024], P('fsdp', 'seq'), may hold values from -6 to 6
- lengths: int32 [16, 16], P('fsdp'), may hold values from 1 to 1024, 2048 in all within a row
- norm_gains: float32 [2, 1024], replicated, may hold values from 0.5 to 1.5
- norm_first: float32 [2, 1024], replicated, may hold values from -128 to 128
- norm_second: float32 [2, 1024], replicated, may hold values from 851.968 to 13762.56
- qk_gains: float32 [2, 64], replicated, may hold values from 0.5 to 1.5
- qk_first: float32 [2, 64], replicated, may hold values from -256 to 256
- qk_second: float32 [2, 64], replicated, may hold values from 3276.8 to 55705.6
- qkv_master: float32 [1024, 2048], P(('fsdp', 'seq')), may hold values from -0.1875 to 0.1875
- qkv_first: float32 [1024, 2048], P(('fsdp', 'seq')), may hold values from -128 to 128
- qkv_second: float32 [1024, 2048], P(('fsdp', 'seq')), may hold values from 851.968 to 13762.56
- out_master: float32 [1024, 1024], P(('fsdp', 'seq')), may hold values from -0.75 to 0.75
- out_first: float32 [1024, 1024], P(('fsdp', 'seq')), may hold values from -32 to 32
- out_second: float32 [1024, 1024], P(('fsdp', 'seq')), may hold values from 78.6432 to 1245.184
- gate_up_master: float32 [1024, 9216], P(('fsdp', 'seq')), may hold values from -0.1875 to 0.1875
- gate_up_first: float32 [1024, 9216], P(('fsdp', 'seq')), may hold values from -32 to 32
- gate_up_second: float32 [1024, 9216], P(('fsdp', 'seq')), may hold values from 78.6432 to 1245.184
- down_master: float32 [4608, 1024], P(('fsdp', 'seq')), may hold values from -0.09375 to 0.09375
- down_first: float32 [4608, 1024], P(('fsdp', 'seq')), may hold values from -64 to 64
- down_second: float32 [4608, 1024], P(('fsdp', 'seq')), may hold values from 311.296 to 4915.2
Outputs:
- outputs: bfloat16 [16, 2048, 1024], P('fsdp', 'seq')
- input_grad: float32 [16, 2048, 1024], P('fsdp', 'seq')
- new_norm_gains: float32 [2, 1024], replicated
- new_norm_first: float32 [2, 1024], replicated
- new_norm_second: float32 [2, 1024], replicated
- new_qk_gains: float32 [2, 64], replicated
- new_qk_first: float32 [2, 64], replicated
- new_qk_second: float32 [2, 64], replicated
- new_qkv: float32 [1024, 2048], P(('fsdp', 'seq'))
- new_qkv_first: float32 [1024, 2048], P(('fsdp', 'seq'))
- new_qkv_second: float32 [1024, 2048], P(('fsdp', 'seq'))
- new_out: float32 [1024, 1024], P(('fsdp', 'seq'))
- new_out_first: float32 [1024, 1024], P(('fsdp', 'seq'))
- new_out_second: float32 [1024, 1024], P(('fsdp', 'seq'))
- new_gate_up: float32 [1024, 9216], P(('fsdp', 'seq'))
- new_gate_up_first: float32 [1024, 9216], P(('fsdp', 'seq'))
- new_gate_up_second: float32 [1024, 9216], P(('fsdp', 'seq'))
- new_down: float32 [4608, 1024], P(('fsdp', 'seq'))
- new_down_first: float32 [4608, 1024], P(('fsdp', 'seq'))
- new_down_second: float32 [4608, 1024], P(('fsdp', 'seq'))
Inputs may be any that keep to these rules, and one draw needn't show every extreme that they name: The 16 lengths of a row sum to 2048 and one of them is 1024.
All inputs are finite; a program needn't handle non-finite values.
Results may differ from a plain program's by a relative error of at most 0.018.
Values may be sent and summed in bfloat16 or wider, within the bound.
A program may use at most 256 MiB of HBM per device.

v0:
```python
import math

import jax
import jax.numpy as jnp
from jax import lax
from jax.sharding import PartitionSpec as P

D = 1024
HQ = 16
KEY_VALUE_HEADS = 8
HEAD_SIZE = 64
FF = 4608
QUERY_FEATURES = 1024
KEY_FEATURES = 512
GROUP_WIDTH = 2
BLOCK_SPAN = 512
STEP = 10


NORM_EPS = 1e-05
ROPE_BASE = 1000000.0
BETA_ONE = 0.9
BETA_TWO = 0.95
ADAM_EPS = 1e-08
DECAY_RATE = 0.1
GAIN_RATE = 0.3
MASKED_FILL = -1e30


def rms_norm(values_in, gain_row):
    scale_row = lax.rsqrt(jnp.mean(values_in * values_in, axis=-1, keepdims=True) + NORM_EPS)
    return values_in * scale_row * gain_row


def doc_layout(row_lengths, places):
    doc_ends = jnp.cumsum(row_lengths)
    passed = doc_ends[None, :] <= places[:, None]
    segment = jnp.sum(passed.astype(jnp.int32), axis=1)
    begins = jnp.sum(jnp.where(passed, row_lengths[None, :], 0), axis=1)
    return (segment, places - begins)


def rotate(values_in, position):
    half_width = values_in.shape[-1] // 2
    index_row = jnp.arange(half_width, dtype=jnp.float32)
    frequency = jnp.exp(index_row * (-2.0 * math.log(ROPE_BASE) / values_in.shape[-1]))
    angles = position.astype(jnp.float32)[:, None] * frequency[None, :]
    cosine = jnp.cos(angles)[:, None, :]
    sine_row = jnp.sin(angles)[:, None, :]
    front_half = values_in[..., :half_width]
    back_half = values_in[..., half_width:]
    return jnp.concatenate(
        [front_half * cosine - back_half * sine_row, back_half * cosine + front_half * sine_row],
        axis=-1,
    )


def contract_rows(left_side, right_side):
    return lax.dot_general(
        left_side, right_side, (((0,), (0,)), ((), ())), preferred_element_type=jnp.float32
    )


def contract_cols(left_side, right_side):
    return lax.dot_general(
        left_side, right_side, (((1,), (1,)), ((), ())), preferred_element_type=jnp.float32
    )


def adam_update(master, first_moment, second_moment, gradient, rate, decay):
    first_moment = BETA_ONE * first_moment + (1.0 - BETA_ONE) * gradient
    second_moment = BETA_TWO * second_moment + (1.0 - BETA_TWO) * gradient * gradient
    corrected = (
        first_moment
        / (1.0 - BETA_ONE**STEP)
        / (jnp.sqrt(second_moment / (1.0 - BETA_TWO**STEP)) + ADAM_EPS)
    )
    return (master - rate * (corrected + decay * master), first_moment, second_moment)


def block_live(key_start, key_total_count, context):
    grouped_heads, segment, places, row_lengths = context
    last_place = jnp.reshape(key_start + key_total_count - 1, (1,))
    last_segment, unused = doc_layout(row_lengths, last_place)
    return (key_start <= places[-1]) & (last_segment[0] >= segment[0])


def block_scores(key_block_rows, key_start, context):
    grouped_heads, segment, places, row_lengths = context
    key_total_count = key_block_rows.shape[0]
    key_places = key_start + jnp.arange(key_total_count, dtype=jnp.int32)
    key_segment, unused = doc_layout(row_lengths, key_places)
    scores = jnp.einsum(
        "qkgd,tkd->kgqt",
        grouped_heads,
        key_block_rows.reshape(key_total_count, KEY_VALUE_HEADS, HEAD_SIZE),
        preferred_element_type=jnp.float32,
    ) * HEAD_SIZE ** (-0.5)
    allowed = (segment[:, None] == key_segment[None, :]) & (key_places[None, :] <= places[:, None])
    return (scores, allowed)


def fold_block(carried, key_block_rows, value_block_rows, key_start, context):
    key_total_count = key_block_rows.shape[0]

    def update(state):
        running, highest, summed = state
        scores, allowed = block_scores(key_block_rows, key_start, context)
        masked = jnp.where(allowed, scores, MASKED_FILL)
        new_high = jnp.maximum(highest, jnp.max(masked, axis=-1))
        powers = jnp.where(allowed, jnp.exp(masked - new_high[..., None]), 0.0)
        factor = jnp.exp(highest - new_high)
        summed = summed * factor + jnp.sum(powers, axis=-1)
        running = running * factor[..., None] + jnp.einsum(
            "kgqt,tkd->kgqd",
            powers.astype(jnp.bfloat16),
            value_block_rows.reshape(key_total_count, KEY_VALUE_HEADS, HEAD_SIZE),
            preferred_element_type=jnp.float32,
        )
        return (running, new_high, summed)

    def keep_state(state):
        return state

    return lax.cond(block_live(key_start, key_total_count, context), update, keep_state, carried)


def fold_piece(carried, pieces, context):
    key_piece, value_piece = pieces
    key_total_count = key_piece.shape[0]

    def advance(state, turn_index):
        offset_in = turn_index * BLOCK_SPAN
        key_block_rows = lax.dynamic_slice_in_dim(key_piece, offset_in, BLOCK_SPAN, 0)
        value_block_rows = lax.dynamic_slice_in_dim(value_piece, offset_in, BLOCK_SPAN, 0)
        return (fold_block(state, key_block_rows, value_block_rows, offset_in, context), None)

    carried, unused = lax.scan(
        advance, carried, jnp.arange(key_total_count // BLOCK_SPAN, dtype=jnp.int32)
    )
    return carried


def per_device(
    inputs,
    cotangent,
    lengths,
    norm_gains,
    norm_first,
    norm_second,
    qk_gains,
    qk_first,
    qk_second,
    qkv_master,
    qkv_first,
    qkv_second,
    out_master,
    out_first,
    out_second,
    gate_up_master,
    gate_up_first,
    gate_up_second,
    down_master,
    down_first,
    down_second,
):
    seq_width = lax.axis_size("seq")
    shard_rows = inputs.shape[1]
    row_tokens = shard_rows * seq_width
    places = lax.axis_index("seq") * shard_rows + jnp.arange(shard_rows, dtype=jnp.int32)
    row_lengths = lengths[0]
    segment, position = doc_layout(row_lengths, places)
    shards = (
        qkv_master.astype(jnp.bfloat16),
        out_master.astype(jnp.bfloat16),
        gate_up_master.astype(jnp.bfloat16),
        down_master.astype(jnp.bfloat16),
    )
    w_qkv, w_out, w_gate_up, w_down = (
        lax.all_gather(shards[0], ("fsdp", "seq"), axis=0, tiled=True),
        lax.all_gather(shards[1], ("fsdp", "seq"), axis=0, tiled=True),
        lax.all_gather(shards[2], ("fsdp", "seq"), axis=0, tiled=True),
        lax.all_gather(shards[3], ("fsdp", "seq"), axis=0, tiled=True),
    )
    x_first = inputs[0].astype(jnp.float32)
    normed_first = rms_norm(x_first, norm_gains[0]).astype(jnp.bfloat16)
    query_key_value_rows = jnp.dot(normed_first, w_qkv, preferred_element_type=jnp.float32)
    query_raw = query_key_value_rows[:, :QUERY_FEATURES].reshape(shard_rows, HQ, HEAD_SIZE)
    unnormed_key = query_key_value_rows[:, QUERY_FEATURES : QUERY_FEATURES + KEY_FEATURES].reshape(
        shard_rows, KEY_VALUE_HEADS, HEAD_SIZE
    )
    unnormed_value = query_key_value_rows[:, QUERY_FEATURES + KEY_FEATURES :]

    def shape_heads(raw_heads, gain_row):
        return rotate(rms_norm(raw_heads, gain_row), position)

    query_matrix = shape_heads(query_raw, qk_gains[0]).astype(jnp.bfloat16)
    keys_local = (
        shape_heads(unnormed_key, qk_gains[1])
        .astype(jnp.bfloat16)
        .reshape(shard_rows, KEY_FEATURES)
    )
    values_local = unnormed_value.astype(jnp.bfloat16)
    grouped_heads = query_matrix.reshape(shard_rows, KEY_VALUE_HEADS, GROUP_WIDTH, HEAD_SIZE)
    context = (grouped_heads, segment, places, row_lengths)
    start_state = (
        jnp.zeros((KEY_VALUE_HEADS, GROUP_WIDTH, shard_rows, HEAD_SIZE), jnp.float32),
        jnp.full((KEY_VALUE_HEADS, GROUP_WIDTH, shard_rows), MASKED_FILL, jnp.float32),
        jnp.zeros((KEY_VALUE_HEADS, GROUP_WIDTH, shard_rows), jnp.float32),
    )
    running, highest, summed = fold_piece(
        start_state,
        (
            lax.all_gather(keys_local, "seq", axis=0, tiled=True),
            lax.all_gather(values_local, "seq", axis=0, tiled=True),
        ),
        context,
    )
    attn_grouped = running / summed[..., None]
    log_total = highest + jnp.log(summed)
    attn_mix = (
        attn_grouped.transpose(2, 0, 1, 3).reshape(shard_rows, QUERY_FEATURES).astype(jnp.bfloat16)
    )
    x_mid = x_first + jnp.dot(attn_mix, w_out, preferred_element_type=jnp.float32)
    normed_second = rms_norm(x_mid, norm_gains[1]).astype(jnp.bfloat16)
    gate_up = jnp.dot(normed_second, w_gate_up, preferred_element_type=jnp.float32)
    hidden = (jax.nn.silu(gate_up[:, :FF]) * gate_up[:, FF:]).astype(jnp.bfloat16)
    outputs = (x_mid + jnp.dot(hidden, w_down, preferred_element_type=jnp.float32)).astype(
        jnp.bfloat16
    )
    w_qkv, w_out, w_gate_up, w_down = (
        lax.all_gather(shards[0], ("fsdp", "seq"), axis=0, tiled=True),
        lax.all_gather(shards[1], ("fsdp", "seq"), axis=0, tiled=True),
        lax.all_gather(shards[2], ("fsdp", "seq"), axis=0, tiled=True),
        lax.all_gather(shards[3], ("fsdp", "seq"), axis=0, tiled=True),
    )
    gate_up = jnp.dot(normed_second, w_gate_up, preferred_element_type=jnp.float32)
    grad_top = cotangent[0]
    grad_down = contract_rows(hidden, grad_top)
    d_hidden = contract_cols(grad_top, w_down)
    unused_value, swiglu_back = jax.vjp(
        lambda gate_in, up_in: jax.nn.silu(gate_in) * up_in, gate_up[:, :FF], gate_up[:, FF:]
    )
    d_gate, d_up = swiglu_back(d_hidden)
    d_gate_up = jnp.concatenate([d_gate, d_up], axis=1).astype(jnp.bfloat16)
    grad_gate_up = contract_rows(normed_second, d_gate_up)
    d_second = contract_cols(d_gate_up, w_gate_up)
    unused_value, second_back = jax.vjp(rms_norm, x_mid, norm_gains[1])
    d_mid_norm, d_gain_second = second_back(d_second)
    d_mid = grad_top.astype(jnp.float32) + d_mid_norm
    d_attn = d_mid.astype(jnp.bfloat16)
    grad_out = contract_rows(attn_mix, d_attn)
    mixed_gradient = contract_cols(d_attn, w_out).astype(jnp.bfloat16)
    grouped_gradient = mixed_gradient.reshape(shard_rows, KEY_VALUE_HEADS, GROUP_WIDTH, HEAD_SIZE)
    delta = jnp.einsum("qkgd,kgqd->kgq", grouped_gradient.astype(jnp.float32), attn_grouped)
    all_keys, all_values = (
        lax.all_gather(keys_local, "seq", axis=0, tiled=True),
        lax.all_gather(values_local, "seq", axis=0, tiled=True),
    )

    def back_block(d_query, turn_index):
        key_start = turn_index * BLOCK_SPAN
        key_block_rows = lax.dynamic_slice_in_dim(all_keys, key_start, BLOCK_SPAN, 0)
        value_block_rows = lax.dynamic_slice_in_dim(all_values, key_start, BLOCK_SPAN, 0)

        def compute(unused_arg):
            scores, allowed = block_scores(key_block_rows, key_start, context)
            probs_block = jnp.exp(jnp.where(allowed, scores - log_total[..., None], MASKED_FILL))
            probs_block = jnp.where(allowed, probs_block, 0.0)
            d_probs = jnp.einsum(
                "qkgd,tkd->kgqt",
                grouped_gradient,
                value_block_rows.reshape(BLOCK_SPAN, KEY_VALUE_HEADS, HEAD_SIZE),
                preferred_element_type=jnp.float32,
            )
            d_scores = (probs_block * (d_probs - delta[..., None])).astype(jnp.bfloat16)
            d_q = jnp.einsum(
                "kgqt,tkd->kgqd",
                d_scores,
                key_block_rows.reshape(BLOCK_SPAN, KEY_VALUE_HEADS, HEAD_SIZE),
                preferred_element_type=jnp.float32,
            ) * HEAD_SIZE ** (-0.5)
            d_k = jnp.einsum(
                "kgqt,qkgd->tkd", d_scores, grouped_heads, preferred_element_type=jnp.float32
            ) * HEAD_SIZE ** (-0.5)
            d_v = jnp.einsum(
                "kgqt,qkgd->tkd",
                probs_block.astype(jnp.bfloat16),
                grouped_gradient,
                preferred_element_type=jnp.float32,
            )
            return (
                d_q,
                d_k.reshape(BLOCK_SPAN, KEY_FEATURES),
                d_v.reshape(BLOCK_SPAN, KEY_FEATURES),
            )

        def skipped(unused_arg):
            return (
                jnp.zeros((KEY_VALUE_HEADS, GROUP_WIDTH, shard_rows, HEAD_SIZE), jnp.float32),
                jnp.zeros((BLOCK_SPAN, KEY_FEATURES), jnp.float32),
                jnp.zeros((BLOCK_SPAN, KEY_FEATURES), jnp.float32),
            )

        d_q, d_k, d_v = lax.cond(block_live(key_start, BLOCK_SPAN, context), compute, skipped, 0)
        return (d_query + d_q, (d_k, d_v))

    d_query, (key_terms, value_terms) = lax.scan(
        back_block,
        jnp.zeros((KEY_VALUE_HEADS, GROUP_WIDTH, shard_rows, HEAD_SIZE), jnp.float32),
        jnp.arange(row_tokens // BLOCK_SPAN, dtype=jnp.int32),
    )
    key_terms = key_terms.reshape(row_tokens, KEY_FEATURES)
    value_terms = value_terms.reshape(row_tokens, KEY_FEATURES)
    keys_gradient, d_values = (
        lax.psum_scatter(
            key_terms.astype(jnp.bfloat16), "seq", scatter_dimension=0, tiled=True
        ).astype(jnp.float32),
        lax.psum_scatter(
            value_terms.astype(jnp.bfloat16), "seq", scatter_dimension=0, tiled=True
        ).astype(jnp.float32),
    )
    query_rows = d_query.transpose(2, 0, 1, 3).reshape(shard_rows, HQ, HEAD_SIZE)
    unused_value, query_back = jax.vjp(shape_heads, query_raw, qk_gains[0])
    d_query_raw, d_gain_query = query_back(query_rows)
    unused_value, key_backward = jax.vjp(shape_heads, unnormed_key, qk_gains[1])
    raw_key_gradient, key_gain_gradient = key_backward(
        keys_gradient.reshape(shard_rows, KEY_VALUE_HEADS, HEAD_SIZE)
    )
    d_qkv = jnp.concatenate(
        [
            d_query_raw.reshape(shard_rows, QUERY_FEATURES),
            raw_key_gradient.reshape(shard_rows, KEY_FEATURES),
            d_values,
        ],
        axis=1,
    ).astype(jnp.bfloat16)
    grad_qkv = contract_rows(normed_first, d_qkv)
    d_first = contract_cols(d_qkv, w_qkv)
    unused_value, first_back = jax.vjp(rms_norm, x_first, norm_gains[0])
    d_x_norm, d_gain_first = first_back(d_first)
    input_grad = (d_mid + d_x_norm)[None]
    norm_terms = jnp.stack([d_gain_first, d_gain_second])
    qk_terms = jnp.stack([d_gain_query, key_gain_gradient])
    norm_grad, qk_grad = lax.psum((norm_terms, qk_terms), ("fsdp", "seq"))
    qkv_grad, out_grad, gate_up_grad, down_grad = (
        lax.psum_scatter(grad_qkv, ("fsdp", "seq"), scatter_dimension=0, tiled=True),
        lax.psum_scatter(grad_out, ("fsdp", "seq"), scatter_dimension=0, tiled=True),
        lax.psum_scatter(grad_gate_up, ("fsdp", "seq"), scatter_dimension=0, tiled=True),
        lax.psum_scatter(grad_down, ("fsdp", "seq"), scatter_dimension=0, tiled=True),
    )
    norm_new = adam_update(norm_gains, norm_first, norm_second, norm_grad, GAIN_RATE, 0.0)
    qk_new = adam_update(qk_gains, qk_first, qk_second, qk_grad, GAIN_RATE, 0.0)
    qkv_new = adam_update(qkv_master, qkv_first, qkv_second, qkv_grad, D ** (-0.5), DECAY_RATE)
    out_new = adam_update(
        out_master, out_first, out_second, out_grad, (QUERY_FEATURES // 16) ** (-0.5), DECAY_RATE
    )
    gate_new = adam_update(
        gate_up_master, gate_up_first, gate_up_second, gate_up_grad, D ** (-0.5), DECAY_RATE
    )
    down_new = adam_update(
        down_master, down_first, down_second, down_grad, FF ** (-0.5), DECAY_RATE
    )
    return (
        outputs[None],
        input_grad,
        norm_new[0],
        norm_new[1],
        norm_new[2],
        qk_new[0],
        qk_new[1],
        qk_new[2],
        qkv_new[0],
        qkv_new[1],
        qkv_new[2],
        out_new[0],
        out_new[1],
        out_new[2],
        gate_new[0],
        gate_new[1],
        gate_new[2],
        down_new[0],
        down_new[1],
        down_new[2],
    )


def solution(mesh):
    return jax.shard_map(
        per_device,
        mesh=mesh,
        in_specs=(
            P("fsdp", "seq", None),
            P("fsdp", "seq", None),
            P("fsdp", None),
            P(),
            P(),
            P(),
            P(),
            P(),
            P(),
            P(("fsdp", "seq"), None),
            P(("fsdp", "seq"), None),
            P(("fsdp", "seq"), None),
            P(("fsdp", "seq"), None),
            P(("fsdp", "seq"), None),
            P(("fsdp", "seq"), None),
            P(("fsdp", "seq"), None),
            P(("fsdp", "seq"), None),
            P(("fsdp", "seq"), None),
            P(("fsdp", "seq"), None),
            P(("fsdp", "seq"), None),
            P(("fsdp", "seq"), None),
        ),
        out_specs=(
            P("fsdp", "seq", None),
            P("fsdp", "seq", None),
            P(),
            P(),
            P(),
            P(),
            P(),
            P(),
            P(("fsdp", "seq"), None),
            P(("fsdp", "seq"), None),
            P(("fsdp", "seq"), None),
            P(("fsdp", "seq"), None),
            P(("fsdp", "seq"), None),
            P(("fsdp", "seq"), None),
            P(("fsdp", "seq"), None),
            P(("fsdp", "seq"), None),
            P(("fsdp", "seq"), None),
            P(("fsdp", "seq"), None),
            P(("fsdp", "seq"), None),
            P(("fsdp", "seq"), None),
        ),
        check_vma=False,
    )
```

profile of v0, /device:TPU:0, one launch (start us, length us, event | category | flops | bytes accessed | tf_op | source)
XLA Modules:
  0.0 1775.4 jit_solution(13790170167547833137)
XLA Ops:
  13.7 62.7 %all-gather.7.cloned.1.call-done = bf16[1024,2048]{1,0:T(8,128)(2,1)} async-done(((bf16[32,2048]{1,0:T(8,128)(2,1)}), bf16[1024,2048]{1,0:T(8,128)(2,1)}) %all-gather.7.cloned.1.call-update) | async-done | bytes 4194320 | tf_op jit(solution)/shard_map/all_gather | solution.py:180
  124.5 30.2 %all-gather.9.cloned.1.call-done = bf16[2048,512]{0,1:T(8,128)(2,1)} async-done(((bf16[1024,512]{0,1:T(8,128)(2,1)}), bf16[2048,512]{0,1:T(8,128)(2,1)}) %all-gather.9.cloned.1.call-update) | async-done | bytes 2097168 | tf_op jit(solution)/shard_map/all_gather | solution.py:214
  157.2 123.3 %while.37 = (s32[]{:T(128)}, f32[8,2,1024,64]{2,3,1,0:T(8,128)}, f32[8,2,1024]{2,1,0:T(2,128)S(1)}, f32[8,2,1024]{2,1,0:T(2,128)S(1)}, s32[4]{0:T(128)S(1)}, /*i...) while((s32[]{:T(128)}, f32[8,2,1024,64]{2,3,1,0:T(8,128)}, ...), condition=%wide.region_15.16_spmd, body=%wide.region_7.15_spmd.sunk | while | flops 2260263168 | bytes 119557056 | solution.py:138
  163.1 50.0 %conditional.5 = ((f32[8,2,1024,64]{2,3,1,0:T(8,128)}, f32[8,2,1024]{2,1,0:T(2,128)S(1)}, f32[8,2,1024]{2,1,0:T(2,128)S(1)})) conditional(s32[]{:T(128)} %convert_element_type.237, (f32[8,2,1024,64]{2,3,1,0:T(8,128)}, f32[8,2,1024]{2,1,0:T(2,128)S(1)}, f32[8,2,1024]{2,1,0:T(2,128)S(1)}) %tuple.167, (s32[1024]{0:T(1024)S(1)}, s32[16]{0:T(128)S(1)}, ...), branch_computations={%region_9.9_spmd, %region_10.14_spmd} | conditional | flops 2260263168 | bytes 119556656 | solution.py:125
  166.5 13.7 fusion
  180.2 14.8 fusion.1
  195.1 18.0 %multiply_add_fusion = f32[8,2,1024,64]{2,3,1,0:T(8,128)} fusion(f32[8,2,1024,64]{2,3,1,0:T(8,128)} %get-tuple-element.735, bf16[512,8,64,1]{0,2,3,1:T(8,128)(2,1)S(1)} %bitcast.190, f32[8,512,1024,2]{2,1,3,0:T(8,128)} %get-tuple-element.1105, f32[8,2,1024]{2,1,0:T(2,128)S(1)} %max.5, pred[1024,512]{0,1:T(8,128)(4,1)S(1)} %compare_and_fusion, ...), kind=kOutput, calls=%fused_computation.7 | convolution fusion | flops 1117782016 | bytes 43122688 | tf_op jit(solution)/shard_map/while/body/eval_jaxpr/cond/branch_1_fun/kgqt,tkd->kgqd/dot_general | solution.py:114
  218.7 50.1 %conditional.5 = ((f32[8,2,1024,64]{2,3,1,0:T(8,128)}, f32[8,2,1024]{2,1,0:T(2,128)S(1)}, f32[8,2,1024]{2,1,0:T(2,128)S(1)})) conditional(s32[]{:T(128)} %convert_element_type.237, (f32[8,2,1024,64]{2,3,1,0:T(8,128)}, f32[8,2,1024]{2,1,0:T(2,128)S(1)}, f32[8,2,1024]{2,1,0:T(2,128)S(1)}) %tuple.167, (s32[1024]{0:T(1024)S(1)}, s32[16]{0:T(128)S(1)}, ...), branch_computations={%region_9.9_spmd, %region_10.14_spmd} | conditional | flops 2260263168 | bytes 119556656 | solution.py:125
  222.1 13.9 fusion
  236.0 15.0 fusion.1
  251.1 17.8 multiply_add_fusion
  293.1 48.4 %all-gather.15.cloned.1.call-done = bf16[1024,9216]{1,0:T(8,128)(2,1)} async-done(((bf16[32,9216]{1,0:T(8,128)(2,1)}), bf16[1024,9216]{1,0:T(8,128)(2,1)}) %all-gather.15.cloned.1.call-update) | async-done | bytes 18874384 | tf_op jit(solution)/shard_map/all_gather | solution.py:182
  341.5 29.8 %fusion.74 = f32[1024,9216]{1,0:T(8,128)} fusion(bf16[1024,9216]{1,0:T(8,128)(2,1)} %all-gather.15.cloned.1.call-done, f32[1024,1024]{0,1:T(8,128)} %get-tuple-element.1126, f32[1024]{0:T(1024)S(1)} %bitcast.222, f32[1024]{0:T(1024)S(1)} %fusion.68), kind=kOutput, calls=%fused_computation.174 | convolution fusion | flops 19330498560 | bytes 60825600 | tf_op jit(solution)/shard_map/dot_general | solution.py:226
  371.3 53.9 %all-gather.17.cloned.1.call-done = bf16[4608,1024]{1,0:T(8,128)(2,1)} async-done(((bf16[144,1024]{1,0:T(8,128)(2,1)}), bf16[4608,1024]{1,0:T(8,128)(2,1)}) %all-gather.17.cloned.1.call-update) | async-done | bytes 9437200 | tf_op jit(solution)/shard_map/all_gather | solution.py:183
  425.2 31.7 %fusion.28 = (bf16[1024,4608]{1,0:T(8,128)(2,1)}, bf16[1024,4608]{1,0:T(8,128)(2,1)}, bf16[1024,4608]{1,0:T(8,128)(2,1)}) fusion(f32[1024,9216]{1,0:T(8,128)} %fusion.74, bf16[4608,1024]{1,0:T(8,128)(2,1)} %all-gather.17.cloned.1.call-done, bf16[1,1024,1024]{2,1,0:T(8,128)(2,1)} %param.30), kind=kOutput, calls=%fused_computation.49 | convolution fusion | flops 9739173888 | bytes 77594624 | tf_op jit(solution)/shard_map/dot_general | solution.py:65
  456.9 30.3 %multiply_reduce_fusion.1 = (f32[1024]{0:T(1024)}, f32[1024]{0:T(1024)S(1)}, f32[1024,1024]{0,1:T(8,128)}) fusion(f32[1024,1024]{0,1:T(8,128)} %get-tuple-element.1126, f32[1024]{0:T(1024)S(1)} %fusion.68, f32[1024]{0:T(1024)S(1)} %bitcast.223, bf16[1024,9216]{1,0:T(8,128)(2,1)} %all-gather.15.cloned.1.call-done, ...), kind=kOutput, calls=%fused_computation.79 | convolution fusion | flops 19371393024 | bytes 46153728 | tf_op jit(solution)/shard_map/dot_general | solution.py:65
  497.6 192.1 %while.38 = (s32[]{:T(128)}, f32[8,2,1024,64]{2,3,1,0:T(8,128)}, bf16[4,512,512]{2,1,0:T(8,128)(2,1)}, bf16[4,512,512]{2,1,0:T(8,128)(2,1)}, s32[4]{0:T(128)S(1)...) while((s32[]{:T(128)}, f32[8,2,1024,64]{2,3,1,0:T(8,128)}, ...), condition=%wide.region_24.25_spmd.clone, body=%wide.region_18.24_spmd.clone.sunk | while | flops 5474639872 | bytes 188959696 | solution.py:308
  503.6 60.0 %conditional.6 = (f32[8,2,1024,64]{2,3,1,0:T(8,128)}, bf16[1,512,512]{1,2,0:T(8,128)(2,1)}, bf16[1,512,512]{1,2,0:T(8,128)(2,1)}) conditional(s32[]{:T(128)} %convert_element_type.239, () %tuple.171, (s32[1024]{0:T(1024)S(1)}, s32[16]{0:T(128)S(1)}, s32[]{:T(128)}, s32[1024]{0:T(1024)S(1)}, bf16[2048,512]{0,1:T(8,128)(2,1)}, ...), branch_computations={%region_20.20_spmd, %region_21.23_spmd} | conditional | flops 5472542720 | bytes 172182048 | solution.py:305
  520.9 15.8 fusion.13
  547.8 15.8 fusion.18
  578.4 60.0 %conditional.6 = (f32[8,2,1024,64]{2,3,1,0:T(8,128)}, bf16[1,512,512]{1,2,0:T(8,128)(2,1)}, bf16[1,512,512]{1,2,0:T(8,128)(2,1)}) conditional(s32[]{:T(128)} %convert_element_type.239, () %tuple.171, (s32[1024]{0:T(1024)S(1)}, s32[16]{0:T(128)S(1)}, s32[]{:T(128)}, s32[1024]{0:T(1024)S(1)}, bf16[2048,512]{0,1:T(8,128)(2,1)}, ...), branch_computations={%region_20.20_spmd, %region_21.23_spmd} | conditional | flops 5472542720 | bytes 172182048 | solution.py:305
  595.7 15.8 fusion.13
  622.6 15.8 fusion.18
  709.5 125.6 %reduce-scatter.7.cloned.1.call-done = bf16[1024,512]{1,0:T(8,128)(2,1)} async-done(((bf16[2048,512]{1,0:T(8,128)(2,1)}), bf16[1024,512]{1,0:T(8,128)(2,1)}) %reduce-scatter.7.cloned.1.call-update) | async-done | bytes 1048592 | tf_op jit(solution)/shard_map/reduce_scatter | solution.py:316
  841.2 28.7 %reduce-scatter.9.cloned.1.call-done = bf16[1024,512]{0,1:T(8,128)(2,1)} async-done(((bf16[2048,512]{0,1:T(8,128)(2,1)}), bf16[1024,512]{0,1:T(8,128)(2,1)}) %reduce-scatter.9.cloned.1.call-update) | async-done | bytes 1048592 | tf_op jit(solution)/shard_map/reduce_scatter | solution.py:319
  881.8 16.3 fusion.45
  898.8 28.9 %fusion.30 = f32[1024,9216]{1,0:T(8,128)} fusion(bf16[1024,4608]{1,0:T(8,128)(2,1)} %get-tuple-element.1109, bf16[1024,4608]{1,0:T(8,128)(2,1)} %get-tuple-element.1108, f32[1024,1024]{0,1:T(8,128)} %get-tuple-element.1126, f32[1024]{0:T(1024)S(1)} %bitcast.225, f32[1024]{0:T(1024)S(1)} %copy-done.43), kind=kOutput, calls=%fused_computation.55 | convolution fusion | flops 19368247296 | bytes 60825600 | tf_op jit(solution)/shard_map/dot_general | solution.py:59
  927.7 16.9 fusion.44
  965.9 40.0 %all-reduce.4 = (f32[2,1024]{1,0:T(2,128)S(1)}, f32[2,64]{1,0:T(2,128)S(1)}) all-reduce(f32[2,1024]{1,0:T(2,128)S(1)} %pad_maximum_fusion.8, f32[2,64]{1,0:T(2,128)S(1)} %pad_maximum_fusion.9), channel_id=1, replica_groups=mesh['fsdp'=16,'seq'=2] {'fsdp','seq'}, use_global_device_ids=true, to_apply=%region_32.33 | all-reduce | flops 2176 | bytes 17408 | tf_op jit(solution)/shard_map/psum | solution.py:345
  1015.9 180.6 %reduce-scatter.11.cloned.1.call-done = f32[32,2048]{1,0:T(8,128)} async-done(((f32[1024,2048]{1,0:T(8,128)}), f32[32,2048]{1,0:T(8,128)}) %reduce-scatter.11.cloned.1.call-update) | async-done | bytes 262160 | tf_op jit(solution)/shard_map/reduce_scatter | solution.py:347
  1198.6 211.9 %reduce-scatter.17.cloned.1.call-done = f32[144,1024]{1,0:T(8,128)} async-done(((f32[4608,1024]{1,0:T(8,128)}), f32[144,1024]{1,0:T(8,128)}) %reduce-scatter.17.cloned.1.call-update) | async-done | bytes 589840 | tf_op jit(solution)/shard_map/reduce_scatter | solution.py:350
  1413.5 350.7 %reduce-scatter.15.cloned.1.call-done = f32[32,9216]{1,0:T(8,128)} async-done(((f32[1024,9216]{1,0:T(8,128)}), f32[32,9216]{1,0:T(8,128)}) %reduce-scatter.15.cloned.1.call-update) | async-done | bytes 1179664 | tf_op jit(solution)/shard_map/reduce_scatter | solution.py:349
  (323 shorter events, 303.3 us)
Async XLA Ops:
  7.2 69.2 %all-gather.7.cloned.1.call-start = ((), (), s32[]{:S(2)}) async-start(), calls=%async_computation.6 | async-start | bytes 4325376 | tf_op jit(solution)/shard_map/all_gather | solution.py:180
  8.9 111.6 %all-gather.11.cloned.1.call-start = ((), (), s32[]{:S(2)}) async-start(), calls=%async_computation.8 | async-start | bytes 3145728 | tf_op jit(solution)/shard_map/all_gather | solution.py:215
  11.8 71.3 %copy-start.7 = (bf16[1,1024,1024]{1,2,0:T(8,128)(2,1)}, bf16[1,1024,1024]{1,2,0:T(8,128)(2,1)S(1)}, u32[]{:S(2)}) copy-start(bf16[1,1024,1024]{1,2,0:T(8,128)(2,1)S(1)} %copy.94) | copy-start | bytes 6291460
  13.1 70.0 %copy-start.40 = (f32[1024]{0:T(1024)}, f32[1024]{0:T(1024)S(1)}, u32[]{:S(2)}) copy-start(f32[1024]{0:T(1024)S(1)} %fusion.67) | copy-start | bytes 12292
  13.7 69.4 %copy-start.44 = (f32[1,1024]{1,0:T(1,128)}, f32[1,1024]{1,0:T(1,128)S(1)}, u32[]{:S(2)}) copy-start(f32[1,1024]{1,0:T(1,128)S(1)} %get-tuple-element.1120) | copy-start | bytes 12292
  87.5 67.1 %all-gather.9.cloned.1.call-start = ((), (), s32[]{:S(2)}) async-start(), calls=%async_computation.7 | async-start | bytes 3145728 | tf_op jit(solution)/shard_map/all_gather | solution.py:214
  97.0 187.9 %all-gather.13.cloned.1.call-start = ((), (), s32[]{:S(2)}) async-start(), calls=%async_computation.9 | async-start | bytes 2162688 | tf_op jit(solution)/shard_map/all_gather | solution.py:181
  98.6 242.9 %all-gather.15.cloned.1.call-start = ((), (), s32[]{:S(2)}) async-start(), calls=%async_computation.10 | async-start | bytes 19464192 | tf_op jit(solution)/shard_map/all_gather | solution.py:182
  99.6 325.6 %all-gather.17.cloned.1.call-start = ((), (), s32[]{:S(2)}) async-start(), calls=%async_computation.11 | async-start | bytes 9732096 | tf_op jit(solution)/shard_map/all_gather | solution.py:183
  101.5 733.5 %reduce-scatter.7.cloned.1.call-start = ((), (), s32[]{:S(2)}) async-start(), calls=%async_computation.12 | async-start | bytes 3145728 | tf_op jit(solution)/shard_map/reduce_scatter | solution.py:316
  284.9 56.6 %copy-start.46 = (f32[1,1024]{1,0:T(1,128)S(1)}, f32[1,1024]{1,0:T(1,128)}, u32[]{:S(2)}) copy-start(f32[1,1024]{1,0:T(1,128)} %get-tuple-element.1119) | copy-start | bytes 12292
  292.5 194.8 %copy-start.42 = (f32[1024]{0:T(1024)}, f32[1024]{0:T(1024)S(1)}, u32[]{:S(2)}) copy-start(f32[1024]{0:T(1024)S(1)} %fusion.68) | copy-start | bytes 12292
  689.7 180.1 %reduce-scatter.9.cloned.1.call-start = ((), (), s32[]{:S(2)}) async-start(), calls=%async_computation.13 | async-start | bytes 3145728 | tf_op jit(solution)/shard_map/reduce_scatter | solution.py:319
  693.8 320.3 %reduce-scatter.13.cloned.1.call-start = ((), (), s32[]{:S(2)}) async-start(), calls=%async_computation.15 | async-start | bytes 4325376 | tf_op jit(solution)/shard_map/reduce_scatter | solution.py:348
  700.6 495.9 %reduce-scatter.11.cloned.1.call-start = ((), (), s32[]{:S(2)}) async-start(), calls=%async_computation.14 | async-start | bytes 8650752 | tf_op jit(solution)/shard_map/reduce_scatter | solution.py:347
  709.5 130.1 %copy-start.3 = (f32[1024,512]{0,1:T(8,128)S(1)}, f32[1024,512]{0,1:T(8,128)}, u32[]{:S(2)}) copy-start(f32[1024,512]{0,1:T(8,128)} %copy-done.2) | copy-start | bytes 6291460
  709.5 130.2 %copy-start.30 = (f32[1024,8]{0,1:T(8,128)S(1)}, f32[1024,8]{0,1:T(8,128)}, u32[]{:S(2)}) copy-start(f32[1024,8]{0,1:T(8,128)} %copy-done.29) | copy-start | bytes 98308
  709.5 130.2 %copy-start.53 = (f32[64]{0:T(128)S(1)}, f32[64]{0:T(128)}, u32[]{:S(2)}) copy-start(f32[64]{0:T(128)} %copy-done.52) | copy-start | bytes 772
  880.3 530.3 %reduce-scatter.17.cloned.1.call-start = ((), (), s32[]{:S(2)}) async-start(), calls=%async_computation.17 | async-start | bytes 19464192 | tf_op jit(solution)/shard_map/reduce_scatter | solution.py:350
  898.2 866.0 %reduce-scatter.15.cloned.1.call-start = ((), (), s32[]{:S(2)}) async-start(), calls=%async_computation.16 | async-start | bytes 38928384 | tf_op jit(solution)/shard_map/reduce_scatter | solution.py:349
  960.2 45.6 %copy-start.55 = (f32[2,64]{1,0:T(2,128)S(1)}, f32[2,64]{1,0:T(2,128)}, u32[]{:S(2)}) copy-start(f32[2,64]{1,0:T(2,128)} %param.35) | copy-start | bytes 1540
  960.2 45.6 %copy-start.57 = (f32[2,64]{1,0:T(2,128)S(1)}, f32[2,64]{1,0:T(2,128)}, u32[]{:S(2)}) copy-start(f32[2,64]{1,0:T(2,128)} %param.36) | copy-start | bytes 1540
  960.2 45.6 %copy-start.58 = (f32[2,64]{1,0:T(2,128)S(1)}, f32[2,64]{1,0:T(2,128)}, u32[]{:S(2)}) copy-start(f32[2,64]{1,0:T(2,128)} %param.37) | copy-start | bytes 1540
  960.2 46.2 %copy-start.39 = (f32[2,1024]{1,0:T(2,128)S(1)}, f32[2,1024]{1,0:T(2,128)}, u32[]{:S(2)}) copy-start(f32[2,1024]{1,0:T(2,128)} %param.32) | copy-start | bytes 24580
  960.2 46.2 %copy-start.50 = (f32[2,1024]{1,0:T(2,128)S(1)}, f32[2,1024]{1,0:T(2,128)}, u32[]{:S(2)}) copy-start(f32[2,1024]{1,0:T(2,128)} %param.33) | copy-start | bytes 24580
  960.2 46.2 %copy-start.51 = (f32[2,1024]{1,0:T(2,128)S(1)}, f32[2,1024]{1,0:T(2,128)}, u32[]{:S(2)}) copy-start(f32[2,1024]{1,0:T(2,128)} %param.34) | copy-start | bytes 24580
  960.2 53.9 %copy-start.31 = (f32[32,1024]{1,0:T(8,128)S(1)}, f32[32,1024]{1,0:T(8,128)}, u32[]{:S(2)}) copy-start(f32[32,1024]{1,0:T(8,128)} %param.41) | copy-start | bytes 393220
  960.3 53.9 %copy-start.34 = (f32[32,1024]{1,0:T(8,128)S(1)}, f32[32,1024]{1,0:T(8,128)}, u32[]{:S(2)}) copy-start(f32[32,1024]{1,0:T(8,128)} %param.42) | copy-start | bytes 393220
  960.3 236.2 %copy-start.26 = (f32[32,2048]{1,0:T(8,128)S(1)}, f32[32,2048]{1,0:T(8,128)}, u32[]{:S(2)}) copy-start(f32[32,2048]{1,0:T(8,128)} %param.38) | copy-start | bytes 786436
  960.3 450.2 %copy-start.18 = (f32[144,1024]{1,0:T(8,128)S(1)}, f32[144,1024]{1,0:T(8,128)}, u32[]{:S(2)}) copy-start(f32[144,1024]{1,0:T(8,128)} %param.47) | copy-start | bytes 1769476
  965.8 798.3 %copy-start.13 = (f32[32,9216]{1,0:T(8,128)S(1)}, f32[32,9216]{1,0:T(8,128)}, u32[]{:S(2)}) copy-start(f32[32,9216]{1,0:T(8,128)} %param.44) | copy-start | bytes 3538948
  965.8 798.3 %copy-start.23 = (f32[32,9216]{1,0:T(8,128)S(1)}, f32[32,9216]{1,0:T(8,128)}, u32[]{:S(2)}) copy-start(f32[32,9216]{1,0:T(8,128)} %param.45) | copy-start | bytes 3538948
  (41 other events, 314.7 us)
Sparse Core Ops, SparseCore 0:
  11.6 64.7 all-gather.6
  87.7 31.6 all-gather.10
  121.5 33.1 all-gather.8
  158.1 56.5 all-gather.12
  218.0 123.5 all-gather.14
  344.9 80.3 all-gather.16
  689.8 145.1 reduce-scatter.6
  837.9 31.8 reduce-scatter.8
  872.1 141.9 reduce-scatter.12
  1016.3 180.1 reduce-scatter.10
  1202.9 207.5 reduce-scatter.16
  1416.8 347.2 reduce-scatter.14
where the time goes:
time: 1790 us; the launch traced here: 1780 us
  waiting for transfers between devices  1100 us (61%)
  matrix products  373 us (21%)
  other arithmetic  122 us (7%)
  local copies, waits for them, and re-layouts  102 us (6%)
  blocking collectives  40 us (2%)
  loops' own time  22.5 us (1%)
    reduce_scatter x1, waiting for transfers between devices, per_device(): lax.psum_scatter(grad_gate_up, ('fsdp', 'seq'), scatter_dimension=0, tile...  351 us
    reduce_scatter x1, waiting for transfers between devices, per_device(): lax.psum_scatter(grad_down, ('fsdp', 'seq'), scatter_dimension=0, tiled=T...  212 us
    reduce_scatter x1, waiting for transfers between devices, per_device(): lax.psum_scatter(grad_qkv, ('fsdp', 'seq'), scatter_dimension=0, tiled=True)  181 us
    reduce_scatter x1, waiting for transfers between devices, per_device(): lax.psum_scatter(key_terms.astype(jnp.bfloat16), 'seq', scatter_dimension...  126 us
    dot_general x4, matrix products, contract_cols(): lax.dot_general(left_side, right_side, (((1,), (1,)), ((), ())), preferre...  74.6 us
    all_gather x1, waiting for transfers between devices, per_device(): lax.all_gather(shards[0], ('fsdp', 'seq'), axis=0, tiled=True)  62.7 us
    dot_general x4, matrix products, contract_rows(): lax.dot_general(left_side, right_side, (((0,), (0,)), ((), ())), preferre...  62.2 us
    all_gather x1, waiting for transfers between devices, per_device(): lax.all_gather(shards[3], ('fsdp', 'seq'), axis=0, tiled=True)  53.9 us
  transfers between devices with their start and end apart: 12, of which 10 were waited for; matrix products, arithmetic and copies ran while one was open for 18% of the time, Pallas kernels for 0%

commit v1 on v0

v1 whole, which is shorter than its diff:
```python
import functools
import math

import jax
import jax.numpy as jnp
from jax import lax
from jax.experimental import pallas as pl
from jax.experimental.pallas import tpu as pltpu
from jax.sharding import PartitionSpec as P

D = 1024
HQ = 16
KEY_VALUE_HEADS = 8
HEAD_SIZE = 64
FF = 4608
QUERY_FEATURES = 1024
KEY_FEATURES = 512
STEP = 10
LANES = 128

NORM_EPS = 1e-05
ROPE_BASE = 1000000.0
BETA_ONE = 0.9
BETA_TWO = 0.95
ADAM_EPS = 1e-08
DECAY_RATE = 0.1
GAIN_RATE = 0.3

F32 = jnp.float32
BF16 = jnp.bfloat16
QUERY_BLOCK = 256
KEY_BLOCK = 256
FF_BLOCK = 256


def dot(a, b):
    return lax.dot_general(a, b, (((1,), (0,)), ((), ())), preferred_element_type=F32)


def dot_cols(a, b):
    return lax.dot_general(a, b, (((1,), (1,)), ((), ())), preferred_element_type=F32)


def dot_rows(a, b):
    return lax.dot_general(a, b, (((0,), (0,)), ((), ())), preferred_element_type=F32)


def params(limit=56):
    return pltpu.CompilerParams(vmem_limit_bytes=limit << 20)


def head_mean(v):
    row = lax.broadcasted_iota(jnp.int32, (LANES, LANES), 0) // HEAD_SIZE
    col = lax.broadcasted_iota(jnp.int32, (LANES, LANES), 1) // HEAD_SIZE
    ones = jnp.where(row == col, 1.0 / HEAD_SIZE, 0.0).astype(BF16)
    high = v.astype(BF16)
    low = (v - high.astype(F32)).astype(BF16)
    return dot(high, ones) + dot(low, ones)


def swap_halves(v):
    lane = lax.broadcasted_iota(jnp.int32, v.shape, 1) % HEAD_SIZE
    return jnp.where(
        lane < HEAD_SIZE // 2,
        pltpu.roll(v, LANES - HEAD_SIZE // 2, 1),
        pltpu.roll(v, HEAD_SIZE // 2, 1),
    )


def prep_kernel(raw_ref, gain_ref, cos_ref, sin_ref, q_ref, kv_ref):
    cosine, sine = cos_ref[...], sin_ref[...]
    for group in range(12):
        part = slice(group * LANES, (group + 1) * LANES)
        u = raw_ref[:, part]
        gain = gain_ref[0:1] if group < 8 else gain_ref[1:2]
        n = u * lax.rsqrt(head_mean(u * u) + NORM_EPS) * gain
        out = n * cosine + swap_halves(n) * sine
        if group < 8:
            q_ref[:, part] = (out * HEAD_SIZE**-0.5).astype(BF16)
        else:
            kv_ref[:, slice((group - 8) * LANES, (group - 7) * LANES)] = out.astype(BF16)
    kv_ref[:, KEY_FEATURES:] = raw_ref[:, QUERY_FEATURES + KEY_FEATURES :].astype(BF16)


def prep(raw, gains, cosine, sine):
    rows = raw.shape[0]
    block = min(rows, 256)
    whole = lambda width: pl.BlockSpec((block, width), lambda i: (i, 0))
    return pl.pallas_call(
        prep_kernel,
        name="prep",
        grid=(rows // block,),
        in_specs=[whole(2048), pl.BlockSpec((8, LANES), lambda i: (0, 0)), whole(LANES), whole(LANES)],
        out_specs=[whole(QUERY_FEATURES), whole(2 * KEY_FEATURES)],
        out_shape=[
            jax.ShapeDtypeStruct((rows, QUERY_FEATURES), BF16),
            jax.ShapeDtypeStruct((rows, 2 * KEY_FEATURES), BF16),
        ],
        compiler_params=params(),
        cost_estimate=pl.CostEstimate(
            flops=rows * 2048 * 40, transcendentals=rows * 24, bytes_accessed=rows * 2048 * 6
        ),
    )(raw, gains, cosine, sine)


def prep_back_kernel(raw_ref, gain_ref, cos_ref, sin_ref, dq_ref, dkv_ref, out_ref, dg_ref):
    cosine, sine = cos_ref[...], sin_ref[...]
    sums = [jnp.zeros((1, LANES), F32), jnp.zeros((1, LANES), F32)]
    for group in range(12):
        part = slice(group * LANES, (group + 1) * LANES)
        u = raw_ref[:, part]
        which = 0 if group < 8 else 1
        gain = gain_ref[which : which + 1]
        if group < 8:
            d = dq_ref[:, part] * HEAD_SIZE**-0.5
        else:
            d = dkv_ref[:, slice((group - 8) * LANES, (group - 7) * LANES)]
        d = d * cosine - swap_halves(d) * sine
        r = lax.rsqrt(head_mean(u * u) + NORM_EPS)
        w = d * gain
        n = u * r
        out_ref[:, part] = (r * (w - n * head_mean(w * n))).astype(BF16)
        sums[which] += jnp.sum(d * n, axis=0, keepdims=True)
    out_ref[:, QUERY_FEATURES + KEY_FEATURES :] = dkv_ref[:, KEY_FEATURES:].astype(BF16)

    @pl.when(pl.program_id(0) == 0)
    def _():
        dg_ref[...] = jnp.zeros_like(dg_ref)

    dg_ref[0:1] += sums[0]
    dg_ref[1:2] += sums[1]


def prep_back(raw, gains, cosine, sine, dq, dkv):
    rows = raw.shape[0]
    block = min(rows, 256)
    whole = lambda width: pl.BlockSpec((block, width), lambda i: (i, 0))
    small = pl.BlockSpec((8, LANES), lambda i: (0, 0))
    return pl.pallas_call(
        prep_back_kernel,
        name="prep_back",
        grid=(rows // block,),
        in_specs=[
            whole(2048),
            small,
            whole(LANES),
            whole(LANES),
            whole(QUERY_FEATURES),
            whole(2 * KEY_FEATURES),
        ],
        out_specs=[whole(2048), small],
        out_shape=[
            jax.ShapeDtypeStruct((rows, 2048), BF16),
            jax.ShapeDtypeStruct((8, LANES), F32),
        ],
        compiler_params=params(),
        cost_estimate=pl.CostEstimate(
            flops=rows * 2048 * 60, transcendentals=rows * 24, bytes_accessed=rows * 2048 * 10
        ),
    )(raw, gains, cosine, sine, dq, dkv)


def twice(pair, odd):
    wide = pair.astype(F32)
    turned = pltpu.roll(wide, HEAD_SIZE, 1)
    lane = lax.broadcasted_iota(jnp.int32, wide.shape, 1)
    first = lane < HEAD_SIZE
    keep = first != (odd == 1)
    return jnp.where(keep, wide, turned).astype(BF16)


def stack_heads(pair):
    lane = lax.broadcasted_iota(jnp.int32, pair.shape, 1)
    zero = jnp.zeros_like(pair)
    return jnp.concatenate(
        [jnp.where(lane < HEAD_SIZE, pair, zero), jnp.where(lane < HEAD_SIZE, zero, pair)], axis=0
    )


def fill(head, others, own, lane_block, target):
    odd = lax.rem(head, 2)
    at = 0
    for source in (others, own):
        rows = source.shape[0]
        for start in range(0, rows, 256):
            target[at + start : at + start + 256, lane_block : lane_block + LANES] = twice(
                source[start : start + 256, :], odd
            )
        at += rows


def attend_kernel(
    low_ref,
    first_ref,
    q_ref,
    ko_ref,
    vo_ref,
    k_ref,
    v_ref,
    out_ref,
    lse_ref,
    keys,
    values,
):
    head, turn = pl.program_id(0), pl.program_id(1)
    block = q_ref.shape[0]
    tall = 2 * block

    @pl.when(turn == 0)
    def _():
        fill(head, ko_ref, k_ref, 0, keys)
        fill(head, vo_ref, v_ref, 0, values)
        values[:, LANES:] = jnp.ones((values.shape[0], LANES), BF16)

    queries = stack_heads(q_ref[...])
    place0 = low_ref[0] + turn * block
    place = place0 + lax.rem(lax.broadcasted_iota(jnp.int32, (tall, 1), 0), block)
    first = first_ref[:, 0:1]
    first = jnp.concatenate([first, first], axis=0)
    begin = low_ref[1 + turn] // KEY_BLOCK
    end = (place0 + block - 1) // KEY_BLOCK + 1

    def step(at, total):
        start = pl.multiple_of(at * KEY_BLOCK, KEY_BLOCK)
        scores = dot_cols(queries, keys[pl.ds(start, KEY_BLOCK), :])
        key_place = start + lax.broadcasted_iota(jnp.int32, (tall, KEY_BLOCK), 1)
        allowed = (key_place >= first) & (key_place <= place)
        powers = jnp.where(allowed, jnp.exp(scores), 0.0).astype(BF16)
        return total + dot(powers, values[pl.ds(start, KEY_BLOCK), :])

    total = lax.fori_loop(begin, end, step, jnp.zeros((tall, 2 * LANES), F32))
    mass = total[:, LANES:]
    mixed = total[:, :LANES] / mass
    lane = lax.broadcasted_iota(jnp.int32, (block, LANES), 1)
    out_ref[...] = jnp.where(lane < HEAD_SIZE, mixed[:block], mixed[block:]).astype(BF16)
    logs = jnp.log(mass)
    lse_ref[0] = jnp.transpose(logs)[0:8, :]


def attend(q, others, own, low, first):
    rows = q.shape[0]
    block = min(QUERY_BLOCK, rows)
    turns = rows // block
    total = others.shape[0] + rows
    pair = lambda size, off: pl.BlockSpec((size, LANES), lambda h, t, low: (0, off + h // 2))
    return pl.pallas_call(
        attend_kernel,
        name="attend",
        grid_spec=pltpu.PrefetchScalarGridSpec(
            num_scalar_prefetch=1,
            grid=(KEY_VALUE_HEADS, turns),
            in_specs=[
                pl.BlockSpec((block, LANES), lambda h, t, low: (t, 0)),
                pl.BlockSpec((block, LANES), lambda h, t, low: (t, h)),
                pair(others.shape[0], 0),
                pair(others.shape[0], 4),
                pair(rows, 0),
                pair(rows, 4),
            ],
            out_specs=[
                pl.BlockSpec((block, LANES), lambda h, t, low: (t, h)),
                pl.BlockSpec((1, 8, 2 * block), lambda h, t, low: (h, t, 0)),
            ],
            scratch_shapes=[pltpu.VMEM((total, LANES), BF16), pltpu.VMEM((total, 2 * LANES), BF16)],
        ),
        out_shape=[
            jax.ShapeDtypeStruct((rows, QUERY_FEATURES), BF16),
            jax.ShapeDtypeStruct((KEY_VALUE_HEADS, 8 * turns, 2 * block), F32),
        ],
        compiler_params=params(),
        cost_estimate=pl.CostEstimate(
            flops=rows * 1024 * 1024 * 8, transcendentals=rows * 1024 * 16, bytes_accessed=16 << 20
        ),
    )(low, first, q, others, others, own, own)


def attend_back_kernel(
    low_ref,
    first_ref,
    q_ref,
    do_ref,
    mixed_ref,
    lse_ref,
    ko_ref,
    vo_ref,
    k_ref,
    v_ref,
    dq_ref,
    dk_ref,
    dv_ref,
    keys,
    values,
    dkeys,
    dvalues,
):
    head, turn = pl.program_id(0), pl.program_id(1)
    block = q_ref.shape[0]
    tall = 2 * block

    @pl.when(turn == 0)
    def _():
        fill(head, ko_ref, k_ref, 0, keys)
        fill(head, vo_ref, v_ref, 0, values)
        dkeys[...] = jnp.zeros_like(dkeys)
        dvalues[...] = jnp.zeros_like(dvalues)

    queries = stack_heads(q_ref[...])
    rising = stack_heads(do_ref[...])
    across = jnp.transpose(do_ref[...].astype(F32) * mixed_ref[...].astype(F32))
    delta = jnp.concatenate(
        [
            jnp.sum(across[:HEAD_SIZE], axis=0, keepdims=True),
            jnp.sum(across[HEAD_SIZE:], axis=0, keepdims=True),
        ],
        axis=1,
    )
    logs = lse_ref[0][0:1]
    place0 = low_ref[0] + turn * block
    place = place0 + lax.rem(lax.broadcasted_iota(jnp.int32, (1, tall), 1), block)
    first = first_ref[0:1]
    first = jnp.concatenate([first, first], axis=1)
    begin = low_ref[1 + turn] // KEY_BLOCK
    end = (place0 + block - 1) // KEY_BLOCK + 1

    def step(at, dq):
        start = pl.multiple_of(at * KEY_BLOCK, KEY_BLOCK)
        span = pl.ds(start, KEY_BLOCK)
        key = keys[span, :]
        scores = dot_cols(key, queries)
        key_place = start + lax.broadcasted_iota(jnp.int32, (KEY_BLOCK, tall), 0)
        allowed = (key_place >= first) & (key_place <= place)
        probs = jnp.where(allowed, jnp.exp(scores - logs), 0.0)
        dprobs = dot_cols(values[span, :], rising)
        dscores = (probs * (dprobs - delta)).astype(BF16)
        dkeys[span, :] += dot(dscores, queries)
        dvalues[span, :] += dot(probs.astype(BF16), rising)
        return dq + dot_rows(dscores, key)

    dq = lax.fori_loop(begin, end, step, jnp.zeros((tall, LANES), F32))
    lane = lax.broadcasted_iota(jnp.int32, (block, LANES), 1)
    dq_ref[...] = jnp.where(lane < HEAD_SIZE, dq[:block], dq[block:])

    @pl.when(turn == pl.num_programs(1) - 1)
    def _():
        odd = lax.rem(head, 2)
        for source, target in ((dkeys, dk_ref), (dvalues, dv_ref)):
            for start in range(0, source.shape[0], 256):
                part = slice(start, start + 256)
                both = source[part, :]
                both = both + pltpu.roll(both, HEAD_SIZE, 1)
                lane = lax.broadcasted_iota(jnp.int32, both.shape, 1)
                mine = (lane < HEAD_SIZE) != (odd == 1)

                @pl.when(odd == 0)
                def _():
                    target[part, :] = both

                @pl.when(odd == 1)
                def _():
                    target[part, :] = jnp.where(mine, both, target[part, :])


def attend_back(q, d_mixed, mixed, lse, others, own, low, first_lane):
    rows = q.shape[0]
    block = min(QUERY_BLOCK, rows)
    turns = rows // block
    total = others.shape[0] + rows
    pair = lambda size, off: pl.BlockSpec((size, LANES), lambda h, t, low: (0, off + h // 2))
    tile = pl.BlockSpec((block, LANES), lambda h, t, low: (t, h))
    return pl.pallas_call(
        attend_back_kernel,
        name="attend_back",
        grid_spec=pltpu.PrefetchScalarGridSpec(
            num_scalar_prefetch=1,
            grid=(KEY_VALUE_HEADS, turns),
            in_specs=[
                pl.BlockSpec((8, block), lambda h, t, low: (0, t)),
                tile,
                tile,
                tile,
                pl.BlockSpec((1, 8, 2 * block), lambda h, t, low: (h, t, 0)),
                pair(others.shape[0], 0),
                pair(others.shape[0], 4),
                pair(rows, 0),
                pair(rows, 4),
            ],
            out_specs=[tile, pair(total, 0), pair(total, 0)],
            scratch_shapes=[
                pltpu.VMEM((total, LANES), BF16),
                pltpu.VMEM((total, LANES), BF16),
                pltpu.VMEM((total, LANES), F32),
                pltpu.VMEM((total, LANES), F32),
            ],
        ),
        out_shape=[
            jax.ShapeDtypeStruct((rows, QUERY_FEATURES), F32),
            jax.ShapeDtypeStruct((total, KEY_FEATURES), F32),
            jax.ShapeDtypeStruct((total, KEY_FEATURES), F32),
        ],
        compiler_params=params(),
        cost_estimate=pl.CostEstimate(
            flops=rows * 1024 * 1024 * 20, transcendentals=rows * 1024 * 16, bytes_accessed=40 << 20
        ),
    )(low, first_lane, q, d_mixed, mixed, lse, others, others, own, own)


def feed_kernel(
    a_ref, at_ref, g_ref, wg_ref, wu_ref, wd_ref, y_in, b_in, y_ref, b_ref, gg_ref, gu_ref, gd_ref
):
    @pl.when(pl.program_id(0) == 0)
    def _():
        y_ref[...] = y_in[...]
        b_ref[...] = b_in[...]

    a, g = a_ref[...], g_ref[...]
    wg, wu, wd = wg_ref[...], wu_ref[...], wd_ref[...]
    gate = dot(a, wg)
    up = dot(a, wu)
    d_hidden = dot_cols(g, wd)
    sigma = 1.0 / (1.0 + jnp.exp(-gate))
    swish = gate * sigma
    hidden = (swish * up).astype(BF16)
    d_gate = (d_hidden * up * sigma * (1.0 + gate * (1.0 - sigma))).astype(BF16)
    d_up = (d_hidden * swish).astype(BF16)
    y_ref[...] += dot(hidden, wd)
    b_ref[...] += dot_cols(d_gate, wg) + dot_cols(d_up, wu)
    at = at_ref[...]
    gg_ref[...] = dot(at, d_gate).astype(BF16)
    gu_ref[...] = dot(at, d_up).astype(BF16)
    gd_ref[...] = dot_rows(hidden, g).astype(BF16)


def feed(a, at, g, w_gate, w_up, w_down, y, b):
    rows, width = a.shape[0], w_gate.shape[1]
    turns = width // FF_BLOCK
    fixed = lambda s: pl.BlockSpec(s, lambda j: (0, 0))
    col = pl.BlockSpec((D, FF_BLOCK), lambda j: (0, j))
    row = pl.BlockSpec((FF_BLOCK, D), lambda j: (j, 0))
    return pl.pallas_call(
        feed_kernel,
        name="feed",
        grid=(turns,),
        in_specs=[
            fixed((rows, D)),
            fixed((D, rows)),
            fixed((rows, D)),
            col,
            col,
            row,
            fixed((rows, D)),
            fixed((rows, D)),
        ],
        out_specs=[fixed((rows, D)), fixed((rows, D)), col, col, row],
        out_shape=[
            jax.ShapeDtypeStruct((rows, D), F32),
            jax.ShapeDtypeStruct((rows, D), F32),
            jax.ShapeDtypeStruct((D, width), BF16),
            jax.ShapeDtypeStruct((D, width), BF16),
            jax.ShapeDtypeStruct((width, D), BF16),
        ],
        compiler_params=params(60),
        cost_estimate=pl.CostEstimate(
            flops=18 * rows * D * width, transcendentals=rows * width, bytes_accessed=12 * D * width
        ),
    )(a, at, g, w_gate, w_up, w_down, y, b)


def rms_scale(v):
    return lax.rsqrt(jnp.mean(v * v, axis=-1, keepdims=True) + NORM_EPS)


def rms_back(v, scale, gain_row, d_out):
    w = d_out * gain_row
    n = v * scale
    d_v = scale * (w - n * jnp.mean(w * n, axis=-1, keepdims=True))
    return d_v, jnp.sum(d_out * n, axis=0)


def adam_update(master, first_moment, second_moment, gradient, rate, decay):
    first_moment = BETA_ONE * first_moment + (1.0 - BETA_ONE) * gradient
    second_moment = BETA_TWO * second_moment + (1.0 - BETA_TWO) * gradient * gradient
    corrected = (
        first_moment
        / (1.0 - BETA_ONE**STEP)
        / (jnp.sqrt(second_moment / (1.0 - BETA_TWO**STEP)) + ADAM_EPS)
    )
    return (master - rate * (corrected + decay * master), first_moment, second_moment)


def rotation_tables(position):
    half = HEAD_SIZE // 2
    index_row = jnp.arange(half, dtype=F32)
    frequency = jnp.exp(index_row * (-2.0 * math.log(ROPE_BASE) / HEAD_SIZE))
    angles = position.astype(F32)[:, None] * frequency[None, :]
    cosine, sine = jnp.cos(angles), jnp.sin(angles)
    return (
        jnp.concatenate([cosine] * 4, axis=1),
        jnp.concatenate([-sine, sine, -sine, sine], axis=1),
    )


ALL = ("fsdp", "seq")


def gather(shard):
    return lax.all_gather(shard, ALL, axis=0, tiled=True)


def scatter(terms):
    return lax.psum_scatter(terms, ALL, scatter_dimension=0, tiled=True).astype(F32)


def per_device(
    inputs,
    cotangent,
    lengths,
    norm_gains,
    norm_first,
    norm_second,
    qk_gains,
    qk_first,
    qk_second,
    qkv_master,
    qkv_first,
    qkv_second,
    out_master,
    out_first,
    out_second,
    gate_up_master,
    gate_up_first,
    gate_up_second,
    down_master,
    down_first,
    down_second,
):
    seq_width = lax.axis_size("seq")
    turn_here = lax.axis_index("seq")
    rows = inputs.shape[1]
    block = min(QUERY_BLOCK, rows)
    w_qkv = gather(qkv_master.astype(BF16))
    w_out = gather(out_master.astype(BF16))
    w_down = gather(down_master.astype(BF16))
    w_gate = gather(gate_up_master[:, :FF].astype(BF16))
    w_up = gather(gate_up_master[:, FF:].astype(BF16))

    places = turn_here * rows + jnp.arange(rows, dtype=jnp.int32)
    row_lengths = lengths[0]
    doc_ends = jnp.cumsum(row_lengths)
    passed = doc_ends[None, :] <= places[:, None]
    begins = jnp.sum(jnp.where(passed, row_lengths[None, :], 0), axis=1)
    cosine, sine = rotation_tables(places - begins)
    if seq_width == 2:
        base = (turn_here - 1) * rows
    else:
        base = turn_here * 0
    first = (begins - base).astype(jnp.int32)
    low = jnp.concatenate([(turn_here * rows - base)[None], first[::block]]).astype(jnp.int32)
    first_wide = jnp.broadcast_to(first[:, None], (rows, LANES))
    first_lane = jnp.broadcast_to(first[None, :], (8, rows))

    x = inputs[0].astype(F32)
    scale_first = rms_scale(x)
    normed_first = (x * scale_first * norm_gains[0]).astype(BF16)
    raw = jnp.dot(normed_first, w_qkv, preferred_element_type=F32)
    gain_rows = jnp.pad(jnp.tile(qk_gains, (1, 2)), ((0, 6), (0, 0)))
    q, kv = prep(raw, gain_rows, cosine, sine)
    if seq_width == 2:
        others = lax.ppermute(kv, "seq", [(0, 1)])
        own = kv
    else:
        everyone = lax.all_gather(kv, "seq", axis=0, tiled=True)
        others, own = everyone, kv
    mixed, lse = attend(q, others, own, low, first_wide)
    x_mid = x + jnp.dot(mixed, w_out, preferred_element_type=F32)
    scale_second = rms_scale(x_mid)
    normed_second = (x_mid * scale_second * norm_gains[1]).astype(BF16)
    g = cotangent[0]
    out_sum, d_b, grad_gate, grad_up, grad_down = feed(
        normed_second, normed_second.T, g, w_gate, w_up, w_down, x_mid, jnp.zeros_like(x_mid)
    )
    outputs = out_sum.astype(BF16)
    gate_grad = scatter(grad_gate)
    up_grad = scatter(grad_up)
    down_grad = scatter(grad_down)
    d_norm, d_gain_second = rms_back(x_mid, scale_second, norm_gains[1], d_b)
    d_mid = g.astype(F32) + d_norm
    d_attn = d_mid.astype(BF16)
    d_mixed = dot_cols(d_attn, w_out).astype(BF16)
    out_grad = scatter(dot_rows(mixed, d_attn).astype(BF16))
    dq, dk, dv = attend_back(q, d_mixed, mixed, lse, others, own, low, first_lane)
    d_all = jnp.concatenate([dk, dv], axis=1)
    if seq_width == 2:
        back = lax.ppermute(d_all[:rows].astype(BF16), "seq", [(1, 0)])
        dkv = d_all[rows:] + back.astype(F32)
    else:
        dkv = lax.psum_scatter(
            d_all[: seq_width * rows].astype(BF16), "seq", scatter_dimension=0, tiled=True
        ).astype(F32)
    d_qkv, d_gain_qk = prep_back(raw, gain_rows, cosine, sine, dq, dkv)
    qkv_grad = scatter(dot_rows(normed_first, d_qkv).astype(BF16))
    d_a = dot_cols(d_qkv, w_qkv)
    d_x, d_gain_first = rms_back(x, scale_first, norm_gains[0], d_a)
    input_grad = (d_mid + d_x)[None]
    norm_terms = jnp.stack([d_gain_first, d_gain_second])
    qk_terms = d_gain_qk[:2, :HEAD_SIZE] + d_gain_qk[:2, HEAD_SIZE:]
    norm_grad, qk_grad = lax.psum((norm_terms, qk_terms), ALL)

    norm_new = adam_update(norm_gains, norm_first, norm_second, norm_grad, GAIN_RATE, 0.0)
    qk_new = adam_update(qk_gains, qk_first, qk_second, qk_grad, GAIN_RATE, 0.0)
    qkv_new = adam_update(qkv_master, qkv_first, qkv_second, qkv_grad, D**-0.5, DECAY_RATE)
    out_new = adam_update(
        out_master, out_first, out_second, out_grad, (QUERY_FEATURES // 16) ** -0.5, DECAY_RATE
    )
    gate_up_grad = jnp.concatenate([gate_grad, up_grad], axis=1)
    gate_new = adam_update(
        gate_up_master, gate_up_first, gate_up_second, gate_up_grad, D**-0.5, DECAY_RATE
    )
    down_new = adam_update(down_master, down_first, down_second, down_grad, FF**-0.5, DECAY_RATE)
    return (
        outputs[None],
        input_grad,
        *norm_new,
        *qk_new,
        *qkv_new,
        *out_new,
        *gate_new,
        *down_new,
    )


def solution(mesh):
    token = P("fsdp", "seq", None)
    weight = P(ALL, None)
    return jax.shard_map(
        per_device,
        mesh=mesh,
        in_specs=(token, token, P("fsdp", None)) + (P(),) * 6 + (weight,) * 12,
        out_specs=(token, token) + (P(),) * 6 + (weight,) * 12,
        check_vma=False,
    )
```

time: 1790 us -> 1270 us (0.71)
  matrix products: 373 us -> 41.7 us
  Pallas kernels: 0 us -> 229 us
  waiting for transfers between devices: 1100 us -> 875 us
  local copies, waits for them, and re-layouts: 102 us -> 18.1 us
  other arithmetic: 122 us -> 45.6 us
  loops' own time: 22.5 us -> 0 us
    reduce_scatter x6 -> x5, waiting for transfers between devices: 904 us -> 493 us  [scatter(): lax.psum_scatter(terms, ALL, scatter_dimension=0, tiled=True).astype(F32)]
    dot_general x26 -> x6, matrix products: 373 us -> 41.7 us  [the longest x2 14.7 us: dot_cols(): lax.dot_general(a, b, (((1,), (1,)), ((), ())), preferred_element_type=F32)]
    pallas_call x0 -> x5, Pallas kernels: none -> 229 us  [the longest x1 104 us: feed(): pl.pallas_call(feed_kernel, name='feed', grid=(turns,), in_specs=[fixed((...]
    ppermute x0 -> x2, waiting for transfers between devices: none -> 137 us  [the longest x1 87.7 us: per_device(): back = lax.ppermute(d_all[:rows].astype(BF16), 'seq', [(1, 0)])]
    all_gather x6 -> x5, waiting for transfers between devices: 195 us -> 243 us  [gather(): return lax.all_gather(shard, ALL, axis=0, tiled=True)]
    reduce_sum x20 -> x3, other arithmetic: 47 us -> 5.25 us  [the longest x1 4.68 us: rms_back(): return (d_v, jnp.sum(d_out * n, axis=0))]
    add x13 -> x4, other arithmetic: 32.2 us -> 4.31 us  [the longest x1 2.69 us: per_device(): dkv = d_all[rows:] + back.astype(F32)]
    slice x22 -> x4, local copies, waits for them, and re-layouts: 25.9 us -> 1.27 us  [the longest x1 0.85 us: per_device(): w_up = gather(gate_up_master[:, FF:].astype(BF16))]
  transfers between devices with their start and end apart: 12 -> 12, of which waited for: 10 -> 10; matrix products, arithmetic and copies ran while one was open for 18% -> 6% of each run, Pallas kernels for 0% -> 10%
where the time goes in v1:
time: 1270 us
  waiting for transfers between devices  875 us (69%)
  Pallas kernels  229 us (18%)
  other arithmetic  45.6 us (4%)
  matrix products  41.7 us (3%)
  blocking collectives  37.7 us (3%)
  local copies, waits for them, and re-layouts  18.1 us (1%)
  between operations  15 us (1%)
    reduce_scatter x5, waiting for transfers between devices, scatter(): lax.psum_scatter(terms, ALL, scatter_dimension=0, tiled=True).astype(F32)  493 us
    all_gather x5, waiting for transfers between devices, gather(): return lax.all_gather(shard, ALL, axis=0, tiled=True)  243 us
    pallas_call x1, Pallas kernels, feed(): pl.pallas_call(feed_kernel, name='feed', grid=(turns,), in_specs=[fixed((...  104 us
    ppermute x1, waiting for transfers between devices, per_device(): back = lax.ppermute(d_all[:rows].astype(BF16), 'seq', [(1, 0)])  87.7 us
    pallas_call x1, Pallas kernels, attend_back(): pl.pallas_call(attend_back_kernel, name='attend_back', grid_spec=pltpu.Pr...  63.8 us
    ppermute x1, waiting for transfers between devices, per_device(): others = lax.ppermute(kv, 'seq', [(0, 1)])  49 us
    pallas_call x1, Pallas kernels, attend(): pl.pallas_call(attend_kernel, name='attend', grid_spec=pltpu.PrefetchScal...  41.6 us
    psum x1, blocking collectives, per_device(): norm_grad, qk_grad = lax.psum((norm_terms, qk_terms), ALL)  37.7 us
  transfers between devices with their start and end apart: 12, of which 10 were waited for; matrix products, arithmetic and copies ran while one was open for 6% of the time, Pallas kernels for 10%

profile of v1, /device:TPU:0, one launch (start us, length us, event | category | flops | bytes accessed | tf_op | source)
XLA Modules:
  0.0 1267.9 jit_solution(3495176716009474572)
XLA Ops:
  19.8 56.6 %all-gather.6.cloned.1.call-done = bf16[1024,2048]{1,0:T(8,128)(2,1)} async-done(((bf16[32,2048]{1,0:T(8,128)(2,1)}), bf16[1024,2048]{1,0:T(8,128)(2,1)}) %all-gather.6.cloned.1.call-update) | async-done | bytes 4194320 | tf_op jit(solution)/shard_map/all_gather | solution.py:506
  76.4 9.2 fusion.17.raw_ref
  85.6 7.9 prep.1
  93.6 4.7 collective-permute-start
  98.9 49.0 %collective-permute-done.ko_ref.vo_ref = bf16[1024,1024]{1,0:T(8,128)(2,1)} collective-permute-done((bf16[1024,1024]{1,0:T(8,128)(2,1)}, bf16[1024,1024]{1,0:T(8,128)(2,1)}, u32[]{:S(2)}, u32[]{:S(2)}) %collective-permute-start) | collective-permute-done | bytes 2097184 | tf_op jit(solution)/shard_map/ppermute | solution.py:568
  148.9 41.6 %attend.1 = (bf16[1024,1024]{1,0:T(8,128)(2,1)}, f32[8,32,512]{2,1,0:T(8,128)}) custom-call(s32[5]{0:T(128)} %pad_add_fusion.low_ref, s32[1024,128]{1,0:T(8,128)} %broadcast_in_dim.50.first_ref, bf16[1024,1024]{1,0:T(8,128)(2,1)} %get-tuple-element.34.q_ref, bf16[1024,1024]{1,0:T(8,128)(2,1)} %collective-permute-done.ko_ref.vo_ref, ...), custom_call_target="tpu_custom_call" | custom-call | flops 8589934592 | bytes 16777216 | tf_op jit(solution)/shard_map/attend/pallas_call | solution.py:246
  190.5 5.4 multiply_reduce_fusion.2
  198.3 2.6 copy.53.at_ref
  200.9 4.0 multiply_convert_fusion.a_ref
  204.9 18.5 %all-gather.10.cloned.1.call-done.wg_ref = bf16[1024,4608]{1,0:T(8,128)(2,1)} async-done(((bf16[32,4608]{1,0:T(8,128)(2,1)}), bf16[1024,4608]{1,0:T(8,128)(2,1)}) %all-gather.10.cloned.1.call-update) | async-done | bytes 9437200 | tf_op jit(solution)/shard_map/all_gather | solution.py:506
  223.4 84.0 %all-gather.12.cloned.1.call-done.wu_ref = bf16[1024,4608]{1,0:T(8,128)(2,1)} async-done(((bf16[32,4608]{1,0:T(8,128)(2,1)}), bf16[1024,4608]{1,0:T(8,128)(2,1)}) %all-gather.12.cloned.1.call-update) | async-done | bytes 9437200 | tf_op jit(solution)/shard_map/all_gather | solution.py:506
  307.4 83.4 %all-gather.14.cloned.1.call-done.wd_ref = bf16[4608,1024]{1,0:T(8,128)(2,1)} async-done(((bf16[144,1024]{1,0:T(8,128)(2,1)}), bf16[4608,1024]{1,0:T(8,128)(2,1)}) %all-gather.14.cloned.1.call-update) | async-done | bytes 9437200 | tf_op jit(solution)/shard_map/all_gather | solution.py:506
  393.4 103.7 %feed.1 = (f32[1024,1024]{1,0:T(8,128)}, f32[1024,1024]{1,0:T(8,128)}, bf16[1024,4608]{1,0:T(8,128)(2,1)}, bf16[1024,4608]{1,0:T(8,128)(2,1)}, bf16[4608,1024]{1,0:T(8,128)(2,1)}) custom-call(bf16[1024,1024]{1,0:T(8,128)(2,1)} %multiply_convert_fusion.a_ref, bf16[1024,1024]{1,0:T(8,128)(2,1)} %copy.53.at_ref, bf16[1024,1024]{1,0:T(8,128)(2,1)} %bitcast.33, ...), custom_call_target="tpu_custom_call" | custom-call | flops 86973087744 | bytes 56623104 | tf_op jit(solution)/shard_map/feed/pallas_call | solution.py:439
  497.1 4.7 multiply_reduce_fusion
  506.6 3.8 convolution_convert_fusion.1
  510.5 5.9 convolution_convert_fusion.2.do_ref
  517.0 63.8 %attend_back.1 = (f32[1024,1024]{1,0:T(8,128)}, f32[2048,512]{1,0:T(8,128)}, f32[2048,512]{1,0:T(8,128)}) custom-call(s32[5]{0:T(128)} %pad_add_fusion.low_ref, s32[8,1024]{1,0:T(8,128)} %broadcast_in_dim.53.first_ref, bf16[1024,1024]{1,0:T(8,128)(2,1)} %get-tuple-element.34.q_ref, bf16[1024,1024]{1,0:T(8,128)(2,1)} %convolution_convert_fusion.2.do_ref, ...), custom_call_target="tpu_custom_call" | custom-call | flops 21474836480 | bytes 41943040 | tf_op jit(solution)/shard_map/attend_back/pallas_call | solution.py:370
  580.8 2.9 constant_dynamic-update-slice_fusion.1
  586.4 87.7 %collective-permute-done.1 = bf16[1024,1024]{1,0:T(8,128)(2,1)S(1)} collective-permute-done((bf16[1024,1024]{1,0:T(8,128)(2,1)S(1)}, bf16[1024,1024]{1,0:T(8,128)(2,1)S(1)}, u32[]{:S(2)}, u32[]{:S(2)}) %collective-permute-start.1) | collective-permute-done | bytes 2097184 | tf_op jit(solution)/shard_map/ppermute | solution.py:593
  674.1 2.7 slice_add_fusion.dkv_ref
  676.8 11.7 prep_back.1
  688.5 8.6 convolution_convert_fusion
  699.3 4.0 convert_bitcast_fusion
  703.3 8.8 fusion.10
  712.3 37.7 %all-reduce.1 = (f32[2,1024]{1,0:T(2,128)S(1)}, f32[2,64]{1,0:T(2,128)S(1)}) all-reduce(f32[2,1024]{1,0:T(2,128)S(1)} %pad_maximum_fusion.3, f32[2,64]{1,0:T(2,128)S(1)} %slice_add_fusion.1), channel_id=1, replica_groups=mesh['fsdp'=16,'seq'=2] {'fsdp','seq'}, use_global_device_ids=true, to_apply=%region_8.9 | all-reduce | flops 2176 | bytes 17408 | tf_op jit(solution)/shard_map/psum | solution.py:606
  751.2 5.5 fusion.9
  758.7 76.9 %reduce-scatter.6.cloned.1.call-done = bf16[32,2048]{1,0:T(8,128)(2,1)} async-done(((bf16[1024,2048]{1,0:T(8,128)(2,1)}), bf16[32,2048]{1,0:T(8,128)(2,1)}) %reduce-scatter.6.cloned.1.call-update) | async-done | bytes 131088 | tf_op jit(solution)/shard_map/reduce_scatter | solution.py:510
  837.6 137.0 %reduce-scatter.14.cloned.1.call-done = bf16[144,1024]{1,0:T(8,128)(2,1)} async-done(((bf16[4608,1024]{1,0:T(8,128)(2,1)}), bf16[144,1024]{1,0:T(8,128)(2,1)}) %reduce-scatter.14.cloned.1.call-update) | async-done | bytes 294928 | tf_op jit(solution)/shard_map/reduce_scatter | solution.py:510
  974.6 2.7 multiply_subtract_fusion.1
  977.3 137.8 %reduce-scatter.10.cloned.1.call-done = bf16[32,4608]{1,0:T(8,128)(2,1)} async-done(((bf16[1024,4608]{1,0:T(8,128)(2,1)}), bf16[32,4608]{1,0:T(8,128)(2,1)}) %reduce-scatter.10.cloned.1.call-update) | async-done | bytes 294928 | tf_op jit(solution)/shard_map/reduce_scatter | solution.py:510
  1115.1 141.3 %reduce-scatter.12.cloned.1.call-done = bf16[32,4608]{1,0:T(8,128)(2,1)} async-done(((bf16[1024,4608]{1,0:T(8,128)(2,1)}), bf16[32,4608]{1,0:T(8,128)(2,1)}) %reduce-scatter.12.cloned.1.call-update) | async-done | bytes 294928 | tf_op jit(solution)/shard_map/reduce_scatter | solution.py:510
  1256.4 4.2 multiply_subtract_fusion
  (121 shorter events, 34.7 us)
Async XLA Ops:
  7.2 7.3 copy-start.23
  7.2 7.5 copy-start.21
  7.2 69.2 %all-gather.6.cloned.1.call-start = ((), (), s32[]{:S(2)}) async-start(), calls=%async_computation.5 | async-start | bytes 4325376 | tf_op jit(solution)/shard_map/all_gather | solution.py:506
  9.0 181.5 %all-gather.8.cloned.1.call-start = ((), (), s32[]{:S(2)}) async-start(), calls=%async_computation.6 | async-start | bytes 2162688 | tf_op jit(solution)/shard_map/all_gather | solution.py:506
  10.6 8.7 copy-start.4
  10.6 212.8 %all-gather.10.cloned.1.call-start = ((), (), s32[]{:S(2)}) async-start(), calls=%async_computation.7 | async-start | bytes 9732096 | tf_op jit(solution)/shard_map/all_gather | solution.py:506
  13.0 294.4 %all-gather.12.cloned.1.call-start = ((), (), s32[]{:S(2)}) async-start(), calls=%async_computation.8 | async-start | bytes 9732096 | tf_op jit(solution)/shard_map/all_gather | solution.py:506
  13.6 377.3 %all-gather.14.cloned.1.call-start = ((), (), s32[]{:S(2)}) async-start(), calls=%async_computation.9 | async-start | bytes 9732096 | tf_op jit(solution)/shard_map/all_gather | solution.py:506
  14.4 742.3 %reduce-scatter.8.cloned.1.call-start = ((), (), s32[]{:S(2)}) async-start(), calls=%async_computation.11 | async-start | bytes 2162688 | tf_op jit(solution)/shard_map/reduce_scatter | solution.py:510
  19.8 65.8 %copy-start.15 = (f32[1024]{0:T(1024)}, f32[1024]{0:T(1024)S(1)}, u32[]{:S(2)}) copy-start(f32[1024]{0:T(1024)S(1)} %add_rsqrt_fusion.1) | copy-start | bytes 12292
  19.8 65.8 %copy-start.17 = (f32[1,1024]{1,0:T(1,128)}, f32[1,1024]{1,0:T(1,128)S(1)}, u32[]{:S(2)}) copy-start(f32[1,1024]{1,0:T(1,128)S(1)} %get-tuple-element.75) | copy-start | bytes 12292
  93.6 54.3 %collective-permute-start = (bf16[1024,1024]{1,0:T(8,128)(2,1)}, bf16[1024,1024]{1,0:T(8,128)(2,1)}, u32[]{:S(2)}, u32[]{:S(2)}) collective-permute-start(bf16[1024,1024]{1,0:T(8,128)(2,1)} %get-tuple-element.35.k_ref.v_ref), channel_id=1, source_target_pairs={{0,1},{2,3},{4,5},{6,7},{8,9},{10,11},{12,13},{14,15},{16,17},{18,... | collective-permute-start | bytes 6291464 | tf_op jit(solution)/shard_map/ppermute | solution.py:568
  393.4 108.4 %copy-start.10 = (bf16[1,1024,1024]{2,1,0:T(8,128)(2,1)S(1)}, bf16[1,1024,1024]{2,1,0:T(8,128)(2,1)}, u32[]{:S(2)}) copy-start(bf16[1,1024,1024]{2,1,0:T(8,128)(2,1)} %param.22) | copy-start | bytes 6291460
  510.4 325.1 %reduce-scatter.6.cloned.1.call-start = ((), (), s32[]{:S(2)}) async-start(), calls=%async_computation.10 | async-start | bytes 4325376 | tf_op jit(solution)/shard_map/reduce_scatter | solution.py:510
  585.1 89.0 %collective-permute-start.1 = (bf16[1024,1024]{1,0:T(8,128)(2,1)S(1)}, bf16[1024,1024]{1,0:T(8,128)(2,1)S(1)}, u32[]{:S(2)}, u32[]{:S(2)}) collective-permute-start(bf16[1024,1024]{1,0:T(8,128)(2,1)S(1)} %slice.49), channel_id=1, source_target_pairs={{1,0},{3,2},{5,4},{7,6},{9,8},{11,10},{13,12},{15,14},{17,16},{19,... | collective-permute-start | bytes 6291464 | tf_op jit(solution)/shard_map/ppermute | solution.py:593
  676.8 11.8 copy-start.5
  676.8 11.8 copy-start.16
  676.8 11.8 copy-start.18
  697.2 277.4 %reduce-scatter.14.cloned.1.call-start = ((), (), s32[]{:S(2)}) async-start(), calls=%async_computation.14 | async-start | bytes 9732096 | tf_op jit(solution)/shard_map/reduce_scatter | solution.py:510
  697.9 417.2 %reduce-scatter.10.cloned.1.call-start = ((), (), s32[]{:S(2)}) async-start(), calls=%async_computation.12 | async-start | bytes 9732096 | tf_op jit(solution)/shard_map/reduce_scatter | solution.py:510
  698.7 557.8 %reduce-scatter.12.cloned.1.call-start = ((), (), s32[]{:S(2)}) async-start(), calls=%async_computation.13 | async-start | bytes 9732096 | tf_op jit(solution)/shard_map/reduce_scatter | solution.py:510
  703.3 8.9 copy-start.26
  703.3 46.6 %copy-start.22 = (f32[2,64]{1,0:T(2,128)S(1)}, f32[2,64]{1,0:T(2,128)}, u32[]{:S(2)}) copy-start(f32[2,64]{1,0:T(2,128)} %param.27) | copy-start | bytes 1540
  703.3 46.6 %copy-start.24 = (f32[2,64]{1,0:T(2,128)S(1)}, f32[2,64]{1,0:T(2,128)}, u32[]{:S(2)}) copy-start(f32[2,64]{1,0:T(2,128)} %param.28) | copy-start | bytes 1540
  703.3 46.6 %copy-start.25 = (f32[2,64]{1,0:T(2,128)S(1)}, f32[2,64]{1,0:T(2,128)}, u32[]{:S(2)}) copy-start(f32[2,64]{1,0:T(2,128)} %param.29) | copy-start | bytes 1540
  703.3 47.2 %copy-start.14 = (f32[2,1024]{1,0:T(2,128)S(1)}, f32[2,1024]{1,0:T(2,128)}, u32[]{:S(2)}) copy-start(f32[2,1024]{1,0:T(2,128)} %param.24) | copy-start | bytes 24580
  703.3 47.2 %copy-start.19 = (f32[2,1024]{1,0:T(2,128)S(1)}, f32[2,1024]{1,0:T(2,128)}, u32[]{:S(2)}) copy-start(f32[2,1024]{1,0:T(2,128)} %param.25) | copy-start | bytes 24580
  703.3 47.2 %copy-start.20 = (f32[2,1024]{1,0:T(2,128)S(1)}, f32[2,1024]{1,0:T(2,128)}, u32[]{:S(2)}) copy-start(f32[2,1024]{1,0:T(2,128)} %param.26) | copy-start | bytes 24580
  751.2 84.4 %copy-start.11 = (f32[32,2048]{1,0:T(8,128)S(1)}, f32[32,2048]{1,0:T(8,128)}, u32[]{:S(2)}) copy-start(f32[32,2048]{1,0:T(8,128)} %param.30) | copy-start | bytes 786436
  751.2 223.5 %copy-start.9 = (f32[144,1024]{1,0:T(8,128)S(1)}, f32[144,1024]{1,0:T(8,128)}, u32[]{:S(2)}) copy-start(f32[144,1024]{1,0:T(8,128)} %param.39) | copy-start | bytes 1769476
  751.2 223.5 %copy-start.12 = (f32[144,1024]{1,0:T(8,128)S(1)}, f32[144,1024]{1,0:T(8,128)}, u32[]{:S(2)}) copy-start(f32[144,1024]{1,0:T(8,128)} %param.40) | copy-start | bytes 1769476
  756.7 499.7 %copy-start.6 = (f32[32,9216]{1,0:T(8,128)S(1)}, f32[32,9216]{1,0:T(8,128)}, u32[]{:S(2)}) copy-start(f32[32,9216]{1,0:T(8,128)} %param.36) | copy-start | bytes 3538948
  (10 other events, 42.8 us)
Sparse Core Ops, SparseCore 0:
  11.6 64.7 all-gather.5
  80.0 56.3 all-gather.7
  139.8 83.5 all-gather.9
  226.8 80.6 all-gather.11
  310.2 80.6 all-gather.13
  510.5 136.6 reduce-scatter.7
  697.3 138.1 reduce-scatter.5
  842.4 132.1 reduce-scatter.13
  980.5 134.5 reduce-scatter.9
  1121.9 134.5 reduce-scatter.11

commit v2 on v1

--- a/solution.py
+++ b/solution.py
@@ -31,6 +31,7 @@
 QUERY_BLOCK = 256
 KEY_BLOCK = 256
 FF_BLOCK = 256
+PIECES = 4
 
 
 def dot(a, b):
@@ -67,7 +68,7 @@
     )
 
 
-def prep_kernel(raw_ref, gain_ref, cos_ref, sin_ref, q_ref, kv_ref):
+def prep_kernel(raw_ref, gain_ref, cos_ref, sin_ref, q_ref, *kv_refs):
     cosine, sine = cos_ref[...], sin_ref[...]
     for group in range(12):
         part = slice(group * LANES, (group + 1) * LANES)
@@ -78,8 +79,10 @@
         if group < 8:
             q_ref[:, part] = (out * HEAD_SIZE**-0.5).astype(BF16)
         else:
-            kv_ref[:, slice((group - 8) * LANES, (group - 7) * LANES)] = out.astype(BF16)
-    kv_ref[:, KEY_FEATURES:] = raw_ref[:, QUERY_FEATURES + KEY_FEATURES :].astype(BF16)
+            kv_ref = kv_refs[group - 8]
+            kv_ref[:, :LANES] = out.astype(BF16)
+            value = raw_ref[:, slice((group + 4) * LANES, (group + 5) * LANES)]
+            kv_ref[:, LANES:] = value.astype(BF16)
 
 
 def prep(raw, gains, cosine, sine):
@@ -91,11 +94,9 @@
         name="prep",
         grid=(rows // block,),
         in_specs=[whole(2048), pl.BlockSpec((8, LANES), lambda i: (0, 0)), whole(LANES), whole(LANES)],
-        out_specs=[whole(QUERY_FEATURES), whole(2 * KEY_FEATURES)],
-        out_shape=[
-            jax.ShapeDtypeStruct((rows, QUERY_FEATURES), BF16),
-            jax.ShapeDtypeStruct((rows, 2 * KEY_FEATURES), BF16),
-        ],
+        out_specs=[whole(QUERY_FEATURES)] + [whole(2 * LANES)] * PIECES,
+        out_shape=[jax.ShapeDtypeStruct((rows, QUERY_FEATURES), BF16)]
+        + [jax.ShapeDtypeStruct((rows, 2 * LANES), BF16)] * PIECES,
         compiler_params=params(),
         cost_estimate=pl.CostEstimate(
             flops=rows * 2048 * 40, transcendentals=rows * 24, bytes_accessed=rows * 2048 * 6
@@ -103,7 +104,9 @@
     )(raw, gains, cosine, sine)
 
 
-def prep_back_kernel(raw_ref, gain_ref, cos_ref, sin_ref, dq_ref, dkv_ref, out_ref, dg_ref):
+def prep_back_kernel(raw_ref, gain_ref, cos_ref, sin_ref, *rest):
+    dq_refs, own_refs, back_refs = (rest[PIECES * i : PIECES * (i + 1)] for i in range(3))
+    out_ref, dg_ref = rest[3 * PIECES :]
     cosine, sine = cos_ref[...], sin_ref[...]
     sums = [jnp.zeros((1, LANES), F32), jnp.zeros((1, LANES), F32)]
     for group in range(12):
@@ -112,16 +115,19 @@
         which = 0 if group < 8 else 1
         gain = gain_ref[which : which + 1]
         if group < 8:
-            d = dq_ref[:, part] * HEAD_SIZE**-0.5
+            half = slice(group % 2 * LANES, (group % 2 + 1) * LANES)
+            d = dq_refs[group // 2][:, half] * HEAD_SIZE**-0.5
         else:
-            d = dkv_ref[:, slice((group - 8) * LANES, (group - 7) * LANES)]
+            own, back = own_refs[group - 8], back_refs[group - 8]
+            d = own[:, :LANES] + back[:, :LANES].astype(F32)
+            value = slice((group + 4) * LANES, (group + 5) * LANES)
+            out_ref[:, value] = (own[:, LANES:] + back[:, LANES:].astype(F32)).astype(BF16)
         d = d * cosine - swap_halves(d) * sine
         r = lax.rsqrt(head_mean(u * u) + NORM_EPS)
         w = d * gain
         n = u * r
         out_ref[:, part] = (r * (w - n * head_mean(w * n))).astype(BF16)
         sums[which] += jnp.sum(d * n, axis=0, keepdims=True)
-    out_ref[:, QUERY_FEATURES + KEY_FEATURES :] = dkv_ref[:, KEY_FEATURES:].astype(BF16)
 
     @pl.when(pl.program_id(0) == 0)
     def _():
@@ -131,7 +137,7 @@
     dg_ref[1:2] += sums[1]
 
 
-def prep_back(raw, gains, cosine, sine, dq, dkv):
+def prep_back(raw, gains, cosine, sine, dq, own, back):
     rows = raw.shape[0]
     block = min(rows, 256)
     whole = lambda width: pl.BlockSpec((block, width), lambda i: (i, 0))
@@ -145,9 +151,8 @@
             small,
             whole(LANES),
             whole(LANES),
-            whole(QUERY_FEATURES),
-            whole(2 * KEY_FEATURES),
-        ],
+        ]
+        + [whole(2 * LANES)] * (3 * PIECES),
         out_specs=[whole(2048), small],
         out_shape=[
             jax.ShapeDtypeStruct((rows, 2048), BF16),
@@ -157,7 +162,7 @@
         cost_estimate=pl.CostEstimate(
             flops=rows * 2048 * 60, transcendentals=rows * 24, bytes_accessed=rows * 2048 * 10
         ),
-    )(raw, gains, cosine, sine, dq, dkv)
+    )(raw, gains, cosine, sine, *dq, *own, *back)
 
 
 def twice(pair, odd):
@@ -237,25 +242,25 @@
     lse_ref[0] = jnp.transpose(logs)[0:8, :]
 
 
-def attend(q, others, own, low, first):
+def attend(piece, q, others, own, low, first):
     rows = q.shape[0]
     block = min(QUERY_BLOCK, rows)
     turns = rows // block
     total = others.shape[0] + rows
-    pair = lambda size, off: pl.BlockSpec((size, LANES), lambda h, t, low: (0, off + h // 2))
+    pair = lambda size, off: pl.BlockSpec((size, LANES), lambda h, t, low: (0, off))
     return pl.pallas_call(
         attend_kernel,
         name="attend",
         grid_spec=pltpu.PrefetchScalarGridSpec(
             num_scalar_prefetch=1,
-            grid=(KEY_VALUE_HEADS, turns),
+            grid=(2, turns),
             in_specs=[
                 pl.BlockSpec((block, LANES), lambda h, t, low: (t, 0)),
-                pl.BlockSpec((block, LANES), lambda h, t, low: (t, h)),
+                pl.BlockSpec((block, LANES), lambda h, t, low: (t, 2 * piece + h)),
                 pair(others.shape[0], 0),
-                pair(others.shape[0], 4),
+                pair(others.shape[0], 1),
                 pair(rows, 0),
-                pair(rows, 4),
+                pair(rows, 1),
             ],
             out_specs=[
                 pl.BlockSpec((block, LANES), lambda h, t, low: (t, h)),
@@ -264,12 +269,12 @@
             scratch_shapes=[pltpu.VMEM((total, LANES), BF16), pltpu.VMEM((total, 2 * LANES), BF16)],
         ),
         out_shape=[
-            jax.ShapeDtypeStruct((rows, QUERY_FEATURES), BF16),
-            jax.ShapeDtypeStruct((KEY_VALUE_HEADS, 8 * turns, 2 * block), F32),
+            jax.ShapeDtypeStruct((rows, 2 * LANES), BF16),
+            jax.ShapeDtypeStruct((2, 8 * turns, 2 * block), F32),
         ],
         compiler_params=params(),
         cost_estimate=pl.CostEstimate(
-            flops=rows * 1024 * 1024 * 8, transcendentals=rows * 1024 * 16, bytes_accessed=16 << 20
+            flops=rows * 1024 * 1024 * 8, transcendentals=rows * 1024 * 4, bytes_accessed=4 << 20
         ),
     )(low, first, q, others, others, own, own)
 
@@ -286,8 +291,8 @@
     k_ref,
     v_ref,
     dq_ref,
-    dk_ref,
-    dv_ref,
+    far_ref,
+    near_ref,
     keys,
     values,
     dkeys,
@@ -343,48 +348,52 @@
     @pl.when(turn == pl.num_programs(1) - 1)
     def _():
         odd = lax.rem(head, 2)
-        for source, target in ((dkeys, dk_ref), (dvalues, dv_ref)):
+        far = far_ref.shape[0]
+        for source, off in ((dkeys, 0), (dvalues, LANES)):
             for start in range(0, source.shape[0], 256):
-                part = slice(start, start + 256)
-                both = source[part, :]
+                both = source[start : start + 256, :]
                 both = both + pltpu.roll(both, HEAD_SIZE, 1)
                 lane = lax.broadcasted_iota(jnp.int32, both.shape, 1)
                 mine = (lane < HEAD_SIZE) != (odd == 1)
+                target, to = (far_ref, start) if start < far else (near_ref, start - far)
+                part = (slice(to, to + 256), slice(off, off + LANES))
 
                 @pl.when(odd == 0)
                 def _():
-                    target[part, :] = both
+                    target[part] = both.astype(target.dtype)
 
                 @pl.when(odd == 1)
                 def _():
-                    target[part, :] = jnp.where(mine, both, target[part, :])
-
-
-def attend_back(q, d_mixed, mixed, lse, others, own, low, first_lane):
+                    target[part] = jnp.where(mine, both, target[part].astype(F32)).astype(target.dtype)
+
+
+def attend_back(piece, q, d_mixed, mixed, lse, others, own, low, first_lane):
     rows = q.shape[0]
     block = min(QUERY_BLOCK, rows)
     turns = rows // block
     total = others.shape[0] + rows
-    pair = lambda size, off: pl.BlockSpec((size, LANES), lambda h, t, low: (0, off + h // 2))
+    pair = lambda size, off: pl.BlockSpec((size, LANES), lambda h, t, low: (0, off))
+    whole = lambda size: pl.BlockSpec((size, 2 * LANES), lambda h, t, low: (0, 0))
     tile = pl.BlockSpec((block, LANES), lambda h, t, low: (t, h))
+    tile_of_all = pl.BlockSpec((block, LANES), lambda h, t, low: (t, 2 * piece + h))
     return pl.pallas_call(
         attend_back_kernel,
         name="attend_back",
         grid_spec=pltpu.PrefetchScalarGridSpec(
             num_scalar_prefetch=1,
-            grid=(KEY_VALUE_HEADS, turns),
+            grid=(2, turns),
             in_specs=[
                 pl.BlockSpec((8, block), lambda h, t, low: (0, t)),
-                tile,
-                tile,
+                tile_of_all,
+                tile_of_all,
                 tile,
                 pl.BlockSpec((1, 8, 2 * block), lambda h, t, low: (h, t, 0)),
                 pair(others.shape[0], 0),
-                pair(others.shape[0], 4),
+                pair(others.shape[0], 1),
                 pair(rows, 0),
-                pair(rows, 4),
+                pair(rows, 1),
             ],
-            out_specs=[tile, pair(total, 0), pair(total, 0)],
+            out_specs=[tile, whole(others.shape[0]), whole(rows)],
             scratch_shapes=[
                 pltpu.VMEM((total, LANES), BF16),
                 pltpu.VMEM((total, LANES), BF16),
@@ -393,24 +402,38 @@
             ],
         ),
         out_shape=[
-            jax.ShapeDtypeStruct((rows, QUERY_FEATURES), F32),
-            jax.ShapeDtypeStruct((total, KEY_FEATURES), F32),
-            jax.ShapeDtypeStruct((total, KEY_FEATURES), F32),
+            jax.ShapeDtypeStruct((rows, 2 * LANES), F32),
+            jax.ShapeDtypeStruct((others.shape[0], 2 * LANES), BF16),
+            jax.ShapeDtypeStruct((rows, 2 * LANES), F32),
         ],
         compiler_params=params(),
         cost_estimate=pl.CostEstimate(
-            flops=rows * 1024 * 1024 * 20, transcendentals=rows * 1024 * 16, bytes_accessed=40 << 20
+            flops=rows * 1024 * 1024 * 12, transcendentals=rows * 1024 * 4, bytes_accessed=10 << 20
         ),
     )(low, first_lane, q, d_mixed, mixed, lse, others, others, own, own)
 
 
 def feed_kernel(
-    a_ref, at_ref, g_ref, wg_ref, wu_ref, wd_ref, y_in, b_in, y_ref, b_ref, gg_ref, gu_ref, gd_ref
+    a_ref,
+    atg_ref,
+    atu_ref,
+    g_ref,
+    wg_ref,
+    wu_ref,
+    wd_ref,
+    y_in,
+    y_ref,
+    b_ref,
+    gg_ref,
+    ggs_ref,
+    gu_ref,
+    gus_ref,
+    gd_ref,
 ):
     @pl.when(pl.program_id(0) == 0)
     def _():
         y_ref[...] = y_in[...]
-        b_ref[...] = b_in[...]
+        b_ref[...] = jnp.zeros_like(b_ref)
 
     a, g = a_ref[...], g_ref[...]
     wg, wu, wd = wg_ref[...], wu_ref[...], wd_ref[...]
@@ -424,17 +447,20 @@
     d_up = (d_hidden * swish).astype(BF16)
     y_ref[...] += dot(hidden, wd)
     b_ref[...] += dot_cols(d_gate, wg) + dot_cols(d_up, wu)
-    at = at_ref[...]
-    gg_ref[...] = dot(at, d_gate).astype(BF16)
-    gu_ref[...] = dot(at, d_up).astype(BF16)
+    half = atg_ref.shape[0] // 2
+    gg_ref[...] = dot(atg_ref[:half], d_gate).astype(BF16)
+    ggs_ref[...] = dot(atg_ref[half:], d_gate).astype(BF16)
+    gu_ref[...] = dot(atu_ref[:half], d_up).astype(BF16)
+    gus_ref[...] = dot(atu_ref[half:], d_up).astype(BF16)
     gd_ref[...] = dot_rows(hidden, g).astype(BF16)
 
 
-def feed(a, at, g, w_gate, w_up, w_down, y, b):
+def feed(a, at_gate, at_up, g, w_gate, w_up, w_down, y):
     rows, width = a.shape[0], w_gate.shape[1]
     turns = width // FF_BLOCK
     fixed = lambda s: pl.BlockSpec(s, lambda j: (0, 0))
     col = pl.BlockSpec((D, FF_BLOCK), lambda j: (0, j))
+    half_col = pl.BlockSpec((D // 2, FF_BLOCK), lambda j: (0, j))
     row = pl.BlockSpec((FF_BLOCK, D), lambda j: (j, 0))
     return pl.pallas_call(
         feed_kernel,
@@ -443,26 +469,25 @@
         in_specs=[
             fixed((rows, D)),
             fixed((D, rows)),
+            fixed((D, rows)),
             fixed((rows, D)),
             col,
             col,
             row,
             fixed((rows, D)),
-            fixed((rows, D)),
         ],
-        out_specs=[fixed((rows, D)), fixed((rows, D)), col, col, row],
+        out_specs=[fixed((rows, D)), fixed((rows, D))] + [half_col] * 4 + [row],
         out_shape=[
             jax.ShapeDtypeStruct((rows, D), F32),
             jax.ShapeDtypeStruct((rows, D), F32),
-            jax.ShapeDtypeStruct((D, width), BF16),
-            jax.ShapeDtypeStruct((D, width), BF16),
-            jax.ShapeDtypeStruct((width, D), BF16),
-        ],
+        ]
+        + [jax.ShapeDtypeStruct((D // 2, width), BF16)] * 4
+        + [jax.ShapeDtypeStruct((width, D), BF16)],
         compiler_params=params(60),
         cost_estimate=pl.CostEstimate(
             flops=18 * rows * D * width, transcendentals=rows * width, bytes_accessed=12 * D * width
         ),
-    )(a, at, g, w_gate, w_up, w_down, y, b)
+    )(a, at_gate, at_up, g, w_gate, w_up, w_down, y)
 
 
 def rms_scale(v):
@@ -506,8 +531,202 @@
     return lax.all_gather(shard, ALL, axis=0, tiled=True)
 
 
-def scatter(terms):
-    return lax.psum_scatter(terms, ALL, scatter_dimension=0, tiled=True).astype(F32)
+def dims():
+    rest = lax.axis_size("fsdp") // 8
+    return {
+        "z": ("fsdp", 2 * rest, 4),
+        "y": ("fsdp", 2, rest),
+        "c": ("fsdp", 1, 2),
+        "x": ("seq", 1, lax.axis_size("seq")),
+    }
+
+
+def place_along(direction):
+    axis, stride, size = dims()[direction]
+    return lax.rem(lax.div(lax.axis_index(axis), stride), size)
+
+
+def swap(value, direction, distance):
+    axis, stride, _ = dims()[direction]
+    pairs = [(i, i ^ (distance * stride)) for i in range(lax.axis_size(axis))]
+    return lax.ppermute(value, axis, pairs)
+
+
+def relative_rows(order, count):
+    sizes = {k: v[2] for k, v in dims().items()}
+    width = count
+    for size in sizes.values():
+        width //= size
+    index = jnp.arange(count, dtype=jnp.int32)
+    left = index // width
+    place = {}
+    for k in reversed(order):
+        place[k] = jnp.bitwise_xor(left % sizes[k], place_along(k))
+        left = left // sizes[k]
+    block = jnp.zeros_like(index)
+    for k in "zycx":
+        block = block * sizes[k] + place[k]
+    row = block * width + index % width
+    return (row[:, None] == index[None, :]).astype(BF16)
+
+
+def transpose_in_order(hot, value):
+    return dot_cols(hot, value).astype(BF16)
+
+
+MESH = pl.DeviceIdType.MESH
+NAMES = "zycx"
+
+
+def neighbour(direction, distance):
+    axis, stride, _ = dims()[direction]
+    here = place_along(direction)
+    return {axis: lax.axis_index(axis) + (jnp.bitwise_xor(here, distance) - here) * stride}
+
+
+def greet():
+    barrier = pltpu.get_barrier_semaphore()
+    count = 0
+    for k in NAMES:
+        for d in range(1, dims()[k][2]):
+            pl.semaphore_signal(barrier, 1, device_id=neighbour(k, d), device_id_type=MESH)
+            count += 1
+    pl.semaphore_wait(barrier, count)
+
+
+def part_view(full, at, columns):
+    index = tuple(at[k] if k in at else slice(None) for k in NAMES)
+    return full.at[index + (slice(None), columns)]
+
+
+def gather_kernel(plan, *refs):
+    count = 1 + max(p[0] for p in plan)
+    shards, fulls = refs[:count], refs[count : 2 * count]
+    local, send, recv = refs[2 * count :]
+    here = {k: place_along(k) for k in NAMES}
+    own = []
+    for t in range(count):
+        copy = pltpu.make_async_copy(shards[t], part_view(fulls[t], here, slice(None)), local.at[t])
+        copy.start()
+        own.append(copy)
+    greet()
+    posted = []
+
+    def post(source, target, k, d):
+        n = len(posted)
+        copy = pltpu.make_async_remote_copy(
+            source, target, send.at[n], recv.at[n], device_id=neighbour(k, d), device_id_type=MESH
+        )
+        copy.start()
+        posted.append(copy)
+        return copy
+
+    coming = {}
+    for when in range(len(plan) + 3):
+        for step in range(4):
+            p = when - step
+            if not 0 <= p < len(plan):
+                continue
+            t, column, width, order = plan[p]
+            columns = pl.ds(column, width)
+            full = fulls[t]
+            if step == 0:
+                k = order[0]
+                target = part_view(full, here, columns)
+                coming[p, 0] = [
+                    post(shards[t].at[:, columns], target, k, d) for d in range(1, dims()[k][2])
+                ]
+                continue
+            if own[t] is not None:
+                own[t].wait()
+                own[t] = None
+            for copy in coming[p, step - 1]:
+                copy.wait_recv()
+            at = {k: v for k, v in here.items() if k not in order[:step]}
+            if step < 3:
+                k = order[step]
+                view = part_view(full, at, columns)
+                coming[p, step] = [post(view, view, k, d) for d in range(1, dims()[k][2])]
+                if step == 2:
+                    coming[p, 3] = [post(view, view, "c", 1)]
+            else:
+                k = order[2]
+                for d in range(1, dims()[k][2]):
+                    view = part_view(full, {**at, k: jnp.bitwise_xor(here[k], d)}, columns)
+                    coming[p, 3].append(post(view, view, "c", 1))
+    for p in range(len(plan)):
+        for copy in coming[p, 3]:
+            copy.wait_recv()
+    for copy in posted:
+        copy.wait_send()
+
+
+def plan_parts(arrays, cut):
+    plan = []
+    for t, shard in enumerate(arrays):
+        pieces = max(1, shard.shape[1] // cut)
+        width = shard.shape[1] // pieces
+        for i in range(pieces):
+            plan.append((t, i * width, width, "zxy" if len(plan) % 2 else "zyx"))
+    return plan
+
+
+def gather_all(shards, cut, number):
+    plan = plan_parts(shards, cut)
+    size = {k: dims()[k][2] for k in NAMES}
+    total = sum(sum(size[k] - 1 for k in order) + size[order[2]] for _, _, _, order in plan)
+    fulls = pl.pallas_call(
+        functools.partial(gather_kernel, plan),
+        name="gather_all",
+        in_specs=[pl.BlockSpec(memory_space=pl.ANY)] * len(shards),
+        out_specs=[pl.BlockSpec(memory_space=pl.ANY)] * len(shards),
+        out_shape=[
+            jax.ShapeDtypeStruct((*(size[k] for k in NAMES), *shard.shape), shard.dtype)
+            for shard in shards
+        ],
+        scratch_shapes=[
+            pltpu.SemaphoreType.DMA((len(shards),)),
+            pltpu.SemaphoreType.DMA((total,)),
+            pltpu.SemaphoreType.DMA((total,)),
+        ],
+        compiler_params=pltpu.CompilerParams(collective_id=number, has_side_effects=True),
+    )(*shards)
+    return [full.reshape(-1, full.shape[-1]) for full in fulls]
+
+
+def after(values, earlier):
+    return lax.optimization_barrier((values, earlier))[0]
+
+
+def sum_everywhere(terms):
+    for k, (_, _, size) in dims().items():
+        d = 1
+        while d < size:
+            terms = terms + swap(terms, k, d)
+            d *= 2
+    return terms
+
+
+def add_swapped(keep, send, direction):
+    return (keep.astype(F32) + swap(send, direction, 1).astype(F32)).astype(BF16)
+
+
+def add_along(terms, direction, last=False):
+    size = dims()[direction][2]
+    step = terms.shape[0] // size
+    total = terms[:step].astype(F32)
+    for d in range(1, size):
+        total = total + swap(terms[d * step : (d + 1) * step], direction, d).astype(F32)
+    return total if last else total.astype(BF16)
+
+
+def own_part(terms, direction, last=False):
+    at, here, size = NAMES.index(direction), place_along(direction), dims()[direction][2]
+    total = lax.dynamic_slice_in_dim(terms, here, 1, at).astype(F32)
+    for d in range(1, size):
+        sent = lax.dynamic_slice_in_dim(terms, jnp.bitwise_xor(here, d), 1, at)
+        total = total + swap(sent, direction, d).astype(F32)
+    return total if last else total.astype(BF16)
 
 
 def per_device(
@@ -537,11 +756,8 @@
     turn_here = lax.axis_index("seq")
     rows = inputs.shape[1]
     block = min(QUERY_BLOCK, rows)
-    w_qkv = gather(qkv_master.astype(BF16))
-    w_out = gather(out_master.astype(BF16))
-    w_down = gather(down_master.astype(BF16))
-    w_gate = gather(gate_up_master[:, :FF].astype(BF16))
-    w_up = gather(gate_up_master[:, FF:].astype(BF16))
+    w_qkv, w_out = gather_all([qkv_master.astype(BF16), out_master.astype(BF16)], 512, 1)
+    w_down = gather(after(down_master.astype(BF16), w_qkv))
 
     places = turn_here * rows + jnp.arange(rows, dtype=jnp.int32)
     row_lengths = lengths[0]
@@ -563,47 +779,83 @@
     normed_first = (x * scale_first * norm_gains[0]).astype(BF16)
     raw = jnp.dot(normed_first, w_qkv, preferred_element_type=F32)
     gain_rows = jnp.pad(jnp.tile(qk_gains, (1, 2)), ((0, 6), (0, 0)))
-    q, kv = prep(raw, gain_rows, cosine, sine)
+    q, *own = prep(raw, gain_rows, cosine, sine)
+    pieces = range(PIECES)
     if seq_width == 2:
-        others = lax.ppermute(kv, "seq", [(0, 1)])
-        own = kv
+        others = [lax.ppermute(p, "seq", [(0, 1)]) for p in own]
     else:
-        everyone = lax.all_gather(kv, "seq", axis=0, tiled=True)
-        others, own = everyone, kv
-    mixed, lse = attend(q, others, own, low, first_wide)
+        others = [lax.all_gather(p, "seq", axis=0, tiled=True) for p in own]
+    mixes, lses = zip(*[attend(p, q, others[p], own[p], low, first_wide) for p in pieces])
+    mixed = jnp.concatenate(mixes, axis=1)
     x_mid = x + jnp.dot(mixed, w_out, preferred_element_type=F32)
     scale_second = rms_scale(x_mid)
     normed_second = (x_mid * scale_second * norm_gains[1]).astype(BF16)
     g = cotangent[0]
-    out_sum, d_b, grad_gate, grad_up, grad_down = feed(
-        normed_second, normed_second.T, g, w_gate, w_up, w_down, x_mid, jnp.zeros_like(x_mid)
+    w_gate, w_up = gather_all(
+        after([gate_up_master[:, :FF].astype(BF16), gate_up_master[:, FF:].astype(BF16)], normed_second),
+        1152,
+        2,
+    )
+    hot_x, hot_y = relative_rows("cxyz", D), relative_rows("cyxz", D)
+    out_sum, d_b, gate_keep, gate_send, up_keep, up_send, grad_down = feed(
+        normed_second,
+        transpose_in_order(hot_x, normed_second),
+        transpose_in_order(hot_y, normed_second),
+        g,
+        w_gate,
+        w_up,
+        w_down,
+        x_mid,
     )
     outputs = out_sum.astype(BF16)
-    gate_grad = scatter(grad_gate)
-    up_grad = scatter(grad_up)
-    down_grad = scatter(grad_down)
+    gate_1 = add_swapped(gate_keep, gate_send, "c")
+    up_1 = add_swapped(up_keep, up_send, "c")
+    sizes = [dims()[k][2] for k in NAMES]
+    down_1 = own_part(grad_down.reshape(*sizes, FF // math.prod(sizes), D), "c")
     d_norm, d_gain_second = rms_back(x_mid, scale_second, norm_gains[1], d_b)
     d_mid = g.astype(F32) + d_norm
     d_attn = d_mid.astype(BF16)
     d_mixed = dot_cols(d_attn, w_out).astype(BF16)
-    out_grad = scatter(dot_rows(mixed, d_attn).astype(BF16))
-    dq, dk, dv = attend_back(q, d_mixed, mixed, lse, others, own, low, first_lane)
-    d_all = jnp.concatenate([dk, dv], axis=1)
+    out_terms = transpose_in_order(hot_y, mixed)
+    half = QUERY_FEATURES // 2
+    out_1 = add_swapped(
+        dot(out_terms[:half], d_attn).astype(BF16), dot(out_terms[half:], d_attn).astype(BF16), "c"
+    )
+
+    def back_piece(p, earlier):
+        d = after(d_mixed, earlier)
+        return attend_back(p, q, d, mixes[p], lses[p], others[p], own[p], low, first_lane)
+
+    parts = [back_piece(0, (gate_1, up_1))]
+    parts.append(back_piece(1, (out_1, down_1)))
+    gate_2, up_2 = add_along(gate_1, "x"), add_along(up_1, "y")
+    parts.append(back_piece(2, (gate_2, up_2)))
+    gate_3, up_3 = add_along(gate_2, "y"), add_along(up_2, "x")
+    down_2, out_2 = own_part(down_1, "x"), add_along(out_1, "y")
+    parts.append(back_piece(3, (gate_3, up_3)))
+    gate_grad, up_grad = add_along(gate_3, "z", True), add_along(up_3, "z", True)
+    down_3, out_3 = own_part(down_2, "y"), add_along(out_2, "x")
+    down_grad, out_grad = own_part(down_3, "z", True), add_along(out_3, "z", True)
+    down_grad = down_grad.reshape(-1, D)
+    dq, far, near = zip(*parts)
     if seq_width == 2:
-        back = lax.ppermute(d_all[:rows].astype(BF16), "seq", [(1, 0)])
-        dkv = d_all[rows:] + back.astype(F32)
+        back = [lax.ppermute(p, "seq", [(1, 0)]) for p in far]
     else:
-        dkv = lax.psum_scatter(
-            d_all[: seq_width * rows].astype(BF16), "seq", scatter_dimension=0, tiled=True
-        ).astype(F32)
-    d_qkv, d_gain_qk = prep_back(raw, gain_rows, cosine, sine, dq, dkv)
-    qkv_grad = scatter(dot_rows(normed_first, d_qkv).astype(BF16))
+        back = [lax.psum_scatter(p, "seq", scatter_dimension=0, tiled=True) for p in far]
+    d_qkv, d_gain_qk = prep_back(raw, gain_rows, cosine, sine, dq, near, back)
+    first_terms = transpose_in_order(hot_x, normed_first)
+    qkv_1 = add_swapped(
+        dot(first_terms[: D // 2], d_qkv).astype(BF16), dot(first_terms[D // 2 :], d_qkv).astype(BF16), "c"
+    )
+    qkv_grad = add_along(add_along(add_along(qkv_1, "x"), "y"), "z", True)
     d_a = dot_cols(d_qkv, w_qkv)
     d_x, d_gain_first = rms_back(x, scale_first, norm_gains[0], d_a)
     input_grad = (d_mid + d_x)[None]
-    norm_terms = jnp.stack([d_gain_first, d_gain_second])
-    qk_terms = d_gain_qk[:2, :HEAD_SIZE] + d_gain_qk[:2, HEAD_SIZE:]
-    norm_grad, qk_grad = lax.psum((norm_terms, qk_terms), ALL)
+    gain_terms = jnp.pad(d_gain_qk[:2], ((0, 0), (0, D - LANES)))
+    gain_terms = jnp.concatenate([d_gain_first[None], d_gain_second[None], gain_terms], axis=0)
+    gain_sums = sum_everywhere(jnp.pad(gain_terms, ((0, 4), (0, 0))))
+    norm_grad = gain_sums[:2]
+    qk_grad = gain_sums[2:4, :HEAD_SIZE] + gain_sums[2:4, HEAD_SIZE:LANES]
 
     norm_new = adam_update(norm_gains, norm_first, norm_second, norm_grad, GAIN_RATE, 0.0)
     qk_new = adam_update(qk_gains, qk_first, qk_second, qk_grad, GAIN_RATE, 0.0)

time: 1270 us -> 830 us (0.65)
  waiting for transfers between devices: 875 us -> 191 us
  Pallas kernels: 229 us -> 416 us
  starting transfers between devices: 6.35 us -> 64.3 us
  blocking collectives: 37.7 us -> 0 us
  other arithmetic: 45.6 us -> 62.7 us
    reduce_scatter x5 -> x0, waiting for transfers between devices: 493 us -> none  [scatter(): lax.psum_scatter(terms, ALL, scatter_dimension=0, tiled=True).astype(F32)]
    all_gather x5 -> x1, waiting for transfers between devices: 243 us -> 0.01 us  [gather(): return lax.all_gather(shard, ALL, axis=0, tiled=True)]
    pallas_call x0 -> x2, Pallas kernels: none -> 162 us  [gather_all(): pl.pallas_call(functools.partial(gather_kernel, plan), name='gather_all',...]
    ppermute x2 -> x43, starting transfers between devices: 5.94 us -> 64.3 us  [the longest x35 50.4 us: swap(): return lax.ppermute(value, axis, pairs)]
    ppermute x2 -> x43, waiting for transfers between devices: 137 us -> 191 us  [the longest x35 139 us: swap(): return lax.ppermute(value, axis, pairs)]
    psum x1 -> x0, blocking collectives: 37.7 us -> none  [per_device(): norm_grad, qk_grad = lax.psum((norm_terms, qk_terms), ALL)]
    convert_element_type x3 -> x17, other arithmetic: 3.97 us -> 33.1 us  [the longest x3 11.5 us: own_part(): return total if last else total.astype(BF16)]
    pallas_call x1 -> x4, Pallas kernels: 63.8 us -> 77.4 us  [attend_back(): pl.pallas_call(attend_back_kernel, name='attend_back', grid_spec=pltpu.Pr...]
  transfers between devices with their start and end apart: 12 -> 44, of which waited for: 10 -> 19; matrix products, arithmetic and copies ran while one was open for 6% -> 13% of each run, Pallas kernels for 10% -> 33%
where the time goes in v2:
time: 830 us; the launch traced here: 820 us
  Pallas kernels  416 us (50%)
  waiting for transfers between devices  191 us (23%)
  starting transfers between devices  64.3 us (8%)
  other arithmetic  62.7 us (8%)
  matrix products  44.8 us (5%)
  local copies, waits for them, and re-layouts  26 us (3%)
  between operations  15.7 us (2%)
    pallas_call x2, Pallas kernels, gather_all(): pl.pallas_call(functools.partial(gather_kernel, plan), name='gather_all',...  162 us
    ppermute x35, waiting for transfers between devices, swap(): return lax.ppermute(value, axis, pairs)  139 us
    pallas_call x1, Pallas kernels, feed(): pl.pallas_call(feed_kernel, name='feed', grid=(turns,), in_specs=[fixed((...  104 us
    pallas_call x4, Pallas kernels, attend_back(): pl.pallas_call(attend_back_kernel, name='attend_back', grid_spec=pltpu.Pr...  77.4 us
    pallas_call x4, Pallas kernels, attend(): pl.pallas_call(attend_kernel, name='attend', grid_spec=pltpu.PrefetchScal...  52.1 us
    ppermute x35, starting transfers between devices, swap(): return lax.ppermute(value, axis, pairs)  50.4 us
    ppermute x4, waiting for transfers between devices, per_device(): others = [lax.ppermute(p, 'seq', [(0, 1)]) for p in own]  35.6 us
    dot_general x6, matrix products, dot_cols(): lax.dot_general(a, b, (((1,), (1,)), ((), ())), preferred_element_type=F32)  25.4 us
  transfers between devices with their start and end apart: 44, of which 19 were waited for; matrix products, arithmetic and copies ran while one was open for 13% of the time, Pallas kernels for 33%

profile of v2, /device:TPU:0, one launch (start us, length us, event | category | flops | bytes accessed | tf_op | source)
XLA Modules:
  0.0 819.8 jit_solution(3229022131037247862)
XLA Ops:
  12.2 44.6 %gather_all.2 = (bf16[4,2,2,2,32,2048]{5,4,3,2,1,0:T(8,128)(2,1)}, bf16[4,2,2,2,32,1024]{5,4,3,2,1,0:T(8,128)(2,1)}) custom-call(bf16[32,2048]{1,0:T(8,128)(2,1)} %convert_element_type.282.refs_0_, bf16[32,1024]{1,0:T(8,128)(2,1)} %convert_element_type.283.refs_1_), custom_call_target="tpu_custom_call" | custom-call | tf_op jit(solution)/shard_map/gather_all/pallas_call | solution.py:678
  64.4 7.1 fusion.22.raw_ref
  71.5 8.2 %prep.1 = (bf16[1024,1024]{1,0:T(8,128)(2,1)}, bf16[1024,256]{1,0:T(8,128)(2,1)}, bf16[1024,256]{1,0:T(8,128)(2,1)}, bf16[1024,256]{1,0:T(8,128)(2,1)}, bf16[1024,256]{1,0:T(8,128)(2,1)}) custom-call(f32[1024,2048]{1,0:T(8,128)} %fusion.22.raw_ref, f32[8,128]{1,0:T(8,128)} %pad.12.gain_ref, f32[1024,128]{1,0:T(8,128)} %get-tuple-element.161.cos_ref, ...), custom_call_target="tpu_custom_call" | custom-call | flops 83886080 | bytes 12582912 | tf_op jit(solution)/shard_map/prep/pallas_call | solution.py:92
  90.1 23.7 %collective-permute-done.2.ko_ref.vo_ref = bf16[1024,256]{1,0:T(8,128)(2,1)} collective-permute-done((bf16[1024,256]{1,0:T(8,128)(2,1)}, bf16[1024,256]{1,0:T(8,128)(2,1)}, u32[]{:S(2)}, u32[]{:S(2)}) %collective-permute-start.2) | collective-permute-done | bytes 524320 | tf_op jit(solution)/shard_map/ppermute | solution.py:785
  114.8 13.0 %attend.6 = (bf16[1024,256]{1,0:T(8,128)(2,1)}, f32[2,32,512]{2,1,0:T(8,128)}) custom-call(s32[5]{0:T(128)} %pad_add_fusion.1.low_ref, s32[1024,128]{1,0:T(8,128)} %broadcast_in_dim.32.first_ref, bf16[1024,1024]{1,0:T(8,128)(2,1)} %get-tuple-element.66.q_ref, bf16[1024,256]{1,0:T(8,128)(2,1)} %collective-permute-done.2.ko_ref.vo_ref, ...), custom_call_target="tpu_custom_call" | custom-call | flops 8589934592 | bytes 4194304 | tf_op jit(solution)/shard_map/attend/pallas_call | solution.py:251
  127.8 7.0 collective-permute-done.1.ko_ref.vo_ref
  134.8 12.9 %attend.5 = (bf16[1024,256]{1,0:T(8,128)(2,1)}, f32[2,32,512]{2,1,0:T(8,128)}) custom-call(s32[5]{0:T(128)} %pad_add_fusion.1.low_ref, s32[1024,128]{1,0:T(8,128)} %broadcast_in_dim.32.first_ref, bf16[1024,1024]{1,0:T(8,128)(2,1)} %get-tuple-element.66.q_ref, bf16[1024,256]{1,0:T(8,128)(2,1)} %collective-permute-done.1.ko_ref.vo_ref, ...), custom_call_target="tpu_custom_call" | custom-call | flops 8589934592 | bytes 4194304 | tf_op jit(solution)/shard_map/attend/pallas_call | solution.py:251
  147.8 4.9 collective-permute-done.ko_ref.vo_ref
  152.7 12.9 %attend.4 = (bf16[1024,256]{1,0:T(8,128)(2,1)}, f32[2,32,512]{2,1,0:T(8,128)}) custom-call(s32[5]{0:T(128)} %pad_add_fusion.1.low_ref, s32[1024,128]{1,0:T(8,128)} %broadcast_in_dim.32.first_ref, bf16[1024,1024]{1,0:T(8,128)(2,1)} %get-tuple-element.66.q_ref, bf16[1024,256]{1,0:T(8,128)(2,1)} %collective-permute-done.ko_ref.vo_ref, ...), custom_call_target="tpu_custom_call" | custom-call | flops 8589934592 | bytes 4194304 | tf_op jit(solution)/shard_map/attend/pallas_call | solution.py:251
  167.7 13.2 %attend.7 = (bf16[1024,256]{1,0:T(8,128)(2,1)}, f32[2,32,512]{2,1,0:T(8,128)}) custom-call(s32[5]{0:T(128)} %pad_add_fusion.1.low_ref, s32[1024,128]{1,0:T(8,128)} %broadcast_in_dim.32.first_ref, bf16[1024,1024]{1,0:T(8,128)(2,1)} %get-tuple-element.66.q_ref, bf16[1024,256]{1,0:T(8,128)(2,1)} %copy-done.50, bf16[1024,256]{1,0:T(8,128)(2,1)} %copy-done.50, ...), custom_call_target="tpu_custom_call" | custom-call | flops 8589934592 | bytes 4194304 | tf_op jit(solution)/shard_map/attend/pallas_call | solution.py:251
  187.2 117.3 %gather_all.3 = (bf16[4,2,2,2,32,4608]{5,4,3,2,1,0:T(8,128)(2,1)}, bf16[4,2,2,2,32,4608]{5,4,3,2,1,0:T(8,128)(2,1)}) custom-call(bf16[32,4608]{1,0:T(8,128)(2,1)} %get-tuple-element.76.refs_0_, bf16[32,4608]{1,0:T(8,128)(2,1)} %get-tuple-element.77.refs_1_), custom_call_target="tpu_custom_call" | custom-call | tf_op jit(solution)/shard_map/gather_all/pallas_call | solution.py:678
  304.5 5.4 fusion.37.atu_ref
  317.4 104.3 %feed.1 = (f32[1024,1024]{1,0:T(8,128)}, f32[1024,1024]{1,0:T(8,128)}, bf16[512,4608]{1,0:T(8,128)(2,1)}, bf16[512,4608]{1,0:T(8,128)(2,1)}, bf16[512,4608]{1,0:...) custom-call(bf16[1024,1024]{1,0:T(8,128)(2,1)} %multiply_convert_fusion.a_ref, ...), custom_call_target="tpu_custom_call" | custom-call | flops 86973087744 | bytes 56623104 | tf_op jit(solution)/shard_map/feed/pallas_call | solution.py:465
  421.7 4.7 multiply_reduce_fusion
  437.4 13.7 %collective-permute-done.27 = bf16[256,1024]{1,0:T(8,128)(2,1)S(1)} collective-permute-done((bf16[256,1024]{1,0:T(8,128)(2,1)S(1)}, bf16[256,1024]{1,0:T(8,128)(2,1)S(1)}, u32[]{:S(2)}, u32[]{:S(2)}) %collective-permute-start.27) | collective-permute-done | bytes 524320 | tf_op jit(solution)/shard_map/ppermute | solution.py:552
  455.3 5.3 constant_dynamic-slice_fusion.5
  485.5 6.9 add_convert_fusion
  499.1 19.3 %attend_back.5 = (f32[1024,256]{1,0:T(8,128)}, bf16[1024,256]{1,0:T(8,128)(2,1)}, f32[1024,256]{1,0:T(8,128)}) custom-call(s32[5]{0:T(128)} %pad_add_fusion.1.low_ref, s32[8,1024]{1,0:T(8,128)} %broadcast_in_dim.59.first_ref, bf16[1024,1024]{1,0:T(8,128)(2,1)} %get-tuple-element.66.q_ref, bf16[1024,1024]{1,0:T(8,128)(2,1)} %convolution_convert_fusion.2.do_ref, ...), custom_call_target="tpu_custom_call" | custom-call | flops 12884901888 | bytes 10485760 | tf_op jit(solution)/shard_map/attend_back/pallas_call | solution.py:379
  519.7 19.3 %attend_back.4 = (f32[1024,256]{1,0:T(8,128)}, bf16[1024,256]{1,0:T(8,128)(2,1)}, f32[1024,256]{1,0:T(8,128)}) custom-call(s32[5]{0:T(128)} %pad_add_fusion.1.low_ref, s32[8,1024]{1,0:T(8,128)} %broadcast_in_dim.59.first_ref, bf16[1024,1024]{1,0:T(8,128)(2,1)} %get-tuple-element.66.q_ref, bf16[1024,1024]{1,0:T(8,128)(2,1)} %convolution_convert_fusion.2.do_ref, ...), custom_call_target="tpu_custom_call" | custom-call | flops 12884901888 | bytes 10485760 | tf_op jit(solution)/shard_map/attend_back/pallas_call | solution.py:379
  540.3 60.1 %collective-permute-done.8 = bf16[256,4608]{1,0:T(8,128)(2,1)} collective-permute-done((bf16[256,4608]{1,0:T(8,128)(2,1)S(1)}, bf16[256,4608]{1,0:T(8,128)(2,1)}, u32[]{:S(2)}, u32[]{:S(2)}) %collective-permute-start.8) | collective-permute-done | bytes 2359328 | tf_op jit(solution)/shard_map/ppermute | solution.py:552
  614.0 19.5 %attend_back.6 = (f32[1024,256]{1,0:T(8,128)}, bf16[1024,256]{1,0:T(8,128)(2,1)}, f32[1024,256]{1,0:T(8,128)}) custom-call(s32[5]{0:T(128)} %pad_add_fusion.1.low_ref, s32[8,1024]{1,0:T(8,128)} %broadcast_in_dim.59.first_ref, bf16[1024,1024]{1,0:T(8,128)(2,1)} %get-tuple-element.66.q_ref, bf16[1024,1024]{1,0:T(8,128)(2,1)} %convolution_convert_fusion.2.do_ref, ...), custom_call_target="tpu_custom_call" | custom-call | flops 12884901888 | bytes 10485760 | tf_op jit(solution)/shard_map/attend_back/pallas_call | solution.py:379
  633.5 29.6 %collective-permute-done.10 = bf16[128,4608]{1,0:T(8,128)(2,1)} collective-permute-done((bf16[128,4608]{1,0:T(8,128)(2,1)S(1)}, bf16[128,4608]{1,0:T(8,128)(2,1)}, u32[]{:S(2)}, u32[]{:S(2)}) %collective-permute-start.10) | collective-permute-done | bytes 1179680 | tf_op jit(solution)/shard_map/ppermute | solution.py:552
  669.2 19.3 %attend_back.7 = (f32[1024,256]{1,0:T(8,128)}, bf16[1024,256]{1,0:T(8,128)(2,1)}, f32[1024,256]{1,0:T(8,128)}) custom-call(s32[5]{0:T(128)} %pad_add_fusion.1.low_ref, s32[8,1024]{1,0:T(8,128)} %broadcast_in_dim.59.first_ref, bf16[1024,1024]{1,0:T(8,128)(2,1)} %get-tuple-element.66.q_ref, bf16[1024,1024]{1,0:T(8,128)(2,1)} %convolution_convert_fusion.2.do_ref, ...), custom_call_target="tpu_custom_call" | custom-call | flops 12884901888 | bytes 10485760 | tf_op jit(solution)/shard_map/attend_back/pallas_call | solution.py:379
  688.7 4.8 collective-permute-start.34
  707.6 5.1 collective-permute-done.14.rest_10_
  713.1 10.8 %collective-permute-done.15.rest_11_ = bf16[1024,256]{1,0:T(8,128)(2,1)S(1)} collective-permute-done((bf16[1024,256]{1,0:T(8,128)(2,1)S(1)}, bf16[1024,256]{1,0:T(8,128)(2,1)S(1)}, u32[]{:S(2)}, u32[]{:S(2)}) %collective-permute-start.15) | collective-permute-done | bytes 524320 | tf_op jit(solution)/shard_map/ppermute | solution.py:842
  725.2 11.9 %prep_back.1 = (bf16[1024,2048]{1,0:T(8,128)(2,1)}, f32[8,128]{1,0:T(8,128)}) custom-call(f32[1024,2048]{1,0:T(8,128)} %fusion.22.raw_ref, f32[8,128]{1,0:T(8,128)} %pad.12.gain_ref, f32[1024,128]{1,0:T(8,128)} %get-tuple-element.161.cos_ref, f32[1024,128]{1,0:T(8,128)} %get-tuple-element.162.sin_ref, f32[1024,256]{1,0:T(8,128)} %get-tuple-element.89.rest_0_, ...), custom_call_target="tpu_custom_call" | custom-call | flops 125829120 | bytes 20971520 | tf_op jit(solution)/shard_map/prep_back/pallas_call | solution.py:145
  737.2 5.0 convolution_convert_fusion
  745.6 4.9 fusion.12
  756.0 16.3 %collective-permute-start.22 = (bf16[256,2048]{1,0:T(8,128)(2,1)S(1)}, bf16[256,2048]{1,0:T(8,128)(2,1)S(1)}, u32[]{:S(2)}, u32[]{:S(2)}) collective-permute-start(bf16[256,2048]{1,0:T(8,128)(2,1)S(1)} %slice.202), channel_id=1, source_target_pairs={{0,1},{1,0},{2,3},{3,2},{4,5},{5,4},{6,7},{7,6},{8,9},{9,8},{10,11... | collective-permute-start | bytes 3145736 | tf_op jit(solution)/shard_map/ppermute | solution.py:552
  781.0 10.1 %collective-permute-done.22 = bf16[256,2048]{1,0:T(8,128)(2,1)S(1)} collective-permute-done((bf16[256,2048]{1,0:T(8,128)(2,1)S(1)}, bf16[256,2048]{1,0:T(8,128)(2,1)S(1)}, u32[]{:S(2)}, u32[]{:S(2)}) %collective-permute-start.22) | collective-permute-done | bytes 1048608 | tf_op jit(solution)/shard_map/ppermute | solution.py:552
  795.2 5.7 collective-permute-done.23
  (290 shorter events, 157.2 us)
Async XLA Ops:
  7.2 310.2 %all-gather.2.cloned.1.call-start = ((), (), s32[]{:S(2)}) async-start(), calls=%async_computation | async-start | bytes 9732096 | tf_op jit(solution)/shard_map/all_gather | solution.py:531
  79.7 87.2 %collective-permute-start.3 = (bf16[1024,256]{1,0:T(8,128)(2,1)}, bf16[1024,256]{1,0:T(8,128)(2,1)S(1)}, u32[]{:S(2)}, u32[]{:S(2)}) collective-permute-start(bf16[1024,256]{1,0:T(8,128)(2,1)} %get-tuple-element.73.k_ref.v_ref), channel_id=1, source_target_pairs={{0,1},{2,3},{4,5},{6,7},{8,9},{10,11},{12,13},{14,15},{16,17},{18,... | collective-permute-start | bytes 1572872 | tf_op jit(solution)/shard_map/ppermute | solution.py:785
  81.7 32.2 %collective-permute-start.2 = (bf16[1024,256]{1,0:T(8,128)(2,1)}, bf16[1024,256]{1,0:T(8,128)(2,1)}, u32[]{:S(2)}, u32[]{:S(2)}) collective-permute-start(bf16[1024,256]{1,0:T(8,128)(2,1)} %get-tuple-element.71.k_ref.v_ref), channel_id=1, source_target_pairs={{0,1},{2,3},{4,5},{6,7},{8,9},{10,11},{12,13},{14,15},{16,17},{18,... | collective-permute-start | bytes 1572872 | tf_op jit(solution)/shard_map/ppermute | solution.py:785
  83.8 51.1 %collective-permute-start.1 = (bf16[1024,256]{1,0:T(8,128)(2,1)}, bf16[1024,256]{1,0:T(8,128)(2,1)}, u32[]{:S(2)}, u32[]{:S(2)}) collective-permute-start(bf16[1024,256]{1,0:T(8,128)(2,1)} %get-tuple-element.69.k_ref.v_ref), channel_id=1, source_target_pairs={{0,1},{2,3},{4,5},{6,7},{8,9},{10,11},{12,13},{14,15},{16,17},{18,... | collective-permute-start | bytes 1572872 | tf_op jit(solution)/shard_map/ppermute | solution.py:785
  85.9 66.8 %collective-permute-start = (bf16[1024,256]{1,0:T(8,128)(2,1)}, bf16[1024,256]{1,0:T(8,128)(2,1)}, u32[]{:S(2)}, u32[]{:S(2)}) collective-permute-start(bf16[1024,256]{1,0:T(8,128)(2,1)} %get-tuple-element.67.k_ref.v_ref), channel_id=1, source_target_pairs={{0,1},{2,3},{4,5},{6,7},{8,9},{10,11},{12,13},{14,15},{16,17},{18,... | collective-permute-start | bytes 1572872 | tf_op jit(solution)/shard_map/ppermute | solution.py:785
  432.6 43.8 %collective-permute-start.4 = (bf16[512,4608]{1,0:T(8,128)(2,1)}, bf16[512,4608]{1,0:T(8,128)(2,1)}, u32[]{:S(2)}, u32[]{:S(2)}) collective-permute-start(bf16[512,4608]{1,0:T(8,128)(2,1)} %get-tuple-element.84), channel_id=1, source_target_pairs={{0,2},{2,0},{4,6},{6,4},{8,10},{10,8},{12,14},{14,12},{16,18},{18,... | collective-permute-start | bytes 14155784 | tf_op jit(solution)/shard_map/ppermute | solution.py:552
  436.9 14.3 %collective-permute-start.27 = (bf16[256,1024]{1,0:T(8,128)(2,1)S(1)}, bf16[256,1024]{1,0:T(8,128)(2,1)S(1)}, u32[]{:S(2)}, u32[]{:S(2)}) collective-permute-start(bf16[256,1024]{1,0:T(8,128)(2,1)S(1)} %slice.210), channel_id=1, source_target_pairs={{0,4},{2,6},{4,0},{6,2},{8,12},{10,14},{12,8},{14,10},{16,20},{18,... | collective-permute-start | bytes 1572872 | tf_op jit(solution)/shard_map/ppermute | solution.py:552
  437.0 43.2 %collective-permute-start.5 = (bf16[512,4608]{1,0:T(8,128)(2,1)}, bf16[512,4608]{1,0:T(8,128)(2,1)}, u32[]{:S(2)}, u32[]{:S(2)}) collective-permute-start(bf16[512,4608]{1,0:T(8,128)(2,1)} %get-tuple-element.86), channel_id=1, source_target_pairs={{0,2},{2,0},{4,6},{6,4},{8,10},{10,8},{12,14},{14,12},{16,18},{18,... | collective-permute-start | bytes 14155784 | tf_op jit(solution)/shard_map/ppermute | solution.py:552
  460.6 24.8 %collective-permute-start.7 = (bf16[4,2,1,2,144,1024]{5,4,3,2,1,0:T(8,128)(2,1)}, bf16[4,2,1,2,144,1024]{5,4,3,2,1,0:T(8,128)(2,1)}, u32[]{:S(2)}, u32[]{:S(2)}) collective-permute-start(bf16[4,2,1,2,144,1024]{5,4,3,2,1,0:T(8,128)(2,1)} %constant_dynamic-slice_fusion.5), channel_id=1, source_target_pairs={{0,2},{2,0},{4,6},{6,4},{8,10},{10,8},{12,14},{14,12},{16,18},{18,... | collective-permute-start | bytes 14155784 | tf_op jit(solution)/shard_map/ppermute | solution.py:552
  495.4 111.6 %collective-permute-start.38 = (bf16[4,2,1,1,144,1024]{5,4,3,2,1,0:T(8,128)(2,1)}, bf16[4,2,1,1,144,1024]{5,4,3,2,1,0:T(8,128)(2,1)}, u32[]{:S(2)}, u32[]{:S(2)}) collective-permute-start(bf16[4,2,1,1,144,1024]{5,4,3,2,1,0:T(8,128)(2,1)} %constant_dynamic-slice_fusion.4), channel_id=1, source_target_pairs={{0,1},{1,0},{2,3},{3,2},{4,5},{5,4},{6,7},{7,6},{8,9},{9,8},{10,11... | collective-permute-start | bytes 7077896 | tf_op jit(solution)/shard_map/ppermute | solution.py:552
  497.3 103.0 %collective-permute-start.8 = (bf16[256,4608]{1,0:T(8,128)(2,1)S(1)}, bf16[256,4608]{1,0:T(8,128)(2,1)}, u32[]{:S(2)}, u32[]{:S(2)}) collective-permute-start(bf16[256,4608]{1,0:T(8,128)(2,1)S(1)} %slice.189), channel_id=1, source_target_pairs={{0,1},{1,0},{2,3},{3,2},{4,5},{5,4},{6,7},{7,6},{8,9},{9,8},{10,11... | collective-permute-start | bytes 7077896 | tf_op jit(solution)/shard_map/ppermute | solution.py:552
  497.4 105.4 %collective-permute-start.9 = (bf16[256,4608]{1,0:T(8,128)(2,1)}, bf16[256,4608]{1,0:T(8,128)(2,1)}, u32[]{:S(2)}, u32[]{:S(2)}) collective-permute-start(bf16[256,4608]{1,0:T(8,128)(2,1)} %slice.191), channel_id=1, source_target_pairs={{0,4},{2,6},{4,0},{6,2},{8,12},{10,14},{12,8},{14,10},{16,20},{18,... | collective-permute-start | bytes 7077896 | tf_op jit(solution)/shard_map/ppermute | solution.py:552
  518.4 185.8 %collective-permute-start.13 = (bf16[1024,256]{1,0:T(8,128)(2,1)}, bf16[1024,256]{1,0:T(8,128)(2,1)}, u32[]{:S(2)}, u32[]{:S(2)}) collective-permute-start(bf16[1024,256]{1,0:T(8,128)(2,1)} %get-tuple-element.105), channel_id=1, source_target_pairs={{1,0},{3,2},{5,4},{7,6},{9,8},{11,10},{13,12},{15,14},{17,16},{19,... | collective-permute-start | bytes 1572872 | tf_op jit(solution)/shard_map/ppermute | solution.py:842
  539.0 168.1 %collective-permute-start.12 = (bf16[1024,256]{1,0:T(8,128)(2,1)}, bf16[1024,256]{1,0:T(8,128)(2,1)}, u32[]{:S(2)}, u32[]{:S(2)}) collective-permute-start(bf16[1024,256]{1,0:T(8,128)(2,1)} %get-tuple-element.104), channel_id=1, source_target_pairs={{1,0},{3,2},{5,4},{7,6},{9,8},{11,10},{13,12},{15,14},{17,16},{19,... | collective-permute-start | bytes 1572872 | tf_op jit(solution)/shard_map/ppermute | solution.py:842
  610.9 77.7 %collective-permute-start.39 = (bf16[4,1,1,1,144,1024]{5,4,3,2,1,0:T(8,128)(2,1)}, bf16[4,1,1,1,144,1024]{5,4,3,2,1,0:T(8,128)(2,1)}, u32[]{:S(2)}, u32[]{:S(2)}) collective-permute-start(bf16[4,1,1,1,144,1024]{5,4,3,2,1,0:T(8,128)(2,1)} %constant_dynamic-slice_fusion.3), channel_id=1, source_target_pairs={{0,4},{2,6},{4,0},{6,2},{8,12},{10,14},{12,8},{14,10},{16,20},{18,... | collective-permute-start | bytes 3538952 | tf_op jit(solution)/shard_map/ppermute | solution.py:552
  612.0 51.1 %collective-permute-start.10 = (bf16[128,4608]{1,0:T(8,128)(2,1)S(1)}, bf16[128,4608]{1,0:T(8,128)(2,1)}, u32[]{:S(2)}, u32[]{:S(2)}) collective-permute-start(bf16[128,4608]{1,0:T(8,128)(2,1)S(1)} %slice.193), channel_id=1, source_target_pairs={{0,4},{2,6},{4,0},{6,2},{8,12},{10,14},{12,8},{14,10},{16,20},{18,... | collective-permute-start | bytes 3538952 | tf_op jit(solution)/shard_map/ppermute | solution.py:552
  613.0 54.7 %collective-permute-start.11 = (bf16[128,4608]{1,0:T(8,128)(2,1)}, bf16[128,4608]{1,0:T(8,128)(2,1)}, u32[]{:S(2)}, u32[]{:S(2)}) collective-permute-start(bf16[128,4608]{1,0:T(8,128)(2,1)} %slice.195), channel_id=1, source_target_pairs={{0,1},{1,0},{2,3},{3,2},{4,5},{5,4},{6,7},{7,6},{8,9},{9,8},{10,11... | collective-permute-start | bytes 3538952 | tf_op jit(solution)/shard_map/ppermute | solution.py:552
  665.7 30.6 %collective-permute-start.32 = (bf16[32,4608]{1,0:T(8,128)(2,1)}, bf16[32,4608]{1,0:T(8,128)(2,1)}, u32[]{:S(2)}, u32[]{:S(2)}) collective-permute-start(bf16[32,4608]{1,0:T(8,128)(2,1)} %get-tuple-element.135), channel_id=1, source_target_pairs={{0,8},{2,10},{4,12},{6,14},{8,0},{10,2},{12,4},{14,6},{16,24},{18,... | collective-permute-start | bytes 884744 | tf_op jit(solution)/shard_map/ppermute | solution.py:552
  667.7 29.8 %collective-permute-start.33 = (bf16[32,4608]{1,0:T(8,128)(2,1)}, bf16[32,4608]{1,0:T(8,128)(2,1)}, u32[]{:S(2)}, u32[]{:S(2)}) collective-permute-start(bf16[32,4608]{1,0:T(8,128)(2,1)} %get-tuple-element.137), channel_id=1, source_target_pairs={{0,16},{2,18},{4,20},{6,22},{8,24},{10,26},{12,28},{14,30},{16,0},... | collective-permute-start | bytes 884744 | tf_op jit(solution)/shard_map/ppermute | solution.py:552
  688.7 13.0 %collective-permute-start.34 = (bf16[32,4608]{1,0:T(8,128)(2,1)}, bf16[32,4608]{1,0:T(8,128)(2,1)S(1)}, u32[]{:S(2)}, u32[]{:S(2)}) collective-permute-start(bf16[32,4608]{1,0:T(8,128)(2,1)} %get-tuple-element.136), channel_id=1, source_target_pairs={{0,24},{2,26},{4,28},{6,30},{8,16},{10,18},{12,20},{14,22},{16,8},... | collective-permute-start | bytes 884744 | tf_op jit(solution)/shard_map/ppermute | solution.py:552
  696.2 16.4 %collective-permute-start.14 = (bf16[1024,256]{1,0:T(8,128)(2,1)S(1)}, bf16[1024,256]{1,0:T(8,128)(2,1)S(1)}, u32[]{:S(2)}, u32[]{:S(2)}) collective-permute-start(bf16[1024,256]{1,0:T(8,128)(2,1)S(1)} %copy-done.51), channel_id=1, source_target_pairs={{1,0},{3,2},{5,4},{7,6},{9,8},{11,10},{13,12},{15,14},{17,16},{19,... | collective-permute-start | bytes 1572872 | tf_op jit(solution)/shard_map/ppermute | solution.py:842
  697.5 77.2 %collective-permute-start.40 = (bf16[1,1,1,1,144,1024]{5,4,3,2,1,0:T(8,128)(2,1)}, bf16[1,1,1,1,144,1024]{5,4,3,2,1,0:T(8,128)(2,1)}, u32[]{:S(2)}, u32[]{:S(2)}) collective-permute-start(bf16[1,1,1,1,144,1024]{5,4,3,2,1,0:T(8,128)(2,1)} %get-tuple-element.132), channel_id=1, source_target_pairs={{0,8},{2,10},{4,12},{6,14},{8,0},{10,2},{12,4},{14,6},{16,24},{18,... | collective-permute-start | bytes 884744 | tf_op jit(solution)/shard_map/ppermute | solution.py:552
  701.6 22.2 %collective-permute-start.15 = (bf16[1024,256]{1,0:T(8,128)(2,1)S(1)}, bf16[1024,256]{1,0:T(8,128)(2,1)S(1)}, u32[]{:S(2)}, u32[]{:S(2)}) collective-permute-start(bf16[1024,256]{1,0:T(8,128)(2,1)S(1)} %copy-done.52), channel_id=1, source_target_pairs={{1,0},{3,2},{5,4},{7,6},{9,8},{11,10},{13,12},{15,14},{17,16},{19,... | collective-permute-start | bytes 1572872 | tf_op jit(solution)/shard_map/ppermute | solution.py:842
  704.1 70.6 %collective-permute-start.41 = (bf16[1,1,1,1,144,1024]{5,4,3,2,1,0:T(8,128)(2,1)}, bf16[1,1,1,1,144,1024]{5,4,3,2,1,0:T(8,128)(2,1)S(1)}, u32[]{:S(2)}, u32[]{:S(2)}) collective-permute-start(bf16[1,1,1,1,144,1024]{5,4,3,2,1,0:T(8,128)(2,1)} %get-tuple-element.134), channel_id=1, source_target_pairs={{0,16},{2,18},{4,20},{6,22},{8,24},{10,26},{12,28},{14,30},{16,0},... | collective-permute-start | bytes 884744 | tf_op jit(solution)/shard_map/ppermute | solution.py:552
  707.0 35.2 %collective-permute-start.35 = (bf16[32,4608]{1,0:T(8,128)(2,1)S(1)}, bf16[32,4608]{1,0:T(8,128)(2,1)S(1)}, u32[]{:S(2)}, u32[]{:S(2)}) collective-permute-start(bf16[32,4608]{1,0:T(8,128)(2,1)S(1)} %get-tuple-element.138), channel_id=1, source_target_pairs={{0,8},{2,10},{4,12},{6,14},{8,0},{10,2},{12,4},{14,6},{16,24},{18,... | collective-permute-start | bytes 884744 | tf_op jit(solution)/shard_map/ppermute | solution.py:552
  712.7 32.1 %collective-permute-start.36 = (bf16[32,4608]{1,0:T(8,128)(2,1)S(1)}, bf16[32,4608]{1,0:T(8,128)(2,1)S(1)}, u32[]{:S(2)}, u32[]{:S(2)}) collective-permute-start(bf16[32,4608]{1,0:T(8,128)(2,1)S(1)} %get-tuple-element.140), channel_id=1, source_target_pairs={{0,16},{2,18},{4,20},{6,22},{8,24},{10,26},{12,28},{14,30},{16,0},... | collective-permute-start | bytes 884744 | tf_op jit(solution)/shard_map/ppermute | solution.py:552
  723.9 20.9 %collective-permute-start.37 = (bf16[32,4608]{1,0:T(8,128)(2,1)S(1)}, bf16[32,4608]{1,0:T(8,128)(2,1)S(1)}, u32[]{:S(2)}, u32[]{:S(2)}) collective-permute-start(bf16[32,4608]{1,0:T(8,128)(2,1)S(1)} %get-tuple-element.139), channel_id=1, source_target_pairs={{0,24},{2,26},{4,28},{6,30},{8,16},{10,18},{12,20},{14,22},{16,8},... | collective-permute-start | bytes 884744 | tf_op jit(solution)/shard_map/ppermute | solution.py:552
  742.2 32.5 %collective-permute-start.42 = (bf16[1,1,1,1,144,1024]{5,4,3,2,1,0:T(8,128)(2,1)}, bf16[1,1,1,1,144,1024]{5,4,3,2,1,0:T(8,128)(2,1)S(1)}, u32[]{:S(2)}, u32[]{:S(2)}) collective-permute-start(bf16[1,1,1,1,144,1024]{5,4,3,2,1,0:T(8,128)(2,1)} %get-tuple-element.133), channel_id=1, source_target_pairs={{0,24},{2,26},{4,28},{6,30},{8,16},{10,18},{12,20},{14,22},{16,8},... | collective-permute-start | bytes 884744 | tf_op jit(solution)/shard_map/ppermute | solution.py:552
  744.8 10.2 %collective-permute-start.21 = (bf16[512,2048]{1,0:T(8,128)(2,1)S(1)}, bf16[512,2048]{1,0:T(8,128)(2,1)S(1)}, u32[]{:S(2)}, u32[]{:S(2)}) collective-permute-start(bf16[512,2048]{1,0:T(8,128)(2,1)S(1)} %convolution_convert_fusion), channel_id=1, source_target_pairs={{0,2},{2,0},{4,6},{6,4},{8,10},{10,8},{12,14},{14,12},{16,18},{18,... | collective-permute-start | bytes 6291464 | tf_op jit(solution)/shard_map/ppermute | solution.py:552
  754.6 20.0 %collective-permute-start.17 = (f32[8,1024]{1,0:T(8,128)S(1)}, f32[8,1024]{1,0:T(8,128)S(1)}, u32[]{:S(2)}, u32[]{:S(2)}) collective-permute-start(f32[8,1024]{1,0:T(8,128)S(1)} %pad_add_fusion), channel_id=1, source_target_pairs={{0,16},{2,18},{4,20},{6,22},{8,24},{10,26},{12,28},{14,30},{16,0},... | collective-permute-start | bytes 98312 | tf_op jit(solution)/shard_map/ppermute | solution.py:552
  756.0 35.2 %collective-permute-start.22 = (bf16[256,2048]{1,0:T(8,128)(2,1)S(1)}, bf16[256,2048]{1,0:T(8,128)(2,1)S(1)}, u32[]{:S(2)}, u32[]{:S(2)}) collective-permute-start(bf16[256,2048]{1,0:T(8,128)(2,1)S(1)} %slice.202), channel_id=1, source_target_pairs={{0,1},{1,0},{2,3},{3,2},{4,5},{5,4},{6,7},{7,6},{8,9},{9,8},{10,11... | collective-permute-start | bytes 3145736 | tf_op jit(solution)/shard_map/ppermute | solution.py:552
  779.8 14.7 %collective-permute-start.20 = (f32[8,1024]{1,0:T(8,128)S(1)}, f32[8,1024]{1,0:T(8,128)S(1)}, u32[]{:S(2)}, u32[]{:S(2)}) collective-permute-start(f32[8,1024]{1,0:T(8,128)S(1)} %add.467), channel_id=1, source_target_pairs={{0,1},{1,0},{2,3},{3,2},{4,5},{5,4},{6,7},{7,6},{8,9},{9,8},{10,11... | collective-permute-start | bytes 98312 | tf_op jit(solution)/shard_map/ppermute | solution.py:552
  (73 other events, 700.1 us)
Sparse Core Ops, SparseCore 0:
  57.0 91.9 all-gather.1

commit v3 on v2

--- a/solution.py
+++ b/solution.py
@@ -413,83 +413,6 @@
     )(low, first_lane, q, d_mixed, mixed, lse, others, others, own, own)
 
 
-def feed_kernel(
-    a_ref,
-    atg_ref,
-    atu_ref,
-    g_ref,
-    wg_ref,
-    wu_ref,
-    wd_ref,
-    y_in,
-    y_ref,
-    b_ref,
-    gg_ref,
-    ggs_ref,
-    gu_ref,
-    gus_ref,
-    gd_ref,
-):
-    @pl.when(pl.program_id(0) == 0)
-    def _():
-        y_ref[...] = y_in[...]
-        b_ref[...] = jnp.zeros_like(b_ref)
-
-    a, g = a_ref[...], g_ref[...]
-    wg, wu, wd = wg_ref[...], wu_ref[...], wd_ref[...]
-    gate = dot(a, wg)
-    up = dot(a, wu)
-    d_hidden = dot_cols(g, wd)
-    sigma = 1.0 / (1.0 + jnp.exp(-gate))
-    swish = gate * sigma
-    hidden = (swish * up).astype(BF16)
-    d_gate = (d_hidden * up * sigma * (1.0 + gate * (1.0 - sigma))).astype(BF16)
-    d_up = (d_hidden * swish).astype(BF16)
-    y_ref[...] += dot(hidden, wd)
-    b_ref[...] += dot_cols(d_gate, wg) + dot_cols(d_up, wu)
-    half = atg_ref.shape[0] // 2
-    gg_ref[...] = dot(atg_ref[:half], d_gate).astype(BF16)
-    ggs_ref[...] = dot(atg_ref[half:], d_gate).astype(BF16)
-    gu_ref[...] = dot(atu_ref[:half], d_up).astype(BF16)
-    gus_ref[...] = dot(atu_ref[half:], d_up).astype(BF16)
-    gd_ref[...] = dot_rows(hidden, g).astype(BF16)
-
-
-def feed(a, at_gate, at_up, g, w_gate, w_up, w_down, y):
-    rows, width = a.shape[0], w_gate.shape[1]
-    turns = width // FF_BLOCK
-    fixed = lambda s: pl.BlockSpec(s, lambda j: (0, 0))
-    col = pl.BlockSpec((D, FF_BLOCK), lambda j: (0, j))
-    half_col = pl.BlockSpec((D // 2, FF_BLOCK), lambda j: (0, j))
-    row = pl.BlockSpec((FF_BLOCK, D), lambda j: (j, 0))
-    return pl.pallas_call(
-        feed_kernel,
-        name="feed",
-        grid=(turns,),
-        in_specs=[
-            fixed((rows, D)),
-            fixed((D, rows)),
-            fixed((D, rows)),
-            fixed((rows, D)),
-            col,
-            col,
-            row,
-            fixed((rows, D)),
-        ],
-        out_specs=[fixed((rows, D)), fixed((rows, D))] + [half_col] * 4 + [row],
-        out_shape=[
-            jax.ShapeDtypeStruct((rows, D), F32),
-            jax.ShapeDtypeStruct((rows, D), F32),
-        ]
-        + [jax.ShapeDtypeStruct((D // 2, width), BF16)] * 4
-        + [jax.ShapeDtypeStruct((width, D), BF16)],
-        compiler_params=params(60),
-        cost_estimate=pl.CostEstimate(
-            flops=18 * rows * D * width, transcendentals=rows * width, bytes_accessed=12 * D * width
-        ),
-    )(a, at_gate, at_up, g, w_gate, w_up, w_down, y)
-
-
 def rms_scale(v):
     return lax.rsqrt(jnp.mean(v * v, axis=-1, keepdims=True) + NORM_EPS)
 
@@ -707,6 +630,298 @@
     return terms
 
 
+FEED_LEAD = 4
+
+
+def feed_kernel(
+    shard_ref,
+    a_ref,
+    at_ref,
+    g_ref,
+    start_ref,
+    wd_ref,
+    full_ref,
+    y_ref,
+    b_ref,
+    gd_ref,
+    sum_ref,
+    weights,
+    terms,
+    total_1,
+    total_2,
+    total_3,
+    got_c,
+    got_1,
+    got_2,
+    got_z,
+    load_sem,
+    start_sem,
+    own_sem,
+    out_send,
+    out_recv,
+    in_send,
+    in_recv,
+):
+    step = pl.program_id(0)
+    width = weights.shape[-1]
+    parts = shard_ref.shape[2] // width
+    size = {k: v[2] for k, v in dims().items()}
+    here = {k: place_along(k) for k in NAMES}
+    shard_rows = shard_ref.shape[1]
+    orders = ("xy", "yx")
+
+    def columns(p):
+        return pl.ds(pl.multiple_of(p * width, width), width)
+
+    def view(which, at, p):
+        index = tuple(at[k] if k in at else slice(None) for k in NAMES)
+        return full_ref.at[(which,) + index + (slice(None), columns(p))]
+
+    def remote(source, target, sems, p, n, k, d):
+        send, recv = sems
+        return pltpu.make_async_remote_copy(
+            source,
+            target,
+            send.at[p, n],
+            recv.at[p, n],
+            device_id=neighbour(k, d),
+            device_id_type=MESH,
+        )
+
+    def gather_copies(p, stage):
+        sems = (out_send, out_recv)
+        copies = []
+        if stage == 0:
+            for d in range(1, size["z"]):
+                copies.append(
+                    remote(shard_ref.at[:, :, columns(p)], view(slice(None), here, p), sems, p, d - 1, "z", d)
+                )
+            return copies
+        slot = size["z"] - 1
+        if stage == 3:
+            slot += 2 * (size["x"] + size["y"] - 2)
+            at = view(slice(None), {"c": here["c"]}, p)
+            return [remote(at, at, sems, p, slot, "c", 1)]
+        for which, order in enumerate(orders):
+            for s in (1, 2):
+                k = order[s - 1]
+                gone = "z" + order[: s - 1]
+                at = view(which, {q: v for q, v in here.items() if q not in gone}, p)
+                for d in range(1, size[k]):
+                    if s == stage:
+                        copies.append(remote(at, at, sems, p, slot, k, d))
+                    slot += 1
+        return copies
+
+    def scatter_copies(p, stage):
+        sems = (in_send, in_recv)
+        if stage == 0:
+            return [remote(terms.at[lax.rem(p, 2), :, 1], got_c.at[p], sems, p, 0, "c", 1)]
+        copies = []
+        slot = 1
+        for which, order in enumerate(orders):
+            for s in (1, 2):
+                k = order[s - 1]
+                for d in range(1, size[k]):
+                    if s == 1:
+                        source = total_1.at[0, d] if k == "x" else total_1.at[1, :, d]
+                    else:
+                        source = total_2[which].at[d]
+                    target = (got_1, got_2)[s - 1][which].at[p, d - 1]
+                    if s == stage:
+                        copies.append(remote(source, target, sems, p, slot, k, d))
+                    slot += 1
+        if stage == 3:
+            for d in range(1, size["z"]):
+                copies.append(remote(total_3.at[:, d], got_z.at[p, d - 1], sems, p, slot + d - 1, "z", d))
+        return copies
+
+    def own_copy():
+        return pltpu.make_async_copy(shard_ref, full_ref.at[(slice(None),) + tuple(here[k] for k in NAMES)], own_sem)
+
+    def load_copy(p):
+        return pltpu.make_async_copy(
+            full_ref.at[:, :, :, :, :, :, columns(p)], weights.at[lax.rem(p, 2)], load_sem.at[lax.rem(p, 2)]
+        )
+
+    def on(offset, run):
+        p = step - offset
+
+        @pl.when((p >= 0) & (p < parts))
+        def _():
+            run(p)
+
+    @pl.when(step == 0)
+    def _():
+        own_copy().start()
+        pltpu.make_async_copy(start_ref, y_ref, start_sem).start()
+        greet()
+
+        def begin(p, _):
+            for copy in gather_copies(p, 0):
+                copy.start()
+            return 0
+
+        lax.fori_loop(0, parts, begin, 0)
+        own_copy().wait()
+        pltpu.make_async_copy(start_ref, y_ref, start_sem).wait()
+        b_ref[...] = jnp.zeros_like(b_ref)
+
+    def pass_on(stage):
+        def run(p):
+            for copy in gather_copies(p, stage - 1):
+                copy.wait_recv()
+            for copy in gather_copies(p, stage):
+                copy.start()
+
+        return run
+
+    def arrived(p):
+        for copy in gather_copies(p, 3):
+            copy.wait_recv()
+        load_copy(p).start()
+
+    on(3, arrived)
+    on(2, pass_on(3))
+    on(1, pass_on(2))
+    on(0, pass_on(1))
+
+    def finish(p):
+        for copy in scatter_copies(p, 3):
+            copy.wait()
+        total = total_3[:, 0].astype(F32)
+        for d in range(1, size["z"]):
+            total = total + got_z[p, d - 1].astype(F32)
+        sum_ref[:, :, columns(p)] = total
+
+    def third(p):
+        for copy in scatter_copies(p, 2):
+            copy.wait()
+        for which, order in enumerate(orders):
+            total = total_2[which][0].astype(F32)
+            for d in range(1, size[order[1]]):
+                total = total + got_2[which][p, d - 1].astype(F32)
+            total_3[which] = total.astype(BF16)
+        for copy in scatter_copies(p, 3):
+            copy.start()
+
+    def second(p):
+        for copy in scatter_copies(p, 1):
+            copy.wait()
+        for which, order in enumerate(orders):
+            kept = total_1[0, 0] if order[0] == "x" else total_1[1, :, 0]
+            total = kept.astype(F32)
+            for d in range(1, size[order[0]]):
+                total = total + got_1[which][p, d - 1].astype(F32)
+            total_2[which][...] = total.astype(BF16)
+        for copy in scatter_copies(p, 2):
+            copy.start()
+
+    def first(p):
+        for copy in scatter_copies(p, 0):
+            copy.wait()
+        total = terms[lax.rem(p, 2), :, 0].astype(F32) + got_c[p].astype(F32)
+        total_1[...] = total.astype(BF16)
+        for copy in scatter_copies(p, 1):
+            copy.start()
+
+    on(FEED_LEAD + 4, finish)
+    on(FEED_LEAD + 3, third)
+    on(FEED_LEAD + 2, second)
+    on(FEED_LEAD + 1, first)
+
+    def compute(p):
+        load_copy(p).wait()
+        slot = lax.rem(p, 2)
+        rows = D
+        a, g, wd = a_ref[...], g_ref[...], wd_ref[...]
+        wg = weights[slot, 0].reshape(rows, width)
+        wu = weights[slot, 1].reshape(rows, width)
+        gate = dot(a, wg)
+        up = dot(a, wu)
+        d_hidden = dot_cols(g, wd)
+        sigma = 1.0 / (1.0 + jnp.exp(-gate))
+        swish = gate * sigma
+        hidden = (swish * up).astype(BF16)
+        d_gate = (d_hidden * up * sigma * (1.0 + gate * (1.0 - sigma))).astype(BF16)
+        d_up = (d_hidden * swish).astype(BF16)
+        y_ref[...] += dot(hidden, wd)
+        b_ref[...] += dot_cols(d_gate, wg) + dot_cols(d_up, wu)
+        at = at_ref[...]
+        shape = (2,) + total_1.shape[1:]
+        terms[slot, 0] = dot(at, d_gate).astype(BF16).reshape(shape)
+        terms[slot, 1] = dot(at, d_up).astype(BF16).reshape(shape)
+        gd_ref[...] = dot_rows(hidden, g).astype(BF16)
+        for copy in scatter_copies(p, 0):
+            copy.start()
+
+    on(FEED_LEAD, compute)
+
+    @pl.when(step == pl.num_programs(0) - 1)
+    def _():
+        def end(p, _):
+            for stage in range(4):
+                for copy in gather_copies(p, stage):
+                    copy.wait_send()
+            return 0
+
+        lax.fori_loop(0, parts, end, 0)
+
+
+def feed(shards, a, at, g, w_down, start, number):
+    rows = a.shape[0]
+    size = {k: v[2] for k, v in dims().items()}
+    _, shard_rows, width = shards.shape
+    parts = width // FF_BLOCK
+    x, y, z = size["x"], size["y"], size["z"]
+    last = (z, shard_rows, FF_BLOCK)
+    whole = pl.BlockSpec(memory_space=pltpu.VMEM)
+    anywhere = pl.BlockSpec(memory_space=pl.ANY)
+    row = pl.BlockSpec((FF_BLOCK, D), lambda t: (jnp.clip(t - FEED_LEAD, 0, parts - 1), 0))
+    out_count = z - 1 + 2 * (x + y - 2) + 1
+    in_count = 1 + 2 * (x + y - 2) + z - 1
+    sems = pltpu.SemaphoreType.DMA
+    _, y_sum, b_sum, grad_down, sums = pl.pallas_call(
+        feed_kernel,
+        name="feed",
+        grid=(parts + FEED_LEAD + 4,),
+        in_specs=[anywhere, whole, whole, whole, anywhere, row],
+        out_specs=[anywhere, whole, whole, row, whole],
+        out_shape=[
+            jax.ShapeDtypeStruct((2, *(size[k] for k in NAMES), shard_rows, width), BF16),
+            jax.ShapeDtypeStruct((rows, D), F32),
+            jax.ShapeDtypeStruct((rows, D), F32),
+            jax.ShapeDtypeStruct((width, D), BF16),
+            jax.ShapeDtypeStruct((2, shard_rows, width), F32),
+        ],
+        scratch_shapes=[
+            pltpu.VMEM((2, 2, *(size[k] for k in NAMES), shard_rows, FF_BLOCK), BF16),
+            pltpu.VMEM((2, 2, 2, x, y, *last), BF16),
+            pltpu.VMEM((2, x, y, *last), BF16),
+            [pltpu.VMEM((y, *last), BF16), pltpu.VMEM((x, *last), BF16)],
+            pltpu.VMEM((2, *last), BF16),
+            pltpu.VMEM((parts, 2, x, y, *last), BF16),
+            [pltpu.VMEM((parts, x - 1, y, *last), BF16), pltpu.VMEM((parts, y - 1, x, *last), BF16)],
+            [pltpu.VMEM((parts, y - 1, *last), BF16), pltpu.VMEM((parts, x - 1, *last), BF16)],
+            pltpu.VMEM((parts, z - 1, 2, shard_rows, FF_BLOCK), BF16),
+            sems((2,)),
+            sems,
+            sems,
+            sems((parts, out_count)),
+            sems((parts, out_count)),
+            sems((parts, in_count)),
+            sems((parts, in_count)),
+        ],
+        compiler_params=pltpu.CompilerParams(
+            collective_id=number, has_side_effects=True, vmem_limit_bytes=60 << 20
+        ),
+        cost_estimate=pl.CostEstimate(
+            flops=18 * rows * D * width, transcendentals=rows * width, bytes_accessed=12 * D * width
+        ),
+    )(shards, a, at, g, start, w_down)
+    return y_sum, b_sum, grad_down, sums
+
+
 def add_swapped(keep, send, direction):
     return (keep.astype(F32) + swap(send, direction, 1).astype(F32)).astype(BF16)
 
@@ -791,25 +1006,18 @@
     scale_second = rms_scale(x_mid)
     normed_second = (x_mid * scale_second * norm_gains[1]).astype(BF16)
     g = cotangent[0]
-    w_gate, w_up = gather_all(
-        after([gate_up_master[:, :FF].astype(BF16), gate_up_master[:, FF:].astype(BF16)], normed_second),
-        1152,
-        2,
-    )
     hot_x, hot_y = relative_rows("cxyz", D), relative_rows("cyxz", D)
-    out_sum, d_b, gate_keep, gate_send, up_keep, up_send, grad_down = feed(
+    shards = jnp.stack([gate_up_master[:, :FF], gate_up_master[:, FF:]]).astype(BF16)
+    out_sum, d_b, grad_down, gate_up_sums = feed(
+        after(shards, normed_second),
         normed_second,
         transpose_in_order(hot_x, normed_second),
-        transpose_in_order(hot_y, normed_second),
         g,
-        w_gate,
-        w_up,
         w_down,
         x_mid,
+        2,
     )
     outputs = out_sum.astype(BF16)
-    gate_1 = add_swapped(gate_keep, gate_send, "c")
-    up_1 = add_swapped(up_keep, up_send, "c")
     sizes = [dims()[k][2] for k in NAMES]
     down_1 = own_part(grad_down.reshape(*sizes, FF // math.prod(sizes), D), "c")
     d_norm, d_gain_second = rms_back(x_mid, scale_second, norm_gains[1], d_b)
@@ -826,17 +1034,14 @@
         d = after(d_mixed, earlier)
         return attend_back(p, q, d, mixes[p], lses[p], others[p], own[p], low, first_lane)
 
-    parts = [back_piece(0, (gate_1, up_1))]
-    parts.append(back_piece(1, (out_1, down_1)))
-    gate_2, up_2 = add_along(gate_1, "x"), add_along(up_1, "y")
-    parts.append(back_piece(2, (gate_2, up_2)))
-    gate_3, up_3 = add_along(gate_2, "y"), add_along(up_2, "x")
+    parts = [back_piece(0, (out_1, down_1))]
     down_2, out_2 = own_part(down_1, "x"), add_along(out_1, "y")
-    parts.append(back_piece(3, (gate_3, up_3)))
-    gate_grad, up_grad = add_along(gate_3, "z", True), add_along(up_3, "z", True)
-    down_3, out_3 = own_part(down_2, "y"), add_along(out_2, "x")
-    down_grad, out_grad = own_part(down_3, "z", True), add_along(out_3, "z", True)
-    down_grad = down_grad.reshape(-1, D)
+    parts.append(back_piece(1, out_2))
+    out_3 = add_along(out_2, "x")
+    parts.append(back_piece(2, (down_2, out_3)))
+    down_3, out_grad = own_part(down_2, "y"), add_along(out_3, "z", True)
+    parts.append(back_piece(3, (down_3, out_grad)))
+    down_grad = own_part(down_3, "z", True).reshape(-1, D)
     dq, far, near = zip(*parts)
     if seq_width == 2:
         back = [lax.ppermute(p, "seq", [(1, 0)]) for p in far]
@@ -863,7 +1068,7 @@
     out_new = adam_update(
         out_master, out_first, out_second, out_grad, (QUERY_FEATURES // 16) ** -0.5, DECAY_RATE
     )
-    gate_up_grad = jnp.concatenate([gate_grad, up_grad], axis=1)
+    gate_up_grad = jnp.concatenate([gate_up_sums[0], gate_up_sums[1]], axis=1)
     gate_new = adam_update(
         gate_up_master, gate_up_first, gate_up_second, gate_up_grad, D**-0.5, DECAY_RATE
     )

time: 830 us -> 697 us (0.84)
  waiting for transfers between devices: 191 us -> 120 us
  other arithmetic: 62.7 us -> 39.2 us
  starting transfers between devices: 64.3 us -> 42.9 us
    pallas_call x1, Pallas kernels: 104 us -> 227 us  [feed(): pl.pallas_call(feed_kernel, name='feed', grid=(parts + FEED_LEAD + 4,), i...]
    pallas_call x2 -> x1, Pallas kernels: 162 us -> 44.6 us  [gather_all(): pl.pallas_call(functools.partial(gather_kernel, plan), name='gather_all',...]
    ppermute x35 -> x23, waiting for transfers between devices: 139 us -> 57 us  [swap(): return lax.ppermute(value, axis, pairs)]
    ppermute x35 -> x23, starting transfers between devices: 50.4 us -> 28.5 us  [swap(): return lax.ppermute(value, axis, pairs)]
    ppermute x4, waiting for transfers between devices: 15.9 us -> 28 us  [per_device(): back = [lax.ppermute(p, 'seq', [(1, 0)]) for p in far]]
    dot_general x6 -> x5, matrix products: 25.4 us -> 20 us  [dot_cols(): lax.dot_general(a, b, (((1,), (1,)), ((), ())), preferred_element_type=F32)]
  transfers between devices with their start and end apart: 44 -> 32, of which waited for: 19 -> 18; matrix products, arithmetic and copies ran while one was open for 13% -> 11% of each run, Pallas kernels for 33% -> 19%
where the time goes in v3:
time: 697 us; the launch traced here: 689 us
  Pallas kernels  413 us (59%)
  waiting for transfers between devices  120 us (17%)
  starting transfers between devices  42.9 us (6%)
  other arithmetic  39.2 us (6%)
  matrix products  39 us (6%)
  local copies, waits for them, and re-layouts  19.4 us (3%)
  between operations  15.2 us (2%)
    pallas_call x1, Pallas kernels, feed(): pl.pallas_call(feed_kernel, name='feed', grid=(parts + FEED_LEAD + 4,), i...  227 us
    pallas_call x4, Pallas kernels, attend_back(): pl.pallas_call(attend_back_kernel, name='attend_back', grid_spec=pltpu.Pr...  72.8 us
    ppermute x23, waiting for transfers between devices, swap(): return lax.ppermute(value, axis, pairs)  57 us
    pallas_call x4, Pallas kernels, attend(): pl.pallas_call(attend_kernel, name='attend', grid_spec=pltpu.PrefetchScal...  48.5 us
    pallas_call x1, Pallas kernels, gather_all(): pl.pallas_call(functools.partial(gather_kernel, plan), name='gather_all',...  44.6 us
    ppermute x4, waiting for transfers between devices, per_device(): others = [lax.ppermute(p, 'seq', [(0, 1)]) for p in own]  35.1 us
    ppermute x23, starting transfers between devices, swap(): return lax.ppermute(value, axis, pairs)  28.5 us
    ppermute x4, waiting for transfers between devices, per_device(): back = [lax.ppermute(p, 'seq', [(1, 0)]) for p in far]  28 us
  transfers between devices with their start and end apart: 32, of which 18 were waited for; matrix products, arithmetic and copies ran while one was open for 11% of the time, Pallas kernels for 19%

profile of v3, /device:TPU:0, one launch (start us, length us, event | category | flops | bytes accessed | tf_op | source)
XLA Modules:
  0.0 689.1 jit_solution(15522105921743047249)
XLA Ops:
  12.2 44.6 %gather_all.1 = (bf16[4,2,2,2,32,2048]{5,4,3,2,1,0:T(8,128)(2,1)}, bf16[4,2,2,2,32,1024]{5,4,3,2,1,0:T(8,128)(2,1)}) custom-call(bf16[32,2048]{1,0:T(8,128)(2,1)} %convert_element_type.200.refs_0_, bf16[32,1024]{1,0:T(8,128)(2,1)} %convert_element_type.201.refs_1_), custom_call_target="tpu_custom_call" | custom-call | tf_op jit(solution)/shard_map/gather_all/pallas_call | solution.py:601
  64.4 7.0 %fusion.21.raw_ref = f32[1024,2048]{1,0:T(8,128)} fusion(bf16[1024,2048]{1,0:T(8,128)(2,1)S(1)} %bitcast.95, bf16[1,1024,1024]{2,1,0:T(8,128)(2,1)S(1)} %copy-done.6, f32[1024]{0:T(1024)S(1)} %bitcast.88, f32[1024]{0:T(1024)S(1)} %add_rsqrt_fusion.1), kind=kOutput, calls=%fused_computation.36 | convolution fusion | flops 4299161600 | bytes 14688256 | tf_op jit(solution)/shard_map/dot_general | solution.py:995
  71.4 8.2 %prep.1 = (bf16[1024,1024]{1,0:T(8,128)(2,1)}, bf16[1024,256]{1,0:T(8,128)(2,1)}, bf16[1024,256]{1,0:T(8,128)(2,1)}, bf16[1024,256]{1,0:T(8,128)(2,1)}, bf16[1024,256]{1,0:T(8,128)(2,1)}) custom-call(f32[1024,2048]{1,0:T(8,128)} %fusion.21.raw_ref, f32[8,128]{1,0:T(8,128)} %pad.12.gain_ref, f32[1024,128]{1,0:T(8,128)} %get-tuple-element.146.cos_ref, ...), custom_call_target="tpu_custom_call" | custom-call | flops 83886080 | bytes 12582912 | tf_op jit(solution)/shard_map/prep/pallas_call | solution.py:92
  92.2 21.5 %collective-permute-done.2.ko_ref.vo_ref = bf16[1024,256]{1,0:T(8,128)(2,1)} collective-permute-done((bf16[1024,256]{1,0:T(8,128)(2,1)}, bf16[1024,256]{1,0:T(8,128)(2,1)}, u32[]{:S(2)}, u32[]{:S(2)}) %collective-permute-start.2) | collective-permute-done | bytes 524320 | tf_op jit(solution)/shard_map/ppermute | solution.py:1000
  114.7 12.3 %attend.6 = (bf16[1024,256]{1,0:T(8,128)(2,1)}, f32[2,32,512]{2,1,0:T(8,128)}) custom-call(s32[5]{0:T(128)} %pad_add_fusion.1.low_ref, s32[1024,128]{1,0:T(8,128)} %broadcast_in_dim.32.first_ref, bf16[1024,1024]{1,0:T(8,128)(2,1)} %get-tuple-element.60.q_ref, bf16[1024,256]{1,0:T(8,128)(2,1)} %collective-permute-done.2.ko_ref.vo_ref, ...), custom_call_target="tpu_custom_call" | custom-call | flops 8589934592 | bytes 4194304 | tf_op jit(solution)/shard_map/attend/pallas_call | solution.py:251
  127.0 7.6 %collective-permute-done.1.ko_ref.vo_ref = bf16[1024,256]{1,0:T(8,128)(2,1)} collective-permute-done((bf16[1024,256]{1,0:T(8,128)(2,1)}, bf16[1024,256]{1,0:T(8,128)(2,1)}, u32[]{:S(2)}, u32[]{:S(2)}) %collective-permute-start.1) | collective-permute-done | bytes 524320 | tf_op jit(solution)/shard_map/ppermute | solution.py:1000
  134.6 12.1 %attend.5 = (bf16[1024,256]{1,0:T(8,128)(2,1)}, f32[2,32,512]{2,1,0:T(8,128)}) custom-call(s32[5]{0:T(128)} %pad_add_fusion.1.low_ref, s32[1024,128]{1,0:T(8,128)} %broadcast_in_dim.32.first_ref, bf16[1024,1024]{1,0:T(8,128)(2,1)} %get-tuple-element.60.q_ref, bf16[1024,256]{1,0:T(8,128)(2,1)} %collective-permute-done.1.ko_ref.vo_ref, ...), custom_call_target="tpu_custom_call" | custom-call | flops 8589934592 | bytes 4194304 | tf_op jit(solution)/shard_map/attend/pallas_call | solution.py:251
  146.7 5.9 collective-permute-done.ko_ref.vo_ref
  152.6 12.0 %attend.4 = (bf16[1024,256]{1,0:T(8,128)(2,1)}, f32[2,32,512]{2,1,0:T(8,128)}) custom-call(s32[5]{0:T(128)} %pad_add_fusion.1.low_ref, s32[1024,128]{1,0:T(8,128)} %broadcast_in_dim.32.first_ref, bf16[1024,1024]{1,0:T(8,128)(2,1)} %get-tuple-element.60.q_ref, bf16[1024,256]{1,0:T(8,128)(2,1)} %collective-permute-done.ko_ref.vo_ref, ...), custom_call_target="tpu_custom_call" | custom-call | flops 8589934592 | bytes 4194304 | tf_op jit(solution)/shard_map/attend/pallas_call | solution.py:251
  166.0 12.2 %attend.7 = (bf16[1024,256]{1,0:T(8,128)(2,1)}, f32[2,32,512]{2,1,0:T(8,128)}) custom-call(s32[5]{0:T(128)} %pad_add_fusion.1.low_ref, s32[1024,128]{1,0:T(8,128)} %broadcast_in_dim.32.first_ref, bf16[1024,1024]{1,0:T(8,128)(2,1)} %get-tuple-element.60.q_ref, bf16[1024,256]{1,0:T(8,128)(2,1)} %collective-permute-done.3.ko_ref.vo_ref, ...), custom_call_target="tpu_custom_call" | custom-call | flops 8589934592 | bytes 4194304 | tf_op jit(solution)/shard_map/attend/pallas_call | solution.py:251
  183.7 3.7 fusion.32.at_ref
  187.5 3.7 fusion.31
  191.2 226.8 %feed.1 = (bf16[2,4,2,2,2,32,4608]{6,5,4,3,2,1,0:T(8,128)(2,1)}, f32[1024,1024]{1,0:T(8,128)}, f32[1024,1024]{1,0:T(8,128)}, bf16[4608,1024]{1,0:T(8,128)(2,1)}, f32[2,32,4608]{2,1,0:T(8,128)}) custom-call(bf16[2,32,4608]{2,1,0:T(8,128)(2,1)} %pad_maximum_fusion.1.shard_ref, bf16[1024,1024]{1,0:T(8,128)(2,1)} %copy-done.12, ...), custom_call_target="tpu_custom_call" | custom-call | flops 86973087744 | bytes 56623104 | tf_op jit(solution)/shard_map/feed/pallas_call | solution.py:884
  418.1 5.6 constant_dynamic-slice_fusion.5
  429.2 3.8 collective-permute-done.4
  436.4 3.9 fusion.33
  440.2 9.2 %collective-permute-done.6 = bf16[256,1024]{1,0:T(8,128)(2,1)} collective-permute-done((bf16[256,1024]{1,0:T(8,128)(2,1)}, bf16[256,1024]{1,0:T(8,128)(2,1)}, u32[]{:S(2)}, u32[]{:S(2)}) %collective-permute-start.6) | collective-permute-done | bytes 524320 | tf_op jit(solution)/shard_map/ppermute | solution.py:475
  452.0 3.7 convolution_convert_fusion.2.do_ref
  463.5 4.7 add_convert_fusion
  470.4 18.3 %attend_back.5 = (f32[1024,256]{1,0:T(8,128)}, bf16[1024,256]{1,0:T(8,128)(2,1)}, f32[1024,256]{1,0:T(8,128)}) custom-call(s32[5]{0:T(128)} %pad_add_fusion.1.low_ref, s32[8,1024]{1,0:T(8,128)} %broadcast_in_dim.59.first_ref, bf16[1024,1024]{1,0:T(8,128)(2,1)} %get-tuple-element.60.q_ref, bf16[1024,1024]{1,0:T(8,128)(2,1)} %convolution_convert_fusion.2.do_ref, ...), custom_call_target="tpu_custom_call" | custom-call | flops 12884901888 | bytes 10485760 | tf_op jit(solution)/shard_map/attend_back/pallas_call | solution.py:379
  491.9 18.0 %attend_back.4 = (f32[1024,256]{1,0:T(8,128)}, bf16[1024,256]{1,0:T(8,128)(2,1)}, f32[1024,256]{1,0:T(8,128)}) custom-call(s32[5]{0:T(128)} %pad_add_fusion.1.low_ref, s32[8,1024]{1,0:T(8,128)} %broadcast_in_dim.59.first_ref, bf16[1024,1024]{1,0:T(8,128)(2,1)} %get-tuple-element.60.q_ref, bf16[1024,1024]{1,0:T(8,128)(2,1)} %convolution_convert_fusion.2.do_ref, ...), custom_call_target="tpu_custom_call" | custom-call | flops 12884901888 | bytes 10485760 | tf_op jit(solution)/shard_map/attend_back/pallas_call | solution.py:379
  511.2 11.6 %collective-permute-done.7 = bf16[4,2,1,1,144,1024]{5,4,3,2,1,0:T(8,128)(2,1)} collective-permute-done((bf16[4,2,1,1,144,1024]{5,4,3,2,1,0:T(8,128)(2,1)S(1)}, bf16[4,2,1,1,144,1024]{5,4,3,2,1,0:T(8,128)(2,1)}, u32[]{:S(2)}, u32[]{:S(2)}) %collective-permute-start.7) | collective-permute-done | bytes 2359328 | tf_op jit(solution)/shard_map/ppermute | solution.py:475
  527.1 18.3 %attend_back.6 = (f32[1024,256]{1,0:T(8,128)}, bf16[1024,256]{1,0:T(8,128)(2,1)}, f32[1024,256]{1,0:T(8,128)}) custom-call(s32[5]{0:T(128)} %pad_add_fusion.1.low_ref, s32[8,1024]{1,0:T(8,128)} %broadcast_in_dim.59.first_ref, bf16[1024,1024]{1,0:T(8,128)(2,1)} %get-tuple-element.60.q_ref, bf16[1024,1024]{1,0:T(8,128)(2,1)} %convolution_convert_fusion.2.do_ref, ...), custom_call_target="tpu_custom_call" | custom-call | flops 12884901888 | bytes 10485760 | tf_op jit(solution)/shard_map/attend_back/pallas_call | solution.py:379
  547.4 18.3 %attend_back.7 = (f32[1024,256]{1,0:T(8,128)}, bf16[1024,256]{1,0:T(8,128)(2,1)}, f32[1024,256]{1,0:T(8,128)}) custom-call(s32[5]{0:T(128)} %pad_add_fusion.1.low_ref, s32[8,1024]{1,0:T(8,128)} %broadcast_in_dim.59.first_ref, bf16[1024,1024]{1,0:T(8,128)(2,1)} %get-tuple-element.60.q_ref, bf16[1024,1024]{1,0:T(8,128)(2,1)} %convolution_convert_fusion.2.do_ref, ...), custom_call_target="tpu_custom_call" | custom-call | flops 12884901888 | bytes 10485760 | tf_op jit(solution)/shard_map/attend_back/pallas_call | solution.py:379
  567.7 27.4 %collective-permute-done.16.rest_11_ = bf16[1024,256]{1,0:T(8,128)(2,1)S(1)} collective-permute-done((bf16[1024,256]{1,0:T(8,128)(2,1)}, bf16[1024,256]{1,0:T(8,128)(2,1)S(1)}, u32[]{:S(2)}, u32[]{:S(2)}) %collective-permute-start.16) | collective-permute-done | bytes 524320 | tf_op jit(solution)/shard_map/ppermute | solution.py:1047
  595.9 12.3 %prep_back.1 = (bf16[1024,2048]{1,0:T(8,128)(2,1)}, f32[8,128]{1,0:T(8,128)}) custom-call(f32[1024,2048]{1,0:T(8,128)} %fusion.21.raw_ref, f32[8,128]{1,0:T(8,128)} %pad.12.gain_ref, f32[1024,128]{1,0:T(8,128)} %get-tuple-element.146.cos_ref, f32[1024,128]{1,0:T(8,128)} %get-tuple-element.147.sin_ref, f32[1024,256]{1,0:T(8,128)} %get-tuple-element.77.rest_0_, ...), custom_call_target="tpu_custom_call" | custom-call | flops 125829120 | bytes 20971520 | tf_op jit(solution)/shard_map/prep_back/pallas_call | solution.py:145
  608.3 4.7 convolution_convert_fusion
  622.0 4.9 fusion.12
  631.0 5.2 collective-permute-done.17
  636.2 6.4 collective-permute-start.18
  660.4 8.4 %collective-permute-done.24 = bf16[128,2048]{1,0:T(8,128)(2,1)S(1)} collective-permute-done((bf16[128,2048]{1,0:T(8,128)(2,1)S(1)}, bf16[128,2048]{1,0:T(8,128)(2,1)S(1)}, u32[]{:S(2)}, u32[]{:S(2)}) %collective-permute-start.24) | collective-permute-done | bytes 524320 | tf_op jit(solution)/shard_map/ppermute | solution.py:475
  675.1 6.0 collective-permute-done.26
  (240 shorter events, 105.6 us)
Async XLA Ops:
  7.2 184.0 %all-gather.2.cloned.1.call-start = ((), (), s32[]{:S(2)}) async-start(), calls=%async_computation | async-start | bytes 9732096 | tf_op jit(solution)/shard_map/all_gather | solution.py:454
  79.7 86.3 %collective-permute-start.3 = (bf16[1024,256]{1,0:T(8,128)(2,1)}, bf16[1024,256]{1,0:T(8,128)(2,1)}, u32[]{:S(2)}, u32[]{:S(2)}) collective-permute-start(bf16[1024,256]{1,0:T(8,128)(2,1)} %get-tuple-element.67.k_ref.v_ref), channel_id=1, source_target_pairs={{0,1},{2,3},{4,5},{6,7},{8,9},{10,11},{12,13},{14,15},{16,17},{18,... | collective-permute-start | bytes 1572872 | tf_op jit(solution)/shard_map/ppermute | solution.py:1000
  82.3 31.4 %collective-permute-start.2 = (bf16[1024,256]{1,0:T(8,128)(2,1)}, bf16[1024,256]{1,0:T(8,128)(2,1)}, u32[]{:S(2)}, u32[]{:S(2)}) collective-permute-start(bf16[1024,256]{1,0:T(8,128)(2,1)} %get-tuple-element.65.k_ref.v_ref), channel_id=1, source_target_pairs={{0,1},{2,3},{4,5},{6,7},{8,9},{10,11},{12,13},{14,15},{16,17},{18,... | collective-permute-start | bytes 1572872 | tf_op jit(solution)/shard_map/ppermute | solution.py:1000
  84.4 50.2 %collective-permute-start.1 = (bf16[1024,256]{1,0:T(8,128)(2,1)}, bf16[1024,256]{1,0:T(8,128)(2,1)}, u32[]{:S(2)}, u32[]{:S(2)}) collective-permute-start(bf16[1024,256]{1,0:T(8,128)(2,1)} %get-tuple-element.63.k_ref.v_ref), channel_id=1, source_target_pairs={{0,1},{2,3},{4,5},{6,7},{8,9},{10,11},{12,13},{14,15},{16,17},{18,... | collective-permute-start | bytes 1572872 | tf_op jit(solution)/shard_map/ppermute | solution.py:1000
  86.5 66.1 %collective-permute-start = (bf16[1024,256]{1,0:T(8,128)(2,1)}, bf16[1024,256]{1,0:T(8,128)(2,1)}, u32[]{:S(2)}, u32[]{:S(2)}) collective-permute-start(bf16[1024,256]{1,0:T(8,128)(2,1)} %get-tuple-element.61.k_ref.v_ref), channel_id=1, source_target_pairs={{0,1},{2,3},{4,5},{6,7},{8,9},{10,11},{12,13},{14,15},{16,17},{18,... | collective-permute-start | bytes 1572872 | tf_op jit(solution)/shard_map/ppermute | solution.py:1000
  423.6 39.8 %collective-permute-start.5 = (bf16[4,2,1,2,144,1024]{5,4,3,2,1,0:T(8,128)(2,1)}, bf16[4,2,1,2,144,1024]{5,4,3,2,1,0:T(8,128)(2,1)}, u32[]{:S(2)}, u32[]{:S(2)}) collective-permute-start(bf16[4,2,1,2,144,1024]{5,4,3,2,1,0:T(8,128)(2,1)} %constant_dynamic-slice_fusion.5), channel_id=1, source_target_pairs={{0,2},{2,0},{4,6},{6,4},{8,10},{10,8},{12,14},{14,12},{16,18},{18,... | collective-permute-start | bytes 14155784 | tf_op jit(solution)/shard_map/ppermute | solution.py:475
  429.2 3.9 collective-permute-start.4
  435.2 14.3 %collective-permute-start.6 = (bf16[256,1024]{1,0:T(8,128)(2,1)}, bf16[256,1024]{1,0:T(8,128)(2,1)}, u32[]{:S(2)}, u32[]{:S(2)}) collective-permute-start(bf16[256,1024]{1,0:T(8,128)(2,1)} %slice.133), channel_id=1, source_target_pairs={{0,4},{2,6},{4,0},{6,2},{8,12},{10,14},{12,8},{14,10},{16,20},{18,... | collective-permute-start | bytes 1572872 | tf_op jit(solution)/shard_map/ppermute | solution.py:475
  450.7 7.6 %collective-permute-start.8 = (bf16[128,1024]{1,0:T(8,128)(2,1)S(1)}, bf16[128,1024]{1,0:T(8,128)(2,1)S(1)}, u32[]{:S(2)}, u32[]{:S(2)}) collective-permute-start(bf16[128,1024]{1,0:T(8,128)(2,1)S(1)} %slice.135), channel_id=1, source_target_pairs={{0,1},{1,0},{2,3},{3,2},{4,5},{5,4},{6,7},{7,6},{8,9},{9,8},{10,11... | collective-permute-start | bytes 786440 | tf_op jit(solution)/shard_map/ppermute | solution.py:475
  459.1 31.1 %collective-permute-start.10 = (bf16[32,1024]{1,0:T(8,128)(2,1)}, bf16[32,1024]{1,0:T(8,128)(2,1)S(1)}, u32[]{:S(2)}, u32[]{:S(2)}) collective-permute-start(bf16[32,1024]{1,0:T(8,128)(2,1)} %get-tuple-element.131), channel_id=1, source_target_pairs={{0,8},{2,10},{4,12},{6,14},{8,0},{10,2},{12,4},{14,6},{16,24},{18,... | collective-permute-start | bytes 196616 | tf_op jit(solution)/shard_map/ppermute | solution.py:475
  459.3 30.9 %collective-permute-start.11 = (bf16[32,1024]{1,0:T(8,128)(2,1)}, bf16[32,1024]{1,0:T(8,128)(2,1)}, u32[]{:S(2)}, u32[]{:S(2)}) collective-permute-start(bf16[32,1024]{1,0:T(8,128)(2,1)} %get-tuple-element.133), channel_id=1, source_target_pairs={{0,16},{2,18},{4,20},{6,22},{8,24},{10,26},{12,28},{14,30},{16,0},... | collective-permute-start | bytes 196616 | tf_op jit(solution)/shard_map/ppermute | solution.py:475
  460.0 30.2 %collective-permute-start.12 = (bf16[32,1024]{1,0:T(8,128)(2,1)}, bf16[32,1024]{1,0:T(8,128)(2,1)}, u32[]{:S(2)}, u32[]{:S(2)}) collective-permute-start(bf16[32,1024]{1,0:T(8,128)(2,1)} %get-tuple-element.132), channel_id=1, source_target_pairs={{0,24},{2,26},{4,28},{6,30},{8,16},{10,18},{12,20},{14,22},{16,8},... | collective-permute-start | bytes 196616 | tf_op jit(solution)/shard_map/ppermute | solution.py:475
  468.5 54.4 %collective-permute-start.7 = (bf16[4,2,1,1,144,1024]{5,4,3,2,1,0:T(8,128)(2,1)S(1)}, bf16[4,2,1,1,144,1024]{5,4,3,2,1,0:T(8,128)(2,1)}, u32[]{:S(2)}, u32[]{:S(2)}) collective-permute-start(bf16[4,2,1,1,144,1024]{5,4,3,2,1,0:T(8,128)(2,1)S(1)} %constant_dynamic-slice_fusion.4), channel_id=1, source_target_pairs={{0,1},{1,0},{2,3},{3,2},{4,5},{5,4},{6,7},{7,6},{8,9},{9,8},{10,11... | collective-permute-start | bytes 7077896 | tf_op jit(solution)/shard_map/ppermute | solution.py:475
  488.6 78.4 %collective-permute-start.14 = (bf16[1024,256]{1,0:T(8,128)(2,1)}, bf16[1024,256]{1,0:T(8,128)(2,1)S(1)}, u32[]{:S(2)}, u32[]{:S(2)}) collective-permute-start(bf16[1024,256]{1,0:T(8,128)(2,1)} %get-tuple-element.92), channel_id=1, source_target_pairs={{1,0},{3,2},{5,4},{7,6},{9,8},{11,10},{13,12},{15,14},{17,16},{19,... | collective-permute-start | bytes 1572872 | tf_op jit(solution)/shard_map/ppermute | solution.py:1047
  509.9 57.2 %collective-permute-start.13 = (bf16[1024,256]{1,0:T(8,128)(2,1)}, bf16[1024,256]{1,0:T(8,128)(2,1)}, u32[]{:S(2)}, u32[]{:S(2)}) collective-permute-start(bf16[1024,256]{1,0:T(8,128)(2,1)} %get-tuple-element.91), channel_id=1, source_target_pairs={{1,0},{3,2},{5,4},{7,6},{9,8},{11,10},{13,12},{15,14},{17,16},{19,... | collective-permute-start | bytes 1572872 | tf_op jit(solution)/shard_map/ppermute | solution.py:1047
  525.8 21.1 %collective-permute-start.9 = (bf16[4,1,1,1,144,1024]{5,4,3,2,1,0:T(8,128)(2,1)S(1)}, bf16[4,1,1,1,144,1024]{5,4,3,2,1,0:T(8,128)(2,1)S(1)}, u32[]{:S(2)}, u32[]{:S(2)}) collective-permute-start(bf16[4,1,1,1,144,1024]{5,4,3,2,1,0:T(8,128)(2,1)S(1)} %constant_dynamic-slice_fusion.3), channel_id=1, source_target_pairs={{0,4},{2,6},{4,0},{6,2},{8,12},{10,14},{12,8},{14,10},{16,20},{18,... | collective-permute-start | bytes 3538952 | tf_op jit(solution)/shard_map/ppermute | solution.py:475
  545.3 22.4 %collective-permute-start.15 = (bf16[1024,256]{1,0:T(8,128)(2,1)}, bf16[1024,256]{1,0:T(8,128)(2,1)S(1)}, u32[]{:S(2)}, u32[]{:S(2)}) collective-permute-start(bf16[1024,256]{1,0:T(8,128)(2,1)} %get-tuple-element.93), channel_id=1, source_target_pairs={{1,0},{3,2},{5,4},{7,6},{9,8},{11,10},{13,12},{15,14},{17,16},{19,... | collective-permute-start | bytes 1572872 | tf_op jit(solution)/shard_map/ppermute | solution.py:1047
  565.7 29.5 %collective-permute-start.16 = (bf16[1024,256]{1,0:T(8,128)(2,1)}, bf16[1024,256]{1,0:T(8,128)(2,1)S(1)}, u32[]{:S(2)}, u32[]{:S(2)}) collective-permute-start(bf16[1024,256]{1,0:T(8,128)(2,1)} %get-tuple-element.94), channel_id=1, source_target_pairs={{1,0},{3,2},{5,4},{7,6},{9,8},{11,10},{13,12},{15,14},{17,16},{19,... | collective-permute-start | bytes 1572872 | tf_op jit(solution)/shard_map/ppermute | solution.py:1047
  612.9 17.0 %collective-permute-start.22 = (bf16[512,2048]{1,0:T(8,128)(2,1)S(1)}, bf16[512,2048]{1,0:T(8,128)(2,1)S(1)}, u32[]{:S(2)}, u32[]{:S(2)}) collective-permute-start(bf16[512,2048]{1,0:T(8,128)(2,1)S(1)} %convolution_convert_fusion), channel_id=1, source_target_pairs={{0,2},{2,0},{4,6},{6,4},{8,10},{10,8},{12,14},{14,12},{16,18},{18,... | collective-permute-start | bytes 6291464 | tf_op jit(solution)/shard_map/ppermute | solution.py:475
  615.5 33.2 %collective-permute-start.28 = (bf16[1,1,1,1,144,1024]{5,4,3,2,1,0:T(8,128)(2,1)S(1)}, bf16[1,1,1,1,144,1024]{5,4,3,2,1,0:T(8,128)(2,1)S(1)}, u32[]{:S(2)}, u32[]{:S(2)}) collective-permute-start(bf16[1,1,1,1,144,1024]{5,4,3,2,1,0:T(8,128)(2,1)S(1)} %get-tuple-element.121), channel_id=1, source_target_pairs={{0,8},{2,10},{4,12},{6,14},{8,0},{10,2},{12,4},{14,6},{16,24},{18,... | collective-permute-start | bytes 884744 | tf_op jit(solution)/shard_map/ppermute | solution.py:475
  616.3 32.4 %collective-permute-start.29 = (bf16[1,1,1,1,144,1024]{5,4,3,2,1,0:T(8,128)(2,1)S(1)}, bf16[1,1,1,1,144,1024]{5,4,3,2,1,0:T(8,128)(2,1)S(1)}, u32[]{:S(2)}, u32[]{:S(2)}) collective-permute-start(bf16[1,1,1,1,144,1024]{5,4,3,2,1,0:T(8,128)(2,1)S(1)} %get-tuple-element.123), channel_id=1, source_target_pairs={{0,16},{2,18},{4,20},{6,22},{8,24},{10,26},{12,28},{14,30},{16,0},... | collective-permute-start | bytes 884744 | tf_op jit(solution)/shard_map/ppermute | solution.py:475
  619.9 28.8 %collective-permute-start.30 = (bf16[1,1,1,1,144,1024]{5,4,3,2,1,0:T(8,128)(2,1)S(1)}, bf16[1,1,1,1,144,1024]{5,4,3,2,1,0:T(8,128)(2,1)S(1)}, u32[]{:S(2)}, u32[]{:S(2)}) collective-permute-start(bf16[1,1,1,1,144,1024]{5,4,3,2,1,0:T(8,128)(2,1)S(1)} %get-tuple-element.122), channel_id=1, source_target_pairs={{0,24},{2,26},{4,28},{6,30},{8,16},{10,18},{12,20},{14,22},{16,8},... | collective-permute-start | bytes 884744 | tf_op jit(solution)/shard_map/ppermute | solution.py:475
  627.0 9.2 %collective-permute-start.17 = (f32[8,1024]{1,0:T(8,128)S(1)}, f32[8,1024]{1,0:T(8,128)S(1)}, u32[]{:S(2)}, u32[]{:S(2)}) collective-permute-start(f32[8,1024]{1,0:T(8,128)S(1)} %pad.14), channel_id=1, source_target_pairs={{0,8},{2,10},{4,12},{6,14},{8,0},{10,2},{12,4},{14,6},{16,24},{18,... | collective-permute-start | bytes 98312 | tf_op jit(solution)/shard_map/ppermute | solution.py:475
  630.9 24.8 %collective-permute-start.23 = (bf16[256,2048]{1,0:T(8,128)(2,1)S(1)}, bf16[256,2048]{1,0:T(8,128)(2,1)S(1)}, u32[]{:S(2)}, u32[]{:S(2)}) collective-permute-start(bf16[256,2048]{1,0:T(8,128)(2,1)S(1)} %slice.146), channel_id=1, source_target_pairs={{0,1},{1,0},{2,3},{3,2},{4,5},{5,4},{6,7},{7,6},{8,9},{9,8},{10,11... | collective-permute-start | bytes 3145736 | tf_op jit(solution)/shard_map/ppermute | solution.py:475
  636.2 11.8 %collective-permute-start.18 = (f32[8,1024]{1,0:T(8,128)S(1)}, f32[8,1024]{1,0:T(8,128)S(1)}, u32[]{:S(2)}, u32[]{:S(2)}) collective-permute-start(f32[8,1024]{1,0:T(8,128)S(1)} %pad_add_fusion), channel_id=1, source_target_pairs={{0,16},{2,18},{4,20},{6,22},{8,24},{10,26},{12,28},{14,30},{16,0},... | collective-permute-start | bytes 98312 | tf_op jit(solution)/shard_map/ppermute | solution.py:475
  647.9 3.9 collective-permute-start.19
  651.9 1.2 collective-permute-start.20
  653.1 6.6 collective-permute-start.21
  656.1 12.6 %collective-permute-start.24 = (bf16[128,2048]{1,0:T(8,128)(2,1)S(1)}, bf16[128,2048]{1,0:T(8,128)(2,1)S(1)}, u32[]{:S(2)}, u32[]{:S(2)}) collective-permute-start(bf16[128,2048]{1,0:T(8,128)(2,1)S(1)} %slice.148), channel_id=1, source_target_pairs={{0,4},{2,6},{4,0},{6,2},{8,12},{10,14},{12,8},{14,10},{16,20},{18,... | collective-permute-start | bytes 1572872 | tf_op jit(solution)/shard_map/ppermute | solution.py:475
  668.9 6.2 collective-permute-start.25
  670.4 10.6 %collective-permute-start.26 = (bf16[32,2048]{1,0:T(8,128)(2,1)S(1)}, bf16[32,2048]{1,0:T(8,128)(2,1)S(1)}, u32[]{:S(2)}, u32[]{:S(2)}) collective-permute-start(bf16[32,2048]{1,0:T(8,128)(2,1)S(1)} %get-tuple-element.130), channel_id=1, source_target_pairs={{0,16},{2,18},{4,20},{6,22},{8,24},{10,26},{12,28},{14,30},{16,0},... | collective-permute-start | bytes 393224 | tf_op jit(solution)/shard_map/ppermute | solution.py:475
  672.1 8.9 %collective-permute-start.27 = (bf16[32,2048]{1,0:T(8,128)(2,1)S(1)}, bf16[32,2048]{1,0:T(8,128)(2,1)S(1)}, u32[]{:S(2)}, u32[]{:S(2)}) collective-permute-start(bf16[32,2048]{1,0:T(8,128)(2,1)S(1)} %get-tuple-element.129), channel_id=1, source_target_pairs={{0,24},{2,26},{4,28},{6,30},{8,16},{10,18},{12,20},{14,22},{16,8},... | collective-permute-start | bytes 393224 | tf_op jit(solution)/shard_map/ppermute | solution.py:475
  (56 other events, 655.1 us)
Sparse Core Ops, SparseCore 0:
  57.0 91.9 all-gather.1

commit v4 on v3

--- a/solution.py
+++ b/solution.py
@@ -28,7 +28,7 @@
 
 F32 = jnp.float32
 BF16 = jnp.bfloat16
-QUERY_BLOCK = 256
+QUERY_BLOCK = 128
 KEY_BLOCK = 256
 FF_BLOCK = 256
 PIECES = 4
@@ -105,8 +105,8 @@
 
 
 def prep_back_kernel(raw_ref, gain_ref, cos_ref, sin_ref, *rest):
-    dq_refs, own_refs, back_refs = (rest[PIECES * i : PIECES * (i + 1)] for i in range(3))
-    out_ref, dg_ref = rest[3 * PIECES :]
+    dq_ref, own_refs, back_refs = rest[0], rest[1 : PIECES + 1], rest[PIECES + 1 : 2 * PIECES + 1]
+    out_ref, dg_ref = rest[2 * PIECES + 1 :]
     cosine, sine = cos_ref[...], sin_ref[...]
     sums = [jnp.zeros((1, LANES), F32), jnp.zeros((1, LANES), F32)]
     for group in range(12):
@@ -115,8 +115,7 @@
         which = 0 if group < 8 else 1
         gain = gain_ref[which : which + 1]
         if group < 8:
-            half = slice(group % 2 * LANES, (group % 2 + 1) * LANES)
-            d = dq_refs[group // 2][:, half] * HEAD_SIZE**-0.5
+            d = dq_ref[:, part] * HEAD_SIZE**-0.5
         else:
             own, back = own_refs[group - 8], back_refs[group - 8]
             d = own[:, :LANES] + back[:, :LANES].astype(F32)
@@ -151,8 +150,9 @@
             small,
             whole(LANES),
             whole(LANES),
+            whole(QUERY_FEATURES),
         ]
-        + [whole(2 * LANES)] * (3 * PIECES),
+        + [whole(2 * LANES)] * (2 * PIECES),
         out_specs=[whole(2048), small],
         out_shape=[
             jax.ShapeDtypeStruct((rows, 2048), BF16),
@@ -162,255 +162,215 @@
         cost_estimate=pl.CostEstimate(
             flops=rows * 2048 * 60, transcendentals=rows * 24, bytes_accessed=rows * 2048 * 10
         ),
-    )(raw, gains, cosine, sine, *dq, *own, *back)
-
-
-def twice(pair, odd):
-    wide = pair.astype(F32)
-    turned = pltpu.roll(wide, HEAD_SIZE, 1)
-    lane = lax.broadcasted_iota(jnp.int32, wide.shape, 1)
-    first = lane < HEAD_SIZE
-    keep = first != (odd == 1)
-    return jnp.where(keep, wide, turned).astype(BF16)
-
-
-def stack_heads(pair):
-    lane = lax.broadcasted_iota(jnp.int32, pair.shape, 1)
-    zero = jnp.zeros_like(pair)
-    return jnp.concatenate(
-        [jnp.where(lane < HEAD_SIZE, pair, zero), jnp.where(lane < HEAD_SIZE, zero, pair)], axis=0
-    )
-
-
-def fill(head, others, own, lane_block, target):
-    odd = lax.rem(head, 2)
-    at = 0
-    for source in (others, own):
-        rows = source.shape[0]
-        for start in range(0, rows, 256):
-            target[at + start : at + start + 256, lane_block : lane_block + LANES] = twice(
-                source[start : start + 256, :], odd
-            )
-        at += rows
-
-
-def attend_kernel(
-    low_ref,
-    first_ref,
-    q_ref,
-    ko_ref,
-    vo_ref,
-    k_ref,
-    v_ref,
-    out_ref,
-    lse_ref,
-    keys,
-    values,
-):
-    head, turn = pl.program_id(0), pl.program_id(1)
+    )(raw, gains, cosine, sine, dq, *own, *back)
+
+
+def stack_heads(rows):
+    first, second = rows[:, :LANES].astype(F32), rows[:, LANES:].astype(F32)
+    lane = lax.broadcasted_iota(jnp.int32, first.shape, 1)
+    low = lane < HEAD_SIZE
+    turn = lambda v: pltpu.roll(v, HEAD_SIZE, 1)
+    heads = [
+        jnp.where(low, first, 0.0),
+        jnp.where(low, turn(first), 0.0),
+        jnp.where(low, 0.0, turn(second)),
+        jnp.where(low, 0.0, second),
+    ]
+    return jnp.concatenate(heads, axis=0).astype(BF16)
+
+
+def unstack_heads(tall):
+    n = tall.shape[0] // 4
+    a, b, c, d = (tall[i * n : (i + 1) * n] for i in range(4))
+    low = lax.broadcasted_iota(jnp.int32, a.shape, 1) < HEAD_SIZE
+    turn = lambda v: pltpu.roll(v, HEAD_SIZE, 1)
+    return jnp.concatenate([jnp.where(low, a, turn(b)), jnp.where(low, turn(c), d)], axis=1)
+
+
+def key_range(low_ref, turn, block, start, rows):
+    begin = low_ref[1 + turn] // KEY_BLOCK
+    end = (low_ref[0] + turn * block + block - 1) // KEY_BLOCK + 1
+    first, last = start // KEY_BLOCK, (start + rows) // KEY_BLOCK
+    return jnp.clip(begin, first, last), jnp.clip(end, first, last)
+
+
+def attend_kernel(low_ref, first_ref, q_ref, *rest):
+    sources = (rest[:PIECES], rest[PIECES : 2 * PIECES])
+    out_ref, lse_ref, queries, totals = rest[2 * PIECES :]
+    turn = pl.program_id(0)
     block = q_ref.shape[0]
-    tall = 2 * block
-
-    @pl.when(turn == 0)
-    def _():
-        fill(head, ko_ref, k_ref, 0, keys)
-        fill(head, vo_ref, v_ref, 0, values)
-        values[:, LANES:] = jnp.ones((values.shape[0], LANES), BF16)
-
-    queries = stack_heads(q_ref[...])
-    place0 = low_ref[0] + turn * block
-    place = place0 + lax.rem(lax.broadcasted_iota(jnp.int32, (tall, 1), 0), block)
-    first = first_ref[:, 0:1]
-    first = jnp.concatenate([first, first], axis=0)
-    begin = low_ref[1 + turn] // KEY_BLOCK
-    end = (place0 + block - 1) // KEY_BLOCK + 1
-
-    def step(at, total):
-        start = pl.multiple_of(at * KEY_BLOCK, KEY_BLOCK)
-        scores = dot_cols(queries, keys[pl.ds(start, KEY_BLOCK), :])
-        key_place = start + lax.broadcasted_iota(jnp.int32, (tall, KEY_BLOCK), 1)
-        allowed = (key_place >= first) & (key_place <= place)
-        powers = jnp.where(allowed, jnp.exp(scores), 0.0).astype(BF16)
-        return total + dot(powers, values[pl.ds(start, KEY_BLOCK), :])
-
-    total = lax.fori_loop(begin, end, step, jnp.zeros((tall, 2 * LANES), F32))
-    mass = total[:, LANES:]
-    mixed = total[:, :LANES] / mass
-    lane = lax.broadcasted_iota(jnp.int32, (block, LANES), 1)
-    out_ref[...] = jnp.where(lane < HEAD_SIZE, mixed[:block], mixed[block:]).astype(BF16)
-    logs = jnp.log(mass)
-    lse_ref[0] = jnp.transpose(logs)[0:8, :]
-
-
-def attend(piece, q, others, own, low, first):
+    for p in range(PIECES):
+        queries[p] = stack_heads(q_ref[:, p * 2 * LANES : (p + 1) * 2 * LANES])
+    totals[...] = jnp.zeros_like(totals)
+    place = low_ref[0] + turn * block + lax.broadcasted_iota(jnp.int32, (block, KEY_BLOCK), 0)
+    first = jnp.concatenate([first_ref[...]] * (KEY_BLOCK // LANES), axis=1)
+    column = lax.broadcasted_iota(jnp.int32, (block, KEY_BLOCK), 1)
+    ones = jnp.ones((KEY_BLOCK, LANES), BF16)
+    start = 0
+    for refs in sources:
+        rows = refs[0].shape[0]
+
+        def step(at, _):
+            span = pl.ds(pl.multiple_of(at * KEY_BLOCK - start, KEY_BLOCK), KEY_BLOCK)
+            key_place = at * KEY_BLOCK + column
+            allowed = (key_place >= first) & (key_place <= place)
+            for p in range(PIECES):
+                scores = dot_cols(queries[p], refs[p][span, :LANES])
+                scores = scores.reshape(4, block, KEY_BLOCK)
+                powers = jnp.where(allowed[None], jnp.exp(scores), 0.0).astype(BF16)
+                values = jnp.concatenate([refs[p][span, LANES:], ones], axis=1)
+                totals[p] += dot(powers.reshape(4 * block, KEY_BLOCK), values)
+            return 0
+
+        begin, end = key_range(low_ref, turn, block, start, rows)
+        lax.fori_loop(begin, end, step, 0)
+        start += rows
+    for p in range(PIECES):
+        mass = totals[p, :, LANES:]
+        mixed = totals[p, :, :LANES] / mass
+        out_ref[:, p * 2 * LANES : (p + 1) * 2 * LANES] = unstack_heads(mixed).astype(BF16)
+        lse_ref[:, p * 4 * block : (p + 1) * 4 * block] = jnp.transpose(jnp.log(mass))[0:8, :]
+
+
+def attend(q, others, own, low, first):
     rows = q.shape[0]
-    block = min(QUERY_BLOCK, rows)
+    block = QUERY_BLOCK
     turns = rows // block
-    total = others.shape[0] + rows
-    pair = lambda size, off: pl.BlockSpec((size, LANES), lambda h, t, low: (0, off))
+    whole = lambda size: pl.BlockSpec((size, 2 * LANES), lambda t, low: (0, 0))
+    wide = pl.BlockSpec((block, QUERY_FEATURES), lambda t, low: (t, 0))
     return pl.pallas_call(
         attend_kernel,
         name="attend",
         grid_spec=pltpu.PrefetchScalarGridSpec(
             num_scalar_prefetch=1,
-            grid=(2, turns),
-            in_specs=[
-                pl.BlockSpec((block, LANES), lambda h, t, low: (t, 0)),
-                pl.BlockSpec((block, LANES), lambda h, t, low: (t, 2 * piece + h)),
-                pair(others.shape[0], 0),
-                pair(others.shape[0], 1),
-                pair(rows, 0),
-                pair(rows, 1),
+            grid=(turns,),
+            in_specs=[pl.BlockSpec((block, LANES), lambda t, low: (t, 0)), wide]
+            + [whole(others[0].shape[0])] * PIECES
+            + [whole(rows)] * PIECES,
+            out_specs=[wide, pl.BlockSpec((8, HQ * block), lambda t, low: (t, 0))],
+            scratch_shapes=[
+                pltpu.VMEM((PIECES, 4 * block, LANES), BF16),
+                pltpu.VMEM((PIECES, 4 * block, 2 * LANES), F32),
             ],
-            out_specs=[
-                pl.BlockSpec((block, LANES), lambda h, t, low: (t, h)),
-                pl.BlockSpec((1, 8, 2 * block), lambda h, t, low: (h, t, 0)),
-            ],
-            scratch_shapes=[pltpu.VMEM((total, LANES), BF16), pltpu.VMEM((total, 2 * LANES), BF16)],
         ),
         out_shape=[
-            jax.ShapeDtypeStruct((rows, 2 * LANES), BF16),
-            jax.ShapeDtypeStruct((2, 8 * turns, 2 * block), F32),
+            jax.ShapeDtypeStruct((rows, QUERY_FEATURES), BF16),
+            jax.ShapeDtypeStruct((8 * turns, HQ * block), F32),
         ],
         compiler_params=params(),
         cost_estimate=pl.CostEstimate(
-            flops=rows * 1024 * 1024 * 8, transcendentals=rows * 1024 * 4, bytes_accessed=4 << 20
+            flops=rows * 1024 * 1024 * 24, transcendentals=rows * 1024 * 16, bytes_accessed=16 << 20
         ),
-    )(low, first, q, others, others, own, own)
-
-
-def attend_back_kernel(
-    low_ref,
-    first_ref,
-    q_ref,
-    do_ref,
-    mixed_ref,
-    lse_ref,
-    ko_ref,
-    vo_ref,
-    k_ref,
-    v_ref,
-    dq_ref,
-    far_ref,
-    near_ref,
-    keys,
-    values,
-    dkeys,
-    dvalues,
-):
-    head, turn = pl.program_id(0), pl.program_id(1)
+    )(low, first, q, *others, *own)
+
+
+def attend_back_kernel(start, low_ref, first_ref, q_ref, do_ref, mixed_ref, lse_ref, before_ref, *rest):
+    refs, d_refs = rest[:PIECES], rest[PIECES : 2 * PIECES]
+    dq_ref, queries, rising, deltas, dqs, dkvs = rest[2 * PIECES :]
+    turn = pl.program_id(0)
     block = q_ref.shape[0]
-    tall = 2 * block
+    rows = refs[0].shape[0]
+    tall = 4 * block
 
     @pl.when(turn == 0)
     def _():
-        fill(head, ko_ref, k_ref, 0, keys)
-        fill(head, vo_ref, v_ref, 0, values)
-        dkeys[...] = jnp.zeros_like(dkeys)
-        dvalues[...] = jnp.zeros_like(dvalues)
-
-    queries = stack_heads(q_ref[...])
-    rising = stack_heads(do_ref[...])
-    across = jnp.transpose(do_ref[...].astype(F32) * mixed_ref[...].astype(F32))
-    delta = jnp.concatenate(
-        [
-            jnp.sum(across[:HEAD_SIZE], axis=0, keepdims=True),
-            jnp.sum(across[HEAD_SIZE:], axis=0, keepdims=True),
-        ],
-        axis=1,
-    )
-    logs = lse_ref[0][0:1]
-    place0 = low_ref[0] + turn * block
-    place = place0 + lax.rem(lax.broadcasted_iota(jnp.int32, (1, tall), 1), block)
-    first = first_ref[0:1]
-    first = jnp.concatenate([first, first], axis=1)
-    begin = low_ref[1 + turn] // KEY_BLOCK
-    end = (place0 + block - 1) // KEY_BLOCK + 1
-
-    def step(at, dq):
-        start = pl.multiple_of(at * KEY_BLOCK, KEY_BLOCK)
-        span = pl.ds(start, KEY_BLOCK)
-        key = keys[span, :]
-        scores = dot_cols(key, queries)
-        key_place = start + lax.broadcasted_iota(jnp.int32, (KEY_BLOCK, tall), 0)
-        allowed = (key_place >= first) & (key_place <= place)
-        probs = jnp.where(allowed, jnp.exp(scores - logs), 0.0)
-        dprobs = dot_cols(values[span, :], rising)
-        dscores = (probs * (dprobs - delta)).astype(BF16)
-        dkeys[span, :] += dot(dscores, queries)
-        dvalues[span, :] += dot(probs.astype(BF16), rising)
-        return dq + dot_rows(dscores, key)
-
-    dq = lax.fori_loop(begin, end, step, jnp.zeros((tall, LANES), F32))
-    lane = lax.broadcasted_iota(jnp.int32, (block, LANES), 1)
-    dq_ref[...] = jnp.where(lane < HEAD_SIZE, dq[:block], dq[block:])
-
-    @pl.when(turn == pl.num_programs(1) - 1)
+        dkvs[...] = jnp.zeros_like(dkvs)
+
+    begin, end = key_range(low_ref, turn, block, start, rows)
+
+    @pl.when(end <= begin)
     def _():
-        odd = lax.rem(head, 2)
-        far = far_ref.shape[0]
-        for source, off in ((dkeys, 0), (dvalues, LANES)):
-            for start in range(0, source.shape[0], 256):
-                both = source[start : start + 256, :]
-                both = both + pltpu.roll(both, HEAD_SIZE, 1)
-                lane = lax.broadcasted_iota(jnp.int32, both.shape, 1)
-                mine = (lane < HEAD_SIZE) != (odd == 1)
-                target, to = (far_ref, start) if start < far else (near_ref, start - far)
-                part = (slice(to, to + 256), slice(off, off + LANES))
-
-                @pl.when(odd == 0)
-                def _():
-                    target[part] = both.astype(target.dtype)
-
-                @pl.when(odd == 1)
-                def _():
-                    target[part] = jnp.where(mine, both, target[part].astype(F32)).astype(target.dtype)
-
-
-def attend_back(piece, q, d_mixed, mixed, lse, others, own, low, first_lane):
+        dq_ref[...] = before_ref[...]
+
+    @pl.when(end > begin)
+    def _():
+        for p in range(PIECES):
+            part = slice(p * 2 * LANES, (p + 1) * 2 * LANES)
+            queries[p] = stack_heads(q_ref[:, part])
+            rising[p] = stack_heads(do_ref[:, part])
+            across = jnp.transpose(do_ref[:, part].astype(F32) * mixed_ref[:, part].astype(F32))
+            deltas[p] = jnp.concatenate(
+                [
+                    jnp.broadcast_to(
+                        jnp.sum(across[i * HEAD_SIZE : (i + 1) * HEAD_SIZE], axis=0, keepdims=True),
+                        (8, block),
+                    )
+                    for i in range(4)
+                ],
+                axis=1,
+            )
+        dqs[...] = jnp.zeros_like(dqs)
+        shape = (KEY_BLOCK, block)
+        place = low_ref[0] + turn * block + lax.broadcasted_iota(jnp.int32, shape, 1)
+        row = lax.broadcasted_iota(jnp.int32, shape, 0)
+        first = first_ref[0:1]
+
+        def step(at, _):
+            span = pl.ds(pl.multiple_of(at * KEY_BLOCK - start, KEY_BLOCK), KEY_BLOCK)
+            key_place = at * KEY_BLOCK + row
+            allowed = (key_place >= first) & (key_place <= place)
+            allowed = jnp.concatenate([allowed] * 4, axis=1)
+            for p in range(PIECES):
+                key, value = refs[p][span, :LANES], refs[p][span, LANES:]
+                logs = lse_ref[0:1, p * tall : (p + 1) * tall]
+                probs = jnp.where(allowed, jnp.exp(dot_cols(key, queries[p]) - logs), 0.0)
+                dprobs = dot_cols(value, rising[p])
+                dscores = (probs * (dprobs - deltas[p, 0:1])).astype(BF16)
+                dkvs[p, span, :LANES] += dot(dscores, queries[p])
+                dkvs[p, span, LANES:] += dot(probs.astype(BF16), rising[p])
+                dqs[p] += dot_rows(dscores, key)
+            return 0
+
+        lax.fori_loop(begin, end, step, 0)
+        for p in range(PIECES):
+            part = slice(p * 2 * LANES, (p + 1) * 2 * LANES)
+            dq_ref[:, part] = before_ref[:, part] + unstack_heads(dqs[p])
+
+    @pl.when(turn == pl.num_programs(0) - 1)
+    def _():
+        for p in range(PIECES):
+            d_refs[p][...] = dkvs[p].astype(d_refs[p].dtype)
+
+
+def attend_back(start, q, d_mixed, mixed, lse, before, source, low, first_lane, kind):
     rows = q.shape[0]
-    block = min(QUERY_BLOCK, rows)
+    block = QUERY_BLOCK
     turns = rows // block
-    total = others.shape[0] + rows
-    pair = lambda size, off: pl.BlockSpec((size, LANES), lambda h, t, low: (0, off))
-    whole = lambda size: pl.BlockSpec((size, 2 * LANES), lambda h, t, low: (0, 0))
-    tile = pl.BlockSpec((block, LANES), lambda h, t, low: (t, h))
-    tile_of_all = pl.BlockSpec((block, LANES), lambda h, t, low: (t, 2 * piece + h))
-    return pl.pallas_call(
-        attend_back_kernel,
+    count = source[0].shape[0]
+    whole = pl.BlockSpec((count, 2 * LANES), lambda t, low: (0, 0))
+    wide = pl.BlockSpec((block, QUERY_FEATURES), lambda t, low: (t, 0))
+    *pieces, dq = pl.pallas_call(
+        functools.partial(attend_back_kernel, start),
         name="attend_back",
         grid_spec=pltpu.PrefetchScalarGridSpec(
             num_scalar_prefetch=1,
-            grid=(2, turns),
+            grid=(turns,),
             in_specs=[
-                pl.BlockSpec((8, block), lambda h, t, low: (0, t)),
-                tile_of_all,
-                tile_of_all,
-                tile,
-                pl.BlockSpec((1, 8, 2 * block), lambda h, t, low: (h, t, 0)),
-                pair(others.shape[0], 0),
-                pair(others.shape[0], 1),
-                pair(rows, 0),
-                pair(rows, 1),
-            ],
-            out_specs=[tile, whole(others.shape[0]), whole(rows)],
+                pl.BlockSpec((8, block), lambda t, low: (0, t)),
+                wide,
+                wide,
+                wide,
+                pl.BlockSpec((8, HQ * block), lambda t, low: (t, 0)),
+                wide,
+            ]
+            + [whole] * PIECES,
+            out_specs=[whole] * PIECES + [wide],
             scratch_shapes=[
-                pltpu.VMEM((total, LANES), BF16),
-                pltpu.VMEM((total, LANES), BF16),
-                pltpu.VMEM((total, LANES), F32),
-                pltpu.VMEM((total, LANES), F32),
+                pltpu.VMEM((PIECES, 4 * block, LANES), BF16),
+                pltpu.VMEM((PIECES, 4 * block, LANES), BF16),
+                pltpu.VMEM((PIECES, 8, 4 * block), F32),
+                pltpu.VMEM((PIECES, 4 * block, LANES), F32),
+                pltpu.VMEM((PIECES, count, 2 * LANES), F32),
             ],
         ),
-        out_shape=[
-            jax.ShapeDtypeStruct((rows, 2 * LANES), F32),
-            jax.ShapeDtypeStruct((others.shape[0], 2 * LANES), BF16),
-            jax.ShapeDtypeStruct((rows, 2 * LANES), F32),
-        ],
+        out_shape=[jax.ShapeDtypeStruct((count, 2 * LANES), kind)] * PIECES
+        + [jax.ShapeDtypeStruct((rows, QUERY_FEATURES), F32)],
         compiler_params=params(),
         cost_estimate=pl.CostEstimate(
-            flops=rows * 1024 * 1024 * 12, transcendentals=rows * 1024 * 4, bytes_accessed=10 << 20
+            flops=rows * 1024 * 1024 * 24, transcendentals=rows * 1024 * 16, bytes_accessed=30 << 20
         ),
-    )(low, first_lane, q, d_mixed, mixed, lse, others, others, own, own)
+    )(low, first_lane, q, d_mixed, mixed, lse, before, *source)
+    return dq, pieces
 
 
 def rms_scale(v):
@@ -630,6 +590,7 @@
     return terms
 
 
+FIRST_PARTS = 3
 FEED_LEAD = 4
 
 
@@ -751,18 +712,18 @@
         def _():
             run(p)
 
+    def begin(p):
+        for copy in gather_copies(p, 0):
+            copy.start()
+
     @pl.when(step == 0)
     def _():
         own_copy().start()
         pltpu.make_async_copy(start_ref, y_ref, start_sem).start()
         greet()
 
-        def begin(p, _):
-            for copy in gather_copies(p, 0):
-                copy.start()
-            return 0
-
-        lax.fori_loop(0, parts, begin, 0)
+        for p in range(FIRST_PARTS):
+            begin(jnp.int32(p))
         own_copy().wait()
         pltpu.make_async_copy(start_ref, y_ref, start_sem).wait()
         b_ref[...] = jnp.zeros_like(b_ref)
@@ -780,6 +741,10 @@
         for copy in gather_copies(p, 3):
             copy.wait_recv()
         load_copy(p).start()
+
+    @pl.when((step > 0) & (step + FIRST_PARTS - 1 < parts))
+    def _():
+        begin(step + FIRST_PARTS - 1)
 
     on(3, arrived)
     on(2, pass_on(3))
@@ -970,9 +935,8 @@
     seq_width = lax.axis_size("seq")
     turn_here = lax.axis_index("seq")
     rows = inputs.shape[1]
-    block = min(QUERY_BLOCK, rows)
+    block = QUERY_BLOCK
     w_qkv, w_out = gather_all([qkv_master.astype(BF16), out_master.astype(BF16)], 512, 1)
-    w_down = gather(after(down_master.astype(BF16), w_qkv))
 
     places = turn_here * rows + jnp.arange(rows, dtype=jnp.int32)
     row_lengths = lengths[0]
@@ -995,13 +959,12 @@
     raw = jnp.dot(normed_first, w_qkv, preferred_element_type=F32)
     gain_rows = jnp.pad(jnp.tile(qk_gains, (1, 2)), ((0, 6), (0, 0)))
     q, *own = prep(raw, gain_rows, cosine, sine)
-    pieces = range(PIECES)
     if seq_width == 2:
         others = [lax.ppermute(p, "seq", [(0, 1)]) for p in own]
     else:
         others = [lax.all_gather(p, "seq", axis=0, tiled=True) for p in own]
-    mixes, lses = zip(*[attend(p, q, others[p], own[p], low, first_wide) for p in pieces])
-    mixed = jnp.concatenate(mixes, axis=1)
+    w_down = gather(after(down_master.astype(BF16), others[3]))
+    mixed, lse = attend(q, others, own, low, first_wide)
     x_mid = x + jnp.dot(mixed, w_out, preferred_element_type=F32)
     scale_second = rms_scale(x_mid)
     normed_second = (x_mid * scale_second * norm_gains[1]).astype(BF16)
@@ -1018,8 +981,7 @@
         2,
     )
     outputs = out_sum.astype(BF16)
-    sizes = [dims()[k][2] for k in NAMES]
-    down_1 = own_part(grad_down.reshape(*sizes, FF // math.prod(sizes), D), "c")
+    down_grad = lax.psum_scatter(grad_down, ALL, scatter_dimension=0, tiled=True).astype(F32)
     d_norm, d_gain_second = rms_back(x_mid, scale_second, norm_gains[1], d_b)
     d_mid = g.astype(F32) + d_norm
     d_attn = d_mid.astype(BF16)
@@ -1030,23 +992,17 @@
         dot(out_terms[:half], d_attn).astype(BF16), dot(out_terms[half:], d_attn).astype(BF16), "c"
     )
 
-    def back_piece(p, earlier):
-        d = after(d_mixed, earlier)
-        return attend_back(p, q, d, mixes[p], lses[p], others[p], own[p], low, first_lane)
-
-    parts = [back_piece(0, (out_1, down_1))]
-    down_2, out_2 = own_part(down_1, "x"), add_along(out_1, "y")
-    parts.append(back_piece(1, out_2))
-    out_3 = add_along(out_2, "x")
-    parts.append(back_piece(2, (down_2, out_3)))
-    down_3, out_grad = own_part(down_2, "y"), add_along(out_3, "z", True)
-    parts.append(back_piece(3, (down_3, out_grad)))
-    down_grad = own_part(down_3, "z", True).reshape(-1, D)
-    dq, far, near = zip(*parts)
+    zero = jnp.zeros((rows, QUERY_FEATURES), F32)
+    dq, far = attend_back(0, q, d_mixed, mixed, lse, zero, others, low, first_lane, BF16)
     if seq_width == 2:
         back = [lax.ppermute(p, "seq", [(1, 0)]) for p in far]
     else:
         back = [lax.psum_scatter(p, "seq", scatter_dimension=0, tiled=True) for p in far]
+    out_2 = add_along(out_1, "y")
+    dq, near = attend_back(
+        others[0].shape[0], q, after(d_mixed, out_2), mixed, lse, dq, own, low, first_lane, F32
+    )
+    out_grad = add_along(add_along(out_2, "x"), "z", True)
     d_qkv, d_gain_qk = prep_back(raw, gain_rows, cosine, sine, dq, near, back)
     first_terms = transpose_in_order(hot_x, normed_first)
     qkv_1 = add_swapped(

time: 697 us -> 630 us (0.904)
  Pallas kernels: 413 us -> 343 us
  waiting for transfers between devices: 120 us -> 133 us
    pallas_call x4 -> x1, Pallas kernels: 48.5 us -> 19.3 us  [attend(): pl.pallas_call(attend_kernel, name='attend', grid_spec=pltpu.PrefetchScal...]
    pallas_call x4 -> x2, Pallas kernels: 72.8 us -> 45.4 us  [attend_back(): pl.pallas_call(functools.partial(attend_back_kernel, start), name='attend...]
    pallas_call x1, Pallas kernels: 227 us -> 213 us  [feed(): pl.pallas_call(feed_kernel, name='feed', grid=(parts + FEED_LEAD + 4,), i...]
    ppermute x23 -> x17, waiting for transfers between devices: 57 us -> 43.6 us  [swap(): return lax.ppermute(value, axis, pairs)]
    all_gather x1, waiting for transfers between devices: 0.01 us -> 10.9 us  [gather(): return lax.all_gather(shard, ALL, axis=0, tiled=True)]
    convert_element_type x4 -> x1, other arithmetic: 9.89 us -> 0.75 us  [per_device(): w_down = gather(after(down_master.astype(BF16), others[3]))]
    ppermute x4, waiting for transfers between devices: 35.1 us -> 43.7 us  [per_device(): others = [lax.ppermute(p, 'seq', [(0, 1)]) for p in own]]
    ppermute x23 -> x17, starting transfers between devices: 28.5 us -> 24.6 us  [swap(): return lax.ppermute(value, axis, pairs)]
  transfers between devices with their start and end apart: 32 -> 27, of which waited for: 18 -> 15; matrix products, arithmetic and copies ran while one was open for 11% -> 8% of each run, Pallas kernels for 19% -> 12%
where the time goes in v4:
time: 630 us; the launch traced here: 626 us
  Pallas kernels  343 us (54%)
  waiting for transfers between devices  133 us (21%)
  matrix products  45.2 us (7%)
  starting transfers between devices  42.4 us (7%)
  other arithmetic  33.3 us (5%)
  between operations  15.4 us (2%)
  local copies, waits for them, and re-layouts  13.7 us (2%)
    pallas_call x1, Pallas kernels, feed(): pl.pallas_call(feed_kernel, name='feed', grid=(parts + FEED_LEAD + 4,), i...  213 us
    pallas_call x2, Pallas kernels, attend_back(): pl.pallas_call(functools.partial(attend_back_kernel, start), name='attend...  45.4 us
    pallas_call x1, Pallas kernels, gather_all(): pl.pallas_call(functools.partial(gather_kernel, plan), name='gather_all',...  44.6 us
    ppermute x4, waiting for transfers between devices, per_device(): others = [lax.ppermute(p, 'seq', [(0, 1)]) for p in own]  43.7 us
    ppermute x17, waiting for transfers between devices, swap(): return lax.ppermute(value, axis, pairs)  43.6 us
    ppermute x4, waiting for transfers between devices, per_device(): back = [lax.ppermute(p, 'seq', [(1, 0)]) for p in far]  34.8 us
    ppermute x17, starting transfers between devices, swap(): return lax.ppermute(value, axis, pairs)  24.6 us
    dot_general x5, matrix products, dot_cols(): lax.dot_general(a, b, (((1,), (1,)), ((), ())), preferred_element_type=F32)  19.9 us
  transfers between devices with their start and end apart: 27, of which 15 were waited for; matrix products, arithmetic and copies ran while one was open for 8% of the time, Pallas kernels for 12%

profile of v4, /device:TPU:0, one launch (start us, length us, event | category | flops | bytes accessed | tf_op | source)
XLA Modules:
  0.0 626.4 jit_solution(12619015414064939616)
XLA Ops:
  15.7 44.6 %gather_all.1 = (bf16[4,2,2,2,32,2048]{5,4,3,2,1,0:T(8,128)(2,1)}, bf16[4,2,2,2,32,1024]{5,4,3,2,1,0:T(8,128)(2,1)}) custom-call(bf16[32,2048]{1,0:T(8,128)(2,1)} %convert_element_type.164.refs_0_, bf16[32,1024]{1,0:T(8,128)(2,1)} %convert_element_type.165.refs_1_), custom_call_target="tpu_custom_call" | custom-call | tf_op jit(solution)/shard_map/gather_all/pallas_call | solution.py:561
  60.9 3.8 pad_maximum_fusion.2
  64.7 9.2 %fusion.21.raw_ref = f32[1024,2048]{1,0:T(8,128)} fusion(bf16[1024,2048]{1,0:T(8,128)(2,1)} %bitcast.83, bf16[1,1024,1024]{2,1,0:T(8,128)(2,1)S(1)} %copy-done.5, f32[1024]{0:T(1024)S(1)} %bitcast.76, f32[1024]{0:T(1024)S(1)} %add_rsqrt_fusion.1), kind=kOutput, calls=%fused_computation.33 | convolution fusion | flops 4299161600 | bytes 14688256 | tf_op jit(solution)/shard_map/dot_general | solution.py:959
  73.9 8.3 %prep.1 = (bf16[1024,1024]{1,0:T(8,128)(2,1)}, bf16[1024,256]{1,0:T(8,128)(2,1)}, bf16[1024,256]{1,0:T(8,128)(2,1)}, bf16[1024,256]{1,0:T(8,128)(2,1)}, bf16[1024,256]{1,0:T(8,128)(2,1)}) custom-call(f32[1024,2048]{1,0:T(8,128)} %fusion.21.raw_ref, f32[8,128]{1,0:T(8,128)} %pad.12.gain_ref, f32[1024,128]{1,0:T(8,128)} %get-tuple-element.118.cos_ref, ...), custom_call_target="tpu_custom_call" | custom-call | flops 83886080 | bytes 12582912 | tf_op jit(solution)/shard_map/prep/pallas_call | solution.py:92
  85.6 10.5 %collective-permute-done.3.rest_3_ = bf16[1024,256]{1,0:T(8,128)(2,1)} collective-permute-done((bf16[1024,256]{1,0:T(8,128)(2,1)}, bf16[1024,256]{1,0:T(8,128)(2,1)}, u32[]{:S(2)}, u32[]{:S(2)}) %collective-permute-start.3) | collective-permute-done | bytes 524320 | tf_op jit(solution)/shard_map/ppermute | solution.py:963
  96.2 5.2 collective-permute-start
  107.9 3.8 fusion.33
  115.4 11.3 %collective-permute-done.1.rest_1_ = bf16[1024,256]{1,0:T(8,128)(2,1)} collective-permute-done((bf16[1024,256]{1,0:T(8,128)(2,1)}, bf16[1024,256]{1,0:T(8,128)(2,1)}, u32[]{:S(2)}, u32[]{:S(2)}) %collective-permute-start.1) | collective-permute-done | bytes 524320 | tf_op jit(solution)/shard_map/ppermute | solution.py:963
  126.7 18.2 %collective-permute-done.2.rest_2_ = bf16[1024,256]{1,0:T(8,128)(2,1)} collective-permute-done((bf16[1024,256]{1,0:T(8,128)(2,1)}, bf16[1024,256]{1,0:T(8,128)(2,1)}, u32[]{:S(2)}, u32[]{:S(2)}) %collective-permute-start.2) | collective-permute-done | bytes 524320 | tf_op jit(solution)/shard_map/ppermute | solution.py:963
  145.9 19.3 %attend.1 = (bf16[1024,1024]{1,0:T(8,128)(2,1)}, f32[64,2048]{1,0:T(8,128)}) custom-call(s32[9]{0:T(128)} %pad_add_fusion.1.low_ref, s32[1024,128]{1,0:T(8,128)} %broadcast_in_dim.60.first_ref, bf16[1024,1024]{1,0:T(8,128)(2,1)} %get-tuple-element.49.q_ref, bf16[1024,256]{1,0:T(8,128)(2,1)} %collective-permute-done.rest_0_, ...), custom_call_target="tpu_custom_call" | custom-call | flops 25769803776 | bytes 16777216 | tf_op jit(solution)/shard_map/attend/pallas_call | solution.py:241
  165.1 4.8 multiply_reduce_fusion.2
  172.0 3.7 fusion.32.at_ref
  175.7 3.7 fusion.31
  179.4 10.9 %all-gather.2.cloned.1.call-done.wd_ref = bf16[4608,1024]{1,0:T(8,128)(2,1)} async-done(((bf16[144,1024]{1,0:T(8,128)(2,1)}), bf16[4608,1024]{1,0:T(8,128)(2,1)}) %all-gather.2.cloned.1.call-update) | async-done | bytes 9437200 | tf_op jit(solution)/shard_map/all_gather | solution.py:414
  190.2 213.4 %feed.1 = (bf16[2,4,2,2,2,32,4608]{6,5,4,3,2,1,0:T(8,128)(2,1)}, f32[1024,1024]{1,0:T(8,128)}, f32[1024,1024]{1,0:T(8,128)}, bf16[4608,1024]{1,0:T(8,128)(2,1)}, f32[2,32,4608]{2,1,0:T(8,128)}) custom-call(bf16[2,32,4608]{2,1,0:T(8,128)(2,1)} %pad_maximum_fusion.1.shard_ref, bf16[1024,1024]{1,0:T(8,128)(2,1)} %copy-done.12, ...), custom_call_target="tpu_custom_call" | custom-call | flops 86973087744 | bytes 56623104 | tf_op jit(solution)/shard_map/feed/pallas_call | solution.py:849
  403.6 4.7 multiply_reduce_fusion
  411.1 3.7 convolution_convert_fusion.2.do_ref
  420.1 11.9 %attend_back.2 = (bf16[1024,256]{1,0:T(8,128)(2,1)}, bf16[1024,256]{1,0:T(8,128)(2,1)}, bf16[1024,256]{1,0:T(8,128)(2,1)}, bf16[1024,256]{1,0:T(8,128)(2,1)}, f32[1024,1024]{1,0:T(8,128)}) custom-call(s32[9]{0:T(128)} %pad_add_fusion.1.low_ref, s32[8,1024]{1,0:T(8,128)} %broadcast_in_dim.62.first_ref, bf16[1024,1024]{1,0:T(8,128)(2,1)} %get-tuple-element.49.q_ref, ...), custom_call_target="tpu_custom_call" | custom-call | flops 25769803776 | bytes 31457280 | tf_op jit(solution)/shard_map/attend_back/pallas_call | solution.py:342
  442.0 7.3 %collective-permute-done.5 = bf16[256,1024]{1,0:T(8,128)(2,1)S(1)} collective-permute-done((bf16[256,1024]{1,0:T(8,128)(2,1)S(1)}, bf16[256,1024]{1,0:T(8,128)(2,1)S(1)}, u32[]{:S(2)}, u32[]{:S(2)}) %collective-permute-start.5) | collective-permute-done | bytes 524320 | tf_op jit(solution)/shard_map/ppermute | solution.py:435
  449.4 33.5 %attend_back.3 = (f32[1024,256]{1,0:T(8,128)}, f32[1024,256]{1,0:T(8,128)}, f32[1024,256]{1,0:T(8,128)}, f32[1024,256]{1,0:T(8,128)}, f32[1024,1024]{1,0:T(8,128)}) custom-call(s32[9]{0:T(128)} %pad_add_fusion.1.low_ref, s32[8,1024]{1,0:T(8,128)} %broadcast_in_dim.62.first_ref, bf16[1024,1024]{1,0:T(8,128)(2,1)} %get-tuple-element.49.q_ref, ...), custom_call_target="tpu_custom_call" | custom-call | flops 25769803776 | bytes 31457280 | tf_op jit(solution)/shard_map/attend_back/pallas_call | solution.py:342
  483.0 5.9 collective-permute-done.7.rest_6_
  488.9 18.2 %collective-permute-done.8.rest_7_ = bf16[1024,256]{1,0:T(8,128)(2,1)S(1)} collective-permute-done((bf16[1024,256]{1,0:T(8,128)(2,1)}, bf16[1024,256]{1,0:T(8,128)(2,1)S(1)}, u32[]{:S(2)}, u32[]{:S(2)}) %collective-permute-start.8) | collective-permute-done | bytes 524320 | tf_op jit(solution)/shard_map/ppermute | solution.py:998
  507.1 10.7 %collective-permute-done.9.rest_8_ = bf16[1024,256]{1,0:T(8,128)(2,1)S(1)} collective-permute-done((bf16[1024,256]{1,0:T(8,128)(2,1)}, bf16[1024,256]{1,0:T(8,128)(2,1)S(1)}, u32[]{:S(2)}, u32[]{:S(2)}) %collective-permute-start.9) | collective-permute-done | bytes 524320 | tf_op jit(solution)/shard_map/ppermute | solution.py:998
  518.7 12.5 %prep_back.1 = (bf16[1024,2048]{1,0:T(8,128)(2,1)}, f32[8,128]{1,0:T(8,128)}) custom-call(f32[1024,2048]{1,0:T(8,128)} %fusion.21.raw_ref, f32[8,128]{1,0:T(8,128)} %pad.12.gain_ref, f32[1024,128]{1,0:T(8,128)} %get-tuple-element.118.cos_ref, f32[1024,128]{1,0:T(8,128)} %get-tuple-element.119.sin_ref, f32[1024,1024]{1,0:T(8,128)} %get-tuple-element.63.rest_0_, ...), custom_call_target="tpu_custom_call" | custom-call | flops 125829120 | bytes 20971520 | tf_op jit(solution)/shard_map/prep_back/pallas_call | solution.py:144
  531.2 5.0 convolution_convert_fusion
  537.0 4.9 fusion.12
  546.0 7.6 %collective-permute-start.11 = (f32[8,1024]{1,0:T(8,128)S(1)}, f32[8,1024]{1,0:T(8,128)S(1)}, u32[]{:S(2)}, u32[]{:S(2)}) collective-permute-start(f32[8,1024]{1,0:T(8,128)S(1)} %pad_add_fusion), channel_id=1, source_target_pairs={{0,16},{2,18},{4,20},{6,22},{8,24},{10,26},{12,28},{14,30},{16,0},... | collective-permute-start | bytes 98312 | tf_op jit(solution)/shard_map/ppermute | solution.py:435
  568.6 20.3 %collective-permute-done.14 = f32[8,1024]{1,0:T(8,128)S(1)} collective-permute-done((f32[8,1024]{1,0:T(8,128)S(1)}, f32[8,1024]{1,0:T(8,128)S(1)}, u32[]{:S(2)}, u32[]{:S(2)}) %collective-permute-start.14) | collective-permute-done | bytes 32800 | tf_op jit(solution)/shard_map/ppermute | solution.py:435
  592.7 3.7 collective-permute-start.23
  597.1 4.8 collective-permute-done.17
  603.6 3.8 collective-permute-start.19
  608.3 7.2 %collective-permute-done.19 = bf16[32,2048]{1,0:T(8,128)(2,1)S(1)} collective-permute-done((bf16[32,2048]{1,0:T(8,128)(2,1)S(1)}, bf16[32,2048]{1,0:T(8,128)(2,1)S(1)}, u32[]{:S(2)}, u32[]{:S(2)}) %collective-permute-start.19) | collective-permute-done | bytes 131104 | tf_op jit(solution)/shard_map/ppermute | solution.py:435
  (206 shorter events, 74.6 us)
Async XLA Ops:
  7.2 183.0 %all-gather.2.cloned.1.call-start = ((), (), s32[]{:S(2)}) async-start(), calls=%async_computation.1 | async-start | bytes 9732096 | tf_op jit(solution)/shard_map/all_gather | solution.py:414
  9.0 98.8 %copy-start.36 = (f32[1,1024]{1,0:T(1,128)}, f32[1,1024]{1,0:T(1,128)S(1)}, u32[]{:S(2)}) copy-start(f32[1,1024]{1,0:T(1,128)S(1)} %get-tuple-element.109) | copy-start | bytes 12292
  11.1 96.7 %copy-start.34 = (f32[1024]{0:T(1024)}, f32[1024]{0:T(1024)S(1)}, u32[]{:S(2)}) copy-start(f32[1024]{0:T(1024)S(1)} %add_rsqrt_fusion.1) | copy-start | bytes 12292
  12.7 132.2 %copy-start.31 = (s32[1024]{0:T(1024)}, s32[1024]{0:T(1024)S(1)}, u32[]{:S(2)}) copy-start(s32[1024]{0:T(1024)S(1)} %get-tuple-element.114) | copy-start | bytes 12292
  12.7 52.0 %copy-start.5 = (bf16[1,1024,1024]{2,1,0:T(8,128)(2,1)S(1)}, bf16[1,1024,1024]{2,1,0:T(8,128)(2,1)}, u32[]{:S(2)}) copy-start(bf16[1,1024,1024]{2,1,0:T(8,128)(2,1)} %param.21) | copy-start | bytes 6291460
  82.2 13.9 %collective-permute-start.3 = (bf16[1024,256]{1,0:T(8,128)(2,1)}, bf16[1024,256]{1,0:T(8,128)(2,1)}, u32[]{:S(2)}, u32[]{:S(2)}) collective-permute-start(bf16[1024,256]{1,0:T(8,128)(2,1)} %get-tuple-element.53.rest_7_.rest_3_), channel_id=1, source_target_pairs={{0,1},{2,3},{4,5},{6,7},{8,9},{10,11},{12,13},{14,15},{16,17},{18,... | collective-permute-start | bytes 1572872 | tf_op jit(solution)/shard_map/ppermute | solution.py:963
  96.2 520.4 %reduce-scatter.2.cloned.1.call-start = ((), (), s32[]{:S(2)}) async-start(), calls=%async_computation.2 | async-start | bytes 9732096 | tf_op jit(solution)/shard_map/reduce_scatter | solution.py:984
  96.2 19.2 %collective-permute-start = (bf16[1024,256]{1,0:T(8,128)(2,1)}, bf16[1024,256]{1,0:T(8,128)(2,1)}, u32[]{:S(2)}, u32[]{:S(2)}) collective-permute-start(bf16[1024,256]{1,0:T(8,128)(2,1)} %get-tuple-element.50.rest_4_.rest_0_), channel_id=1, source_target_pairs={{0,1},{2,3},{4,5},{6,7},{8,9},{10,11},{12,13},{14,15},{16,17},{18,... | collective-permute-start | bytes 1572872 | tf_op jit(solution)/shard_map/ppermute | solution.py:963
  101.4 25.3 %collective-permute-start.1 = (bf16[1024,256]{1,0:T(8,128)(2,1)}, bf16[1024,256]{1,0:T(8,128)(2,1)}, u32[]{:S(2)}, u32[]{:S(2)}) collective-permute-start(bf16[1024,256]{1,0:T(8,128)(2,1)} %get-tuple-element.51.rest_5_.rest_1_), channel_id=1, source_target_pairs={{0,1},{2,3},{4,5},{6,7},{8,9},{10,11},{12,13},{14,15},{16,17},{18,... | collective-permute-start | bytes 1572872 | tf_op jit(solution)/shard_map/ppermute | solution.py:963
  103.5 41.4 %collective-permute-start.2 = (bf16[1024,256]{1,0:T(8,128)(2,1)}, bf16[1024,256]{1,0:T(8,128)(2,1)}, u32[]{:S(2)}, u32[]{:S(2)}) collective-permute-start(bf16[1024,256]{1,0:T(8,128)(2,1)} %get-tuple-element.52.rest_6_.rest_2_), channel_id=1, source_target_pairs={{0,1},{2,3},{4,5},{6,7},{8,9},{10,11},{12,13},{14,15},{16,17},{18,... | collective-permute-start | bytes 1572872 | tf_op jit(solution)/shard_map/ppermute | solution.py:963
  190.2 218.1 %copy-start.13 = (bf16[1,1024,1024]{2,1,0:T(8,128)(2,1)S(1)}, bf16[1,1024,1024]{2,1,0:T(8,128)(2,1)}, u32[]{:S(2)}) copy-start(bf16[1,1024,1024]{2,1,0:T(8,128)(2,1)} %param.22) | copy-start | bytes 6291460
  416.2 15.8 %collective-permute-start.4 = (bf16[512,1024]{1,0:T(8,128)(2,1)S(1)}, bf16[512,1024]{1,0:T(8,128)(2,1)S(1)}, u32[]{:S(2)}, u32[]{:S(2)}) collective-permute-start(bf16[512,1024]{1,0:T(8,128)(2,1)S(1)} %convolution_convert_fusion.3), channel_id=1, source_target_pairs={{0,2},{2,0},{4,6},{6,4},{8,10},{10,8},{12,14},{14,12},{16,18},{18,... | collective-permute-start | bytes 3145736 | tf_op jit(solution)/shard_map/ppermute | solution.py:435
  434.7 14.5 %collective-permute-start.5 = (bf16[256,1024]{1,0:T(8,128)(2,1)S(1)}, bf16[256,1024]{1,0:T(8,128)(2,1)S(1)}, u32[]{:S(2)}, u32[]{:S(2)}) collective-permute-start(bf16[256,1024]{1,0:T(8,128)(2,1)S(1)} %slice.133), channel_id=1, source_target_pairs={{0,4},{2,6},{4,0},{6,2},{8,12},{10,14},{12,8},{14,10},{16,20},{18,... | collective-permute-start | bytes 1572872 | tf_op jit(solution)/shard_map/ppermute | solution.py:435
  436.8 46.2 %collective-permute-start.6 = (bf16[1024,256]{1,0:T(8,128)(2,1)}, bf16[1024,256]{1,0:T(8,128)(2,1)S(1)}, u32[]{:S(2)}, u32[]{:S(2)}) collective-permute-start(bf16[1024,256]{1,0:T(8,128)(2,1)} %get-tuple-element.68), channel_id=1, source_target_pairs={{1,0},{3,2},{5,4},{7,6},{9,8},{11,10},{13,12},{15,14},{17,16},{19,... | collective-permute-start | bytes 1572872 | tf_op jit(solution)/shard_map/ppermute | solution.py:998
  438.1 50.8 %collective-permute-start.7 = (bf16[1024,256]{1,0:T(8,128)(2,1)}, bf16[1024,256]{1,0:T(8,128)(2,1)S(1)}, u32[]{:S(2)}, u32[]{:S(2)}) collective-permute-start(bf16[1024,256]{1,0:T(8,128)(2,1)} %get-tuple-element.69), channel_id=1, source_target_pairs={{1,0},{3,2},{5,4},{7,6},{9,8},{11,10},{13,12},{15,14},{17,16},{19,... | collective-permute-start | bytes 1572872 | tf_op jit(solution)/shard_map/ppermute | solution.py:998
  439.4 67.8 %collective-permute-start.8 = (bf16[1024,256]{1,0:T(8,128)(2,1)}, bf16[1024,256]{1,0:T(8,128)(2,1)S(1)}, u32[]{:S(2)}, u32[]{:S(2)}) collective-permute-start(bf16[1024,256]{1,0:T(8,128)(2,1)} %get-tuple-element.70), channel_id=1, source_target_pairs={{1,0},{3,2},{5,4},{7,6},{9,8},{11,10},{13,12},{15,14},{17,16},{19,... | collective-permute-start | bytes 1572872 | tf_op jit(solution)/shard_map/ppermute | solution.py:998
  440.7 77.1 %collective-permute-start.9 = (bf16[1024,256]{1,0:T(8,128)(2,1)}, bf16[1024,256]{1,0:T(8,128)(2,1)S(1)}, u32[]{:S(2)}, u32[]{:S(2)}) collective-permute-start(bf16[1024,256]{1,0:T(8,128)(2,1)} %get-tuple-element.71), channel_id=1, source_target_pairs={{1,0},{3,2},{5,4},{7,6},{9,8},{11,10},{13,12},{15,14},{17,16},{19,... | collective-permute-start | bytes 1572872 | tf_op jit(solution)/shard_map/ppermute | solution.py:998
  536.2 22.1 %collective-permute-start.15 = (bf16[512,2048]{1,0:T(8,128)(2,1)S(1)}, bf16[512,2048]{1,0:T(8,128)(2,1)S(1)}, u32[]{:S(2)}, u32[]{:S(2)}) collective-permute-start(bf16[512,2048]{1,0:T(8,128)(2,1)S(1)} %convolution_convert_fusion), channel_id=1, source_target_pairs={{0,2},{2,0},{4,6},{6,4},{8,10},{10,8},{12,14},{14,12},{16,18},{18,... | collective-permute-start | bytes 6291464 | tf_op jit(solution)/shard_map/ppermute | solution.py:435
  542.0 4.0 collective-permute-start.10
  546.0 11.4 %collective-permute-start.11 = (f32[8,1024]{1,0:T(8,128)S(1)}, f32[8,1024]{1,0:T(8,128)S(1)}, u32[]{:S(2)}, u32[]{:S(2)}) collective-permute-start(f32[8,1024]{1,0:T(8,128)S(1)} %pad_add_fusion), channel_id=1, source_target_pairs={{0,16},{2,18},{4,20},{6,22},{8,24},{10,26},{12,28},{14,30},{16,0},... | collective-permute-start | bytes 98312 | tf_op jit(solution)/shard_map/ppermute | solution.py:435
  557.4 5.7 collective-permute-start.12
  559.2 30.3 %collective-permute-start.16 = (bf16[256,2048]{1,0:T(8,128)(2,1)S(1)}, bf16[256,2048]{1,0:T(8,128)(2,1)S(1)}, u32[]{:S(2)}, u32[]{:S(2)}) collective-permute-start(bf16[256,2048]{1,0:T(8,128)(2,1)S(1)} %slice.140), channel_id=1, source_target_pairs={{0,1},{1,0},{2,3},{3,2},{4,5},{5,4},{6,7},{7,6},{8,9},{9,8},{10,11... | collective-permute-start | bytes 3145736 | tf_op jit(solution)/shard_map/ppermute | solution.py:435
  562.2 30.3 %collective-permute-start.21 = (bf16[128,1024]{1,0:T(8,128)(2,1)S(1)}, bf16[128,1024]{1,0:T(8,128)(2,1)S(1)}, u32[]{:S(2)}, u32[]{:S(2)}) collective-permute-start(bf16[128,1024]{1,0:T(8,128)(2,1)S(1)} %slice.148), channel_id=1, source_target_pairs={{0,1},{1,0},{2,3},{3,2},{4,5},{5,4},{6,7},{7,6},{8,9},{9,8},{10,11... | collective-permute-start | bytes 786440 | tf_op jit(solution)/shard_map/ppermute | solution.py:435
  563.1 1.3 collective-permute-start.13
  564.4 24.5 %collective-permute-start.14 = (f32[8,1024]{1,0:T(8,128)S(1)}, f32[8,1024]{1,0:T(8,128)S(1)}, u32[]{:S(2)}, u32[]{:S(2)}) collective-permute-start(f32[8,1024]{1,0:T(8,128)S(1)} %add.377), channel_id=1, source_target_pairs={{0,1},{1,0},{2,3},{3,2},{4,5},{5,4},{6,7},{7,6},{8,9},{9,8},{10,11... | collective-permute-start | bytes 98312 | tf_op jit(solution)/shard_map/ppermute | solution.py:435
  590.0 11.8 %collective-permute-start.17 = (bf16[128,2048]{1,0:T(8,128)(2,1)S(1)}, bf16[128,2048]{1,0:T(8,128)(2,1)S(1)}, u32[]{:S(2)}, u32[]{:S(2)}) collective-permute-start(bf16[128,2048]{1,0:T(8,128)(2,1)S(1)} %slice.142), channel_id=1, source_target_pairs={{0,4},{2,6},{4,0},{6,2},{8,12},{10,14},{12,8},{14,10},{16,20},{18,... | collective-permute-start | bytes 1572872 | tf_op jit(solution)/shard_map/ppermute | solution.py:435
  592.6 14.8 %collective-permute-start.22 = (bf16[32,1024]{1,0:T(8,128)(2,1)S(1)}, bf16[32,1024]{1,0:T(8,128)(2,1)S(1)}, u32[]{:S(2)}, u32[]{:S(2)}) collective-permute-start(bf16[32,1024]{1,0:T(8,128)(2,1)S(1)} %get-tuple-element.105), channel_id=1, source_target_pairs={{0,8},{2,10},{4,12},{6,14},{8,0},{10,2},{12,4},{14,6},{16,24},{18,... | collective-permute-start | bytes 196616 | tf_op jit(solution)/shard_map/ppermute | solution.py:435
  592.7 14.7 %collective-permute-start.23 = (bf16[32,1024]{1,0:T(8,128)(2,1)S(1)}, bf16[32,1024]{1,0:T(8,128)(2,1)S(1)}, u32[]{:S(2)}, u32[]{:S(2)}) collective-permute-start(bf16[32,1024]{1,0:T(8,128)(2,1)S(1)} %get-tuple-element.107), channel_id=1, source_target_pairs={{0,16},{2,18},{4,20},{6,22},{8,24},{10,26},{12,28},{14,30},{16,0},... | collective-permute-start | bytes 196616 | tf_op jit(solution)/shard_map/ppermute | solution.py:435
  596.4 11.0 %collective-permute-start.24 = (bf16[32,1024]{1,0:T(8,128)(2,1)S(1)}, bf16[32,1024]{1,0:T(8,128)(2,1)S(1)}, u32[]{:S(2)}, u32[]{:S(2)}) collective-permute-start(bf16[32,1024]{1,0:T(8,128)(2,1)S(1)} %get-tuple-element.106), channel_id=1, source_target_pairs={{0,24},{2,26},{4,28},{6,30},{8,16},{10,18},{12,20},{14,22},{16,8},... | collective-permute-start | bytes 196616 | tf_op jit(solution)/shard_map/ppermute | solution.py:435
  602.1 6.2 collective-permute-start.18
  603.6 11.9 %collective-permute-start.19 = (bf16[32,2048]{1,0:T(8,128)(2,1)S(1)}, bf16[32,2048]{1,0:T(8,128)(2,1)S(1)}, u32[]{:S(2)}, u32[]{:S(2)}) collective-permute-start(bf16[32,2048]{1,0:T(8,128)(2,1)S(1)} %get-tuple-element.104), channel_id=1, source_target_pairs={{0,16},{2,18},{4,20},{6,22},{8,24},{10,26},{12,28},{14,30},{16,0},... | collective-permute-start | bytes 393224 | tf_op jit(solution)/shard_map/ppermute | solution.py:435
  607.4 8.0 %collective-permute-start.20 = (bf16[32,2048]{1,0:T(8,128)(2,1)S(1)}, bf16[32,2048]{1,0:T(8,128)(2,1)S(1)}, u32[]{:S(2)}, u32[]{:S(2)}) collective-permute-start(bf16[32,2048]{1,0:T(8,128)(2,1)S(1)} %get-tuple-element.103), channel_id=1, source_target_pairs={{0,24},{2,26},{4,28},{6,30},{8,16},{10,18},{12,20},{14,22},{16,8},... | collective-permute-start | bytes 393224 | tf_op jit(solution)/shard_map/ppermute | solution.py:435
  (46 other events, 483.5 us)
Sparse Core Ops, SparseCore 0:
  96.3 93.9 all-gather.1
  416.4 144.1 reduce-scatter.1

commit v5 on v4

--- a/solution.py
+++ b/solution.py
@@ -102,67 +102,6 @@
             flops=rows * 2048 * 40, transcendentals=rows * 24, bytes_accessed=rows * 2048 * 6
         ),
     )(raw, gains, cosine, sine)
-
-
-def prep_back_kernel(raw_ref, gain_ref, cos_ref, sin_ref, *rest):
-    dq_ref, own_refs, back_refs = rest[0], rest[1 : PIECES + 1], rest[PIECES + 1 : 2 * PIECES + 1]
-    out_ref, dg_ref = rest[2 * PIECES + 1 :]
-    cosine, sine = cos_ref[...], sin_ref[...]
-    sums = [jnp.zeros((1, LANES), F32), jnp.zeros((1, LANES), F32)]
-    for group in range(12):
-        part = slice(group * LANES, (group + 1) * LANES)
-        u = raw_ref[:, part]
-        which = 0 if group < 8 else 1
-        gain = gain_ref[which : which + 1]
-        if group < 8:
-            d = dq_ref[:, part] * HEAD_SIZE**-0.5
-        else:
-            own, back = own_refs[group - 8], back_refs[group - 8]
-            d = own[:, :LANES] + back[:, :LANES].astype(F32)
-            value = slice((group + 4) * LANES, (group + 5) * LANES)
-            out_ref[:, value] = (own[:, LANES:] + back[:, LANES:].astype(F32)).astype(BF16)
-        d = d * cosine - swap_halves(d) * sine
-        r = lax.rsqrt(head_mean(u * u) + NORM_EPS)
-        w = d * gain
-        n = u * r
-        out_ref[:, part] = (r * (w - n * head_mean(w * n))).astype(BF16)
-        sums[which] += jnp.sum(d * n, axis=0, keepdims=True)
-
-    @pl.when(pl.program_id(0) == 0)
-    def _():
-        dg_ref[...] = jnp.zeros_like(dg_ref)
-
-    dg_ref[0:1] += sums[0]
-    dg_ref[1:2] += sums[1]
-
-
-def prep_back(raw, gains, cosine, sine, dq, own, back):
-    rows = raw.shape[0]
-    block = min(rows, 256)
-    whole = lambda width: pl.BlockSpec((block, width), lambda i: (i, 0))
-    small = pl.BlockSpec((8, LANES), lambda i: (0, 0))
-    return pl.pallas_call(
-        prep_back_kernel,
-        name="prep_back",
-        grid=(rows // block,),
-        in_specs=[
-            whole(2048),
-            small,
-            whole(LANES),
-            whole(LANES),
-            whole(QUERY_FEATURES),
-        ]
-        + [whole(2 * LANES)] * (2 * PIECES),
-        out_specs=[whole(2048), small],
-        out_shape=[
-            jax.ShapeDtypeStruct((rows, 2048), BF16),
-            jax.ShapeDtypeStruct((8, LANES), F32),
-        ],
-        compiler_params=params(),
-        cost_estimate=pl.CostEstimate(
-            flops=rows * 2048 * 60, transcendentals=rows * 24, bytes_accessed=rows * 2048 * 10
-        ),
-    )(raw, gains, cosine, sine, dq, *own, *back)
 
 
 def stack_heads(rows):
@@ -265,8 +204,8 @@
 
 
 def attend_back_kernel(start, low_ref, first_ref, q_ref, do_ref, mixed_ref, lse_ref, before_ref, *rest):
-    refs, d_refs = rest[:PIECES], rest[PIECES : 2 * PIECES]
-    dq_ref, queries, rising, deltas, dqs, dkvs = rest[2 * PIECES :]
+    refs = rest[:PIECES]
+    d_ref, dq_ref, queries, rising, deltas, dqs, dkvs = rest[PIECES:]
     turn = pl.program_id(0)
     block = q_ref.shape[0]
     rows = refs[0].shape[0]
@@ -329,7 +268,9 @@
     @pl.when(turn == pl.num_programs(0) - 1)
     def _():
         for p in range(PIECES):
-            d_refs[p][...] = dkvs[p].astype(d_refs[p].dtype)
+            for half in range(2):
+                part = slice(half * KEY_FEATURES + p * LANES, half * KEY_FEATURES + (p + 1) * LANES)
+                d_ref[:, part] = dkvs[p, :, half * LANES : (half + 1) * LANES].astype(d_ref.dtype)
 
 
 def attend_back(start, q, d_mixed, mixed, lse, before, source, low, first_lane, kind):
@@ -337,9 +278,9 @@
     block = QUERY_BLOCK
     turns = rows // block
     count = source[0].shape[0]
-    whole = pl.BlockSpec((count, 2 * LANES), lambda t, low: (0, 0))
+    whole = pl.BlockSpec((count, 2 * KEY_FEATURES), lambda t, low: (0, 0))
     wide = pl.BlockSpec((block, QUERY_FEATURES), lambda t, low: (t, 0))
-    *pieces, dq = pl.pallas_call(
+    d_keys, dq = pl.pallas_call(
         functools.partial(attend_back_kernel, start),
         name="attend_back",
         grid_spec=pltpu.PrefetchScalarGridSpec(
@@ -353,8 +294,8 @@
                 pl.BlockSpec((8, HQ * block), lambda t, low: (t, 0)),
                 wide,
             ]
-            + [whole] * PIECES,
-            out_specs=[whole] * PIECES + [wide],
+            + [pl.BlockSpec((count, 2 * LANES), lambda t, low: (0, 0))] * PIECES,
+            out_specs=[whole, wide],
             scratch_shapes=[
                 pltpu.VMEM((PIECES, 4 * block, LANES), BF16),
                 pltpu.VMEM((PIECES, 4 * block, LANES), BF16),
@@ -363,14 +304,16 @@
                 pltpu.VMEM((PIECES, count, 2 * LANES), F32),
             ],
         ),
-        out_shape=[jax.ShapeDtypeStruct((count, 2 * LANES), kind)] * PIECES
-        + [jax.ShapeDtypeStruct((rows, QUERY_FEATURES), F32)],
+        out_shape=[
+            jax.ShapeDtypeStruct((count, 2 * KEY_FEATURES), kind),
+            jax.ShapeDtypeStruct((rows, QUERY_FEATURES), F32),
+        ],
         compiler_params=params(),
         cost_estimate=pl.CostEstimate(
-            flops=rows * 1024 * 1024 * 24, transcendentals=rows * 1024 * 16, bytes_accessed=30 << 20
+            flops=rows << 18, transcendentals=0, bytes_accessed=rows << 8
         ),
     )(low, first_lane, q, d_mixed, mixed, lse, before, *source)
-    return dq, pieces
+    return dq, d_keys
 
 
 def rms_scale(v):
@@ -581,15 +524,6 @@
     return lax.optimization_barrier((values, earlier))[0]
 
 
-def sum_everywhere(terms):
-    for k, (_, _, size) in dims().items():
-        d = 1
-        while d < size:
-            terms = terms + swap(terms, k, d)
-            d *= 2
-    return terms
-
-
 FIRST_PARTS = 3
 FEED_LEAD = 4
 
@@ -757,7 +691,8 @@
         total = total_3[:, 0].astype(F32)
         for d in range(1, size["z"]):
             total = total + got_z[p, d - 1].astype(F32)
-        sum_ref[:, :, columns(p)] = total
+        for which in range(2):
+            sum_ref[:, pl.ds(pl.multiple_of(which * parts * width + p * width, width), width)] = total[which]
 
     def third(p):
         for copy in scatter_copies(p, 2):
@@ -857,7 +792,7 @@
             jax.ShapeDtypeStruct((rows, D), F32),
             jax.ShapeDtypeStruct((rows, D), F32),
             jax.ShapeDtypeStruct((width, D), BF16),
-            jax.ShapeDtypeStruct((2, shard_rows, width), F32),
+            jax.ShapeDtypeStruct((shard_rows, 2 * width), F32),
         ],
         scratch_shapes=[
             pltpu.VMEM((2, 2, *(size[k] for k in NAMES), shard_rows, FF_BLOCK), BF16),
@@ -885,6 +820,307 @@
         ),
     )(shards, a, at, g, start, w_down)
     return y_sum, b_sum, grad_down, sums
+
+
+OUT_PARTS = 2
+EXIT_PARTS = OUT_PARTS + 4
+
+
+def exit_kernel(
+    raw_ref,
+    dq_ref,
+    near_ref,
+    back_ref,
+    w_ref,
+    attn_ref,
+    mixed_ref,
+    at_ref,
+    gain_ref,
+    cos_ref,
+    sin_ref,
+    x_ref,
+    norm_ref,
+    second_ref,
+    grad_ref,
+    sum_ref,
+    gains_ref,
+    part_ref,
+    first_ref,
+    head_ref,
+    terms,
+    total_1,
+    total_2,
+    total_3,
+    got_c,
+    got_1,
+    got_2,
+    got_z,
+    gains_got,
+    in_send,
+    in_recv,
+    gain_send,
+    gain_recv,
+):
+    step = pl.program_id(0)
+    width = terms.shape[-1]
+    parts = EXIT_PARTS
+    size = {k: v[2] for k, v in dims().items()}
+    here = {k: place_along(k) for k in NAMES}
+    orders = ("xy", "yx")
+    rows = x_ref.shape[0]
+
+    def columns(p):
+        return pl.ds(pl.multiple_of(p * width, width), width)
+
+    def remote(source, target, p, n, k, d):
+        return pltpu.make_async_remote_copy(
+            source,
+            target,
+            in_send.at[p, n],
+            in_recv.at[p, n],
+            device_id=neighbour(k, d),
+            device_id_type=MESH,
+        )
+
+    def scatter_copies(p, stage):
+        if stage == 0:
+            return [remote(terms.at[lax.rem(p, 2), :, 1], got_c.at[p], p, 0, "c", 1)]
+        copies = []
+        slot = 1
+        for which, order in enumerate(orders):
+            for s in (1, 2):
+                k = order[s - 1]
+                for d in range(1, size[k]):
+                    if s == 1:
+                        source = total_1.at[0, d] if k == "x" else total_1.at[1, :, d]
+                    else:
+                        source = total_2[which].at[d]
+                    if s == stage:
+                        target = (got_1, got_2)[s - 1][which].at[p, d - 1]
+                        copies.append(remote(source, target, p, slot, k, d))
+                    slot += 1
+        if stage == 3:
+            for d in range(1, size["z"]):
+                copies.append(remote(total_3.at[:, d], got_z.at[p, d - 1], p, slot + d - 1, "z", d))
+        return copies
+
+    def on(offset, run):
+        p = step - offset
+
+        @pl.when((p >= 0) & (p < parts))
+        def _():
+            run(p)
+
+    def finish(p):
+        for copy in scatter_copies(p, 3):
+            copy.wait()
+        total = total_3[:, 0].astype(F32)
+        for d in range(1, size["z"]):
+            total = total + got_z[p, d - 1].astype(F32)
+        for which in range(2):
+            sum_ref[:, pl.ds(pl.multiple_of((2 * p + which) * width, width), width)] = total[which]
+
+    def third(p):
+        for copy in scatter_copies(p, 2):
+            copy.wait()
+        for which, order in enumerate(orders):
+            total = total_2[which][0].astype(F32)
+            for d in range(1, size[order[1]]):
+                total = total + got_2[which][p, d - 1].astype(F32)
+            total_3[which] = total.astype(BF16)
+        for copy in scatter_copies(p, 3):
+            copy.start()
+
+    def second(p):
+        for copy in scatter_copies(p, 1):
+            copy.wait()
+        for which, order in enumerate(orders):
+            kept = total_1[0, 0] if order[0] == "x" else total_1[1, :, 0]
+            total = kept.astype(F32)
+            for d in range(1, size[order[0]]):
+                total = total + got_1[which][p, d - 1].astype(F32)
+            total_2[which][...] = total.astype(BF16)
+        for copy in scatter_copies(p, 2):
+            copy.start()
+
+    def first(p):
+        for copy in scatter_copies(p, 0):
+            copy.wait()
+        total = terms[lax.rem(p, 2), :, 0].astype(F32) + got_c[p].astype(F32)
+        total_1[...] = total.astype(BF16)
+        for copy in scatter_copies(p, 1):
+            copy.start()
+
+    @pl.when(step == 0)
+    def _():
+        greet()
+        first_ref[...] = jnp.zeros_like(first_ref)
+        head_ref[...] = jnp.zeros_like(head_ref)
+
+    on(4, finish)
+    on(3, third)
+    on(2, second)
+    on(1, first)
+
+    block = 256
+
+    def turn_back(which, scale):
+        def some(i, sums):
+            at = pl.ds(pl.multiple_of(i * block, block), block)
+            cosine, sine = cos_ref[at, :], sin_ref[at, :]
+            for j in range(4):
+                part = slice(j * LANES, (j + 1) * LANES)
+                u = raw_ref[at, part]
+                if which == 0:
+                    d = dq_ref[at, part]
+                else:
+                    d = near_ref[at, part] + back_ref[at, part].astype(F32)
+                d = (d * cosine - swap_halves(d) * sine) * scale
+                r = lax.rsqrt(head_mean(u * u) + NORM_EPS)
+                w = d * gain_ref[which : which + 1]
+                n = u * r
+                part_ref[at, part] = (r * (w - n * head_mean(w * n))).astype(BF16)
+                sums = sums + jnp.sum(d * n, axis=0, keepdims=True)
+            return sums
+
+        sums = lax.fori_loop(0, rows // block, some, jnp.zeros((1, LANES), F32))
+        head_ref[which : which + 1] += sums
+
+    @pl.when((step >= OUT_PARTS) & (step < OUT_PARTS + 2))
+    def _():
+        turn_back(0, HEAD_SIZE**-0.5)
+
+    @pl.when(step == OUT_PARTS + 2)
+    def _():
+        turn_back(1, 1.0)
+
+    @pl.when(step == OUT_PARTS + 3)
+    def _():
+        part_ref[...] = (near_ref[...] + back_ref[...].astype(F32)).astype(BF16)
+
+    def compute(p):
+        shape = (2,) + total_1.shape[1:]
+        slot = lax.rem(p, 2)
+
+        @pl.when(p < OUT_PARTS)
+        def _():
+            for half in range(2):
+                some = attn_ref[:, half * width : (half + 1) * width]
+                terms[slot, half] = dot(mixed_ref[...], some).astype(BF16).reshape(shape)
+
+        @pl.when(p >= OUT_PARTS)
+        def _():
+            first_ref[...] += dot_cols(part_ref[...], w_ref[...])
+            for half in range(2):
+                some = part_ref[:, half * width : (half + 1) * width]
+                terms[slot, half] = dot(at_ref[...], some).astype(BF16).reshape(shape)
+
+        for copy in scatter_copies(p, 0):
+            copy.start()
+
+    on(0, compute)
+
+    @pl.when(step == parts - 1)
+    def _():
+        gain = norm_ref[0:1]
+
+        def some(i, sums):
+            at = pl.ds(pl.multiple_of(i * block, block), block)
+            v = x_ref[at, :].astype(F32)
+            scale = lax.rsqrt(jnp.mean(v * v, axis=-1, keepdims=True) + NORM_EPS)
+            d = first_ref[at, :]
+            n = v * scale
+            w = d * gain
+            mean = jnp.mean(w * n, axis=-1, keepdims=True)
+            grad_ref[at, :] = (scale * (w - n * mean)).astype(BF16)
+            return sums + jnp.sum(d * n, axis=0, keepdims=True)
+
+        sums = lax.fori_loop(0, rows // block, some, jnp.zeros((1, D), F32))
+        gains_ref[...] = jnp.zeros_like(gains_ref)
+        gains_ref[0:1] = sums
+        gains_ref[1:2] = second_ref[0:1]
+        gains_ref[2:4, :LANES] = head_ref[0:2]
+
+    stage = 0
+    for k in NAMES:
+        d = 1
+        while d < size[k]:
+
+            @pl.when(step == parts + stage // 2)
+            def _(k=k, d=d, stage=stage):
+                copy = pltpu.make_async_remote_copy(
+                    gains_ref,
+                    gains_got.at[stage],
+                    gain_send.at[stage],
+                    gain_recv.at[stage],
+                    device_id=neighbour(k, d),
+                    device_id_type=MESH,
+                )
+                copy.start()
+                copy.wait()
+                gains_ref[...] += gains_got[stage]
+
+            d *= 2
+            stage += 1
+
+
+def leave(raw, dq, near, back, w, d_attn, mixed_rows, at, gains, cosine, sine, x, norm_gains, second, number):
+    rows = x.shape[0]
+    size = {k: v[2] for k, v in dims().items()}
+    xs, ys, zs = size["x"], size["y"], size["z"]
+    width = 256
+    shard_rows = D // math.prod(size.values())
+    last = (zs, shard_rows, width)
+    parts = EXIT_PARTS
+    whole = pl.BlockSpec(memory_space=pltpu.VMEM)
+    block = lambda size, start, count: pl.BlockSpec(
+        (size, 2 * width), lambda t: (0, jnp.clip(t - start, 0, count - 1))
+    )
+    in_count = 1 + 2 * (xs + ys - 2) + zs - 1
+    stages = sum(v.bit_length() - 1 for v in size.values())
+    sems = pltpu.SemaphoreType.DMA
+    return pl.pallas_call(
+        exit_kernel,
+        name="leave",
+        grid=(parts + 4,),
+        in_specs=[
+            block(rows, OUT_PARTS, 4),
+            block(rows, OUT_PARTS, 2),
+            block(rows, OUT_PARTS + 2, 2),
+            block(rows, OUT_PARTS + 2, 2),
+            block(D, OUT_PARTS, 4),
+            block(rows, 0, 2),
+        ]
+        + [whole] * 8,
+        out_specs=[whole] * 3,
+        out_shape=[
+            jax.ShapeDtypeStruct((rows, D), BF16),
+            jax.ShapeDtypeStruct((shard_rows, 2 * parts * width), F32),
+            jax.ShapeDtypeStruct((8, D), F32),
+        ],
+        scratch_shapes=[
+            pltpu.VMEM((rows, 2 * width), BF16),
+            pltpu.VMEM((rows, D), F32),
+            pltpu.VMEM((8, LANES), F32),
+            pltpu.VMEM((2, 2, 2, xs, ys, *last), BF16),
+            pltpu.VMEM((2, xs, ys, *last), BF16),
+            [pltpu.VMEM((ys, *last), BF16), pltpu.VMEM((xs, *last), BF16)],
+            pltpu.VMEM((2, *last), BF16),
+            pltpu.VMEM((parts, 2, xs, ys, *last), BF16),
+            [pltpu.VMEM((parts, xs - 1, ys, *last), BF16), pltpu.VMEM((parts, ys - 1, xs, *last), BF16)],
+            [pltpu.VMEM((parts, ys - 1, *last), BF16), pltpu.VMEM((parts, xs - 1, *last), BF16)],
+            pltpu.VMEM((parts, zs - 1, 2, shard_rows, width), BF16),
+            pltpu.VMEM((stages, 8, D), F32),
+            sems((parts, in_count)),
+            sems((parts, in_count)),
+            sems((stages,)),
+            sems((stages,)),
+        ],
+        compiler_params=pltpu.CompilerParams(
+            collective_id=number, has_side_effects=True, vmem_limit_bytes=56 << 20
+        ),
+        cost_estimate=pl.CostEstimate(flops=rows << 20, transcendentals=0, bytes_accessed=rows << 10),
+    )(raw, dq, near, back, w, d_attn, mixed_rows, at, gains, cosine, sine, x, norm_gains, second)
 
 
 def add_swapped(keep, send, direction):
@@ -969,7 +1205,7 @@
     scale_second = rms_scale(x_mid)
     normed_second = (x_mid * scale_second * norm_gains[1]).astype(BF16)
     g = cotangent[0]
-    hot_x, hot_y = relative_rows("cxyz", D), relative_rows("cyxz", D)
+    hot_x = relative_rows("cxyz", D)
     shards = jnp.stack([gate_up_master[:, :FF], gate_up_master[:, FF:]]).astype(BF16)
     out_sum, d_b, grad_down, gate_up_sums = feed(
         after(shards, normed_second),
@@ -986,35 +1222,34 @@
     d_mid = g.astype(F32) + d_norm
     d_attn = d_mid.astype(BF16)
     d_mixed = dot_cols(d_attn, w_out).astype(BF16)
-    out_terms = transpose_in_order(hot_y, mixed)
-    half = QUERY_FEATURES // 2
-    out_1 = add_swapped(
-        dot(out_terms[:half], d_attn).astype(BF16), dot(out_terms[half:], d_attn).astype(BF16), "c"
-    )
-
     zero = jnp.zeros((rows, QUERY_FEATURES), F32)
     dq, far = attend_back(0, q, d_mixed, mixed, lse, zero, others, low, first_lane, BF16)
     if seq_width == 2:
-        back = [lax.ppermute(p, "seq", [(1, 0)]) for p in far]
+        back = lax.ppermute(far, "seq", [(1, 0)])
     else:
-        back = [lax.psum_scatter(p, "seq", scatter_dimension=0, tiled=True) for p in far]
-    out_2 = add_along(out_1, "y")
+        back = lax.psum_scatter(far, "seq", scatter_dimension=0, tiled=True)
     dq, near = attend_back(
-        others[0].shape[0], q, after(d_mixed, out_2), mixed, lse, dq, own, low, first_lane, F32
+        others[0].shape[0], q, d_mixed, mixed, lse, dq, own, low, first_lane, F32
     )
-    out_grad = add_along(add_along(out_2, "x"), "z", True)
-    d_qkv, d_gain_qk = prep_back(raw, gain_rows, cosine, sine, dq, near, back)
-    first_terms = transpose_in_order(hot_x, normed_first)
-    qkv_1 = add_swapped(
-        dot(first_terms[: D // 2], d_qkv).astype(BF16), dot(first_terms[D // 2 :], d_qkv).astype(BF16), "c"
+    d_x, sums, gain_sums = leave(
+        raw,
+        dq,
+        near,
+        back,
+        w_qkv,
+        d_attn,
+        transpose_in_order(hot_x, mixed),
+        transpose_in_order(hot_x, normed_first),
+        gain_rows,
+        cosine,
+        sine,
+        inputs[0],
+        jnp.pad(norm_gains, ((0, 6), (0, 0))),
+        jnp.broadcast_to(d_gain_second[None], (8, D)),
+        3,
     )
-    qkv_grad = add_along(add_along(add_along(qkv_1, "x"), "y"), "z", True)
-    d_a = dot_cols(d_qkv, w_qkv)
-    d_x, d_gain_first = rms_back(x, scale_first, norm_gains[0], d_a)
-    input_grad = (d_mid + d_x)[None]
-    gain_terms = jnp.pad(d_gain_qk[:2], ((0, 0), (0, D - LANES)))
-    gain_terms = jnp.concatenate([d_gain_first[None], d_gain_second[None], gain_terms], axis=0)
-    gain_sums = sum_everywhere(jnp.pad(gain_terms, ((0, 4), (0, 0))))
+    input_grad = (d_mid + d_x.astype(F32))[None]
+    out_grad, qkv_grad = sums[:, :D], sums[:, D:]
     norm_grad = gain_sums[:2]
     qk_grad = gain_sums[2:4, :HEAD_SIZE] + gain_sums[2:4, HEAD_SIZE:LANES]
 
@@ -1024,9 +1259,8 @@
     out_new = adam_update(
         out_master, out_first, out_second, out_grad, (QUERY_FEATURES // 16) ** -0.5, DECAY_RATE
     )
-    gate_up_grad = jnp.concatenate([gate_up_sums[0], gate_up_sums[1]], axis=1)
     gate_new = adam_update(
-        gate_up_master, gate_up_first, gate_up_second, gate_up_grad, D**-0.5, DECAY_RATE
+        gate_up_master, gate_up_first, gate_up_second, gate_up_sums, D**-0.5, DECAY_RATE
     )
     down_new = adam_update(down_master, down_first, down_second, down_grad, FF**-0.5, DECAY_RATE)
     return (

time: 630 us -> 614 us (0.975)
  Pallas kernels: 343 us -> 433 us
  waiting for transfers between devices: 133 us -> 66.4 us
  starting transfers between devices: 42.4 us -> 13.4 us
  matrix products: 45.2 us -> 28.2 us
    pallas_call x1, Pallas kernels: 12.5 us -> 100 us  [leave(): pl.pallas_call(exit_kernel, name='leave', grid=(parts + 4,), in_specs=[bl...]
    ppermute x21 -> x1, waiting for transfers between devices: 78.4 us -> 5.49 us  [per_device(): back = lax.ppermute(far, 'seq', [(1, 0)])]
    ppermute x21 -> x1, starting transfers between devices: 29.8 us -> 1.28 us  [per_device(): back = lax.ppermute(far, 'seq', [(1, 0)])]
    dot_general x4 -> x0, matrix products: 11.3 us -> none  [dot(): lax.dot_general(a, b, (((1,), (0,)), ((), ())), preferred_element_type=F32)]
    dot_general x5 -> x4, matrix products: 19.9 us -> 15 us  [dot_cols(): lax.dot_general(a, b, (((1,), (1,)), ((), ())), preferred_element_type=F32)]
  transfers between devices with their start and end apart: 27 -> 7, of which waited for: 15 -> 6; matrix products, arithmetic and copies ran while one was open for 8% -> 8% of each run, Pallas kernels for 12% -> 28%
where the time goes in v5:
time: 614 us; the launch traced here: 606 us
  Pallas kernels  433 us (71%)
  waiting for transfers between devices  66.4 us (11%)
  other arithmetic  37.9 us (6%)
  matrix products  28.2 us (5%)
  between operations  14.6 us (2%)
  starting transfers between devices  13.4 us (2%)
  local copies, waits for them, and re-layouts  13 us (2%)
    pallas_call x1, Pallas kernels, feed(): pl.pallas_call(feed_kernel, name='feed', grid=(parts + FEED_LEAD + 4,), i...  212 us
    pallas_call x1, Pallas kernels, leave(): pl.pallas_call(exit_kernel, name='leave', grid=(parts + 4,), in_specs=[bl...  100 us
    ppermute x4, waiting for transfers between devices, per_device(): others = [lax.ppermute(p, 'seq', [(0, 1)]) for p in own]  48.1 us
    pallas_call x2, Pallas kernels, attend_back(): pl.pallas_call(functools.partial(attend_back_kernel, start), name='attend...  47.5 us
    pallas_call x1, Pallas kernels, gather_all(): pl.pallas_call(functools.partial(gather_kernel, plan), name='gather_all',...  44.6 us
    pallas_call x1, Pallas kernels, attend(): pl.pallas_call(attend_kernel, name='attend', grid_spec=pltpu.PrefetchScal...  20.4 us
    dot_general x4, matrix products, dot_cols(): lax.dot_general(a, b, (((1,), (1,)), ((), ())), preferred_element_type=F32)  15 us
    all_gather x1, waiting for transfers between devices, gather(): return lax.all_gather(shard, ALL, axis=0, tiled=True)  12.7 us
  transfers between devices with their start and end apart: 7, of which 6 were waited for; matrix products, arithmetic and copies ran while one was open for 8% of the time, Pallas kernels for 28%

profile of v5, /device:TPU:0, one launch (start us, length us, event | category | flops | bytes accessed | tf_op | source)
XLA Modules:
  0.0 606.3 jit_solution(3491954952082364361)
XLA Ops:
  12.1 2.1 fusion
  14.4 3.0 fusion.26
  17.4 44.6 %gather_all.1 = (bf16[4,2,2,2,32,2048]{5,4,3,2,1,0:T(8,128)(2,1)}, bf16[4,2,2,2,32,1024]{5,4,3,2,1,0:T(8,128)(2,1)}) custom-call(bf16[32,2048]{1,0:T(8,128)(2,1)} %convert_element_type.70.refs_0_, bf16[32,1024]{1,0:T(8,128)(2,1)} %convert_element_type.71.refs_1_), custom_call_target="tpu_custom_call" | custom-call | tf_op jit(solution)/shard_map/gather_all/pallas_call | solution.py:504
  62.7 3.9 pad_maximum_fusion.1
  66.6 9.1 %fusion.7.raw_ref = f32[1024,2048]{1,0:T(8,128)} fusion(bf16[1024,2048]{1,0:T(8,128)(2,1)} %bitcast.40, bf16[1,1024,1024]{2,1,0:T(8,128)(2,1)S(1)} %copy-done.6, f32[1024]{0:T(1024)S(1)} %bitcast.46, f32[1024]{0:T(1024)S(1)} %add_rsqrt_fusion.1), kind=kOutput, calls=%fused_computation.18 | convolution fusion | flops 4299161600 | bytes 14688256 | tf_op jit(solution)/shard_map/dot_general | solution.py:1195
  75.7 8.3 %prep.1 = (bf16[1024,1024]{1,0:T(8,128)(2,1)}, bf16[1024,256]{1,0:T(8,128)(2,1)}, bf16[1024,256]{1,0:T(8,128)(2,1)}, bf16[1024,256]{1,0:T(8,128)(2,1)}, bf16[1024,256]{1,0:T(8,128)(2,1)}) custom-call(f32[1024,2048]{1,0:T(8,128)} %fusion.7.raw_ref, f32[8,128]{1,0:T(8,128)} %pad.8.gain_ref, f32[1024,128]{1,0:T(8,128)} %get-tuple-element.95.cos_ref, ...), custom_call_target="tpu_custom_call" | custom-call | flops 83886080 | bytes 12582912 | tf_op jit(solution)/shard_map/prep/pallas_call | solution.py:92
  84.0 2.7 collective-permute-start.3
  87.4 10.5 %collective-permute-done.3.rest_3_ = bf16[1024,256]{1,0:T(8,128)(2,1)} collective-permute-done((bf16[1024,256]{1,0:T(8,128)(2,1)}, bf16[1024,256]{1,0:T(8,128)(2,1)}, u32[]{:S(2)}, u32[]{:S(2)}) %collective-permute-start.3) | collective-permute-done | bytes 524320 | tf_op jit(solution)/shard_map/ppermute | solution.py:1199
  98.0 5.2 collective-permute-start
  103.2 2.1 collective-permute-start.1
  105.3 2.1 collective-permute-start.2
  109.1 8.1 %collective-permute-done.rest_0_ = bf16[1024,256]{1,0:T(8,128)(2,1)} collective-permute-done((bf16[1024,256]{1,0:T(8,128)(2,1)}, bf16[1024,256]{1,0:T(8,128)(2,1)}, u32[]{:S(2)}, u32[]{:S(2)}) %collective-permute-start) | collective-permute-done | bytes 524320 | tf_op jit(solution)/shard_map/ppermute | solution.py:1199
  117.2 11.3 %collective-permute-done.1.rest_1_ = bf16[1024,256]{1,0:T(8,128)(2,1)} collective-permute-done((bf16[1024,256]{1,0:T(8,128)(2,1)}, bf16[1024,256]{1,0:T(8,128)(2,1)}, u32[]{:S(2)}, u32[]{:S(2)}) %collective-permute-start.1) | collective-permute-done | bytes 524320 | tf_op jit(solution)/shard_map/ppermute | solution.py:1199
  128.5 18.2 %collective-permute-done.2.rest_2_ = bf16[1024,256]{1,0:T(8,128)(2,1)} collective-permute-done((bf16[1024,256]{1,0:T(8,128)(2,1)}, bf16[1024,256]{1,0:T(8,128)(2,1)}, u32[]{:S(2)}, u32[]{:S(2)}) %collective-permute-start.2) | collective-permute-done | bytes 524320 | tf_op jit(solution)/shard_map/ppermute | solution.py:1199
  147.7 20.4 %attend.1 = (bf16[1024,1024]{1,0:T(8,128)(2,1)}, f32[64,2048]{1,0:T(8,128)}) custom-call(s32[9]{0:T(128)} %pad_add_fusion.low_ref, s32[1024,128]{1,0:T(8,128)} %broadcast_in_dim.32.first_ref, bf16[1024,1024]{1,0:T(8,128)(2,1)} %get-tuple-element.43.q_ref, bf16[1024,256]{1,0:T(8,128)(2,1)} %collective-permute-done.rest_0_, ...), custom_call_target="tpu_custom_call" | custom-call | flops 25769803776 | bytes 16777216 | tf_op jit(solution)/shard_map/attend/pallas_call | solution.py:180
  168.1 4.1 multiply_reduce_fusion.2
  175.5 3.7 fusion.17.at_ref
  179.2 12.7 %all-gather.2.cloned.1.call-done.wd_ref = bf16[4608,1024]{1,0:T(8,128)(2,1)} async-done(((bf16[144,1024]{1,0:T(8,128)(2,1)}), bf16[4608,1024]{1,0:T(8,128)(2,1)}) %all-gather.2.cloned.1.call-update) | async-done | bytes 9437200 | tf_op jit(solution)/shard_map/all_gather | solution.py:357
  192.0 211.6 %feed.1 = (bf16[2,4,2,2,2,32,4608]{6,5,4,3,2,1,0:T(8,128)(2,1)}, f32[1024,1024]{1,0:T(8,128)}, f32[1024,1024]{1,0:T(8,128)}, bf16[4608,1024]{1,0:T(8,128)(2,1)}, f32[32,9216]{1,0:T(8,128)}) custom-call(bf16[2,32,4608]{2,1,0:T(8,128)(2,1)} %pad_maximum_fusion.shard_ref, bf16[1024,1024]{1,0:T(8,128)(2,1)} %copy-done.12, bf16[1024,1024]{1,0:T(8,128)(2,1)} %fusion.17.at_ref, ...), custom_call_target="tpu_custom_call" | custom-call | flops 86973087744 | bytes 56623104 | tf_op jit(solution)/shard_map/feed/pallas_call | solution.py:784
  404.9 3.8 fusion.19.at_ref
  408.7 3.7 fusion.18.mixed_ref
  416.7 3.8 convolution_convert_fusion.do_ref
  421.1 2.5 broadcast_in_dim.60.before_ref
  423.7 11.6 %attend_back.2 = (bf16[1024,1024]{1,0:T(8,128)(2,1)}, f32[1024,1024]{1,0:T(8,128)}) custom-call(s32[9]{0:T(128)} %pad_add_fusion.low_ref, s32[8,1024]{1,0:T(8,128)} %broadcast_in_dim.59.first_ref, bf16[1024,1024]{1,0:T(8,128)(2,1)} %get-tuple-element.43.q_ref, bf16[1024,1024]{1,0:T(8,128)(2,1)} %convolution_convert_fusion.do_ref, ...), custom_call_target="tpu_custom_call" | custom-call | flops 268435456 | bytes 262144 | tf_op jit(solution)/shard_map/attend_back/pallas_call | solution.py:283
  436.6 35.9 %attend_back.3 = (f32[1024,1024]{1,0:T(8,128)}, f32[1024,1024]{1,0:T(8,128)}) custom-call(s32[9]{0:T(128)} %pad_add_fusion.low_ref, s32[8,1024]{1,0:T(8,128)} %broadcast_in_dim.59.first_ref, bf16[1024,1024]{1,0:T(8,128)(2,1)} %get-tuple-element.43.q_ref, bf16[1024,1024]{1,0:T(8,128)(2,1)} %convolution_convert_fusion.do_ref, ...), custom_call_target="tpu_custom_call" | custom-call | flops 268435456 | bytes 262144 | tf_op jit(solution)/shard_map/attend_back/pallas_call | solution.py:283
  472.5 4.0 convert_bitcast_fusion
  476.5 2.3 multiply_subtract_fusion
  478.8 5.5 collective-permute-done.4.back_ref
  485.0 100.4 %leave.1 = (bf16[1024,1024]{1,0:T(8,128)(2,1)}, f32[32,3072]{1,0:T(8,128)}, f32[8,1024]{1,0:T(8,128)}) custom-call(f32[1024,2048]{1,0:T(8,128)} %fusion.7.raw_ref, f32[1024,1024]{1,0:T(8,128)} %get-tuple-element.56.dq_ref, f32[1024,1024]{1,0:T(8,128)} %get-tuple-element.57.near_ref, bf16[1024,1024]{1,0:T(8,128)(2,1)} %collective-permute-done.4.back_ref, ...), custom_call_target="tpu_custom_call" | custom-call | flops 1073741824 | bytes 1048576 | tf_op jit(solution)/shard_map/leave/pallas_call | solution.py:1082
  590.1 1.9 multiply_subtract_fusion.2
  592.1 4.5 add_bitcast_fusion
  596.6 2.7 multiply_subtract_fusion.1
  (109 shorter events, 25.3 us)
Async XLA Ops:
  7.2 7.1 %copy-start.30 = (s32[1,16]{1,0:T(1,128)S(1)}, s32[1,16]{1,0:T(1,128)}, u32[]{:S(2)}) copy-start(s32[1,16]{1,0:T(1,128)} %param.23) | copy-start | bytes 196
  7.2 7.0 %copy-start.28 = (f32[2,64]{1,0:T(2,128)S(1)}, f32[2,64]{1,0:T(2,128)}, u32[]{:S(2)}) copy-start(f32[2,64]{1,0:T(2,128)} %param.27) | copy-start | bytes 1540
  7.2 184.8 %all-gather.2.cloned.1.call-start = ((), (), s32[]{:S(2)}) async-start(), calls=%async_computation.1 | async-start | bytes 9732096 | tf_op jit(solution)/shard_map/all_gather | solution.py:357
  14.4 132.3 %copy-start.24 = (s32[1024]{0:T(1024)}, s32[1024]{0:T(1024)S(1)}, u32[]{:S(2)}) copy-start(s32[1024]{0:T(1024)S(1)} %get-tuple-element.92) | copy-start | bytes 12292
  14.4 52.2 %copy-start.6 = (bf16[1,1024,1024]{2,1,0:T(8,128)(2,1)S(1)}, bf16[1,1024,1024]{2,1,0:T(8,128)(2,1)}, u32[]{:S(2)}) copy-start(bf16[1,1024,1024]{2,1,0:T(8,128)(2,1)} %param.21) | copy-start | bytes 6291460
  75.7 10.9 %copy-start.9 = (f32[144,1024]{1,0:T(8,128)S(1)}, f32[144,1024]{1,0:T(8,128)}, u32[]{:S(2)}) copy-start(f32[144,1024]{1,0:T(8,128)} %param.39) | copy-start | bytes 1769476
  75.7 31.8 %copy-start.7 = (f32[32,9216]{1,0:T(8,128)S(1)}, f32[32,9216]{1,0:T(8,128)}, u32[]{:S(2)}) copy-start(f32[32,9216]{1,0:T(8,128)} %param.36) | copy-start | bytes 3538948
  84.0 13.9 %collective-permute-start.3 = (bf16[1024,256]{1,0:T(8,128)(2,1)}, bf16[1024,256]{1,0:T(8,128)(2,1)}, u32[]{:S(2)}, u32[]{:S(2)}) collective-permute-start(bf16[1024,256]{1,0:T(8,128)(2,1)} %get-tuple-element.47.rest_7_.rest_3_), channel_id=1, source_target_pairs={{0,1},{2,3},{4,5},{6,7},{8,9},{10,11},{12,13},{14,15},{16,17},{18,... | collective-permute-start | bytes 1572872 | tf_op jit(solution)/shard_map/ppermute | solution.py:1199
  97.9 498.6 %reduce-scatter.2.cloned.1.call-start = ((), (), s32[]{:S(2)}) async-start(), calls=%async_computation.2 | async-start | bytes 9732096 | tf_op jit(solution)/shard_map/reduce_scatter | solution.py:1220
  98.0 19.2 %collective-permute-start = (bf16[1024,256]{1,0:T(8,128)(2,1)}, bf16[1024,256]{1,0:T(8,128)(2,1)}, u32[]{:S(2)}, u32[]{:S(2)}) collective-permute-start(bf16[1024,256]{1,0:T(8,128)(2,1)} %get-tuple-element.44.rest_4_.rest_0_), channel_id=1, source_target_pairs={{0,1},{2,3},{4,5},{6,7},{8,9},{10,11},{12,13},{14,15},{16,17},{18,... | collective-permute-start | bytes 1572872 | tf_op jit(solution)/shard_map/ppermute | solution.py:1199
  103.2 25.3 %collective-permute-start.1 = (bf16[1024,256]{1,0:T(8,128)(2,1)}, bf16[1024,256]{1,0:T(8,128)(2,1)}, u32[]{:S(2)}, u32[]{:S(2)}) collective-permute-start(bf16[1024,256]{1,0:T(8,128)(2,1)} %get-tuple-element.45.rest_5_.rest_1_), channel_id=1, source_target_pairs={{0,1},{2,3},{4,5},{6,7},{8,9},{10,11},{12,13},{14,15},{16,17},{18,... | collective-permute-start | bytes 1572872 | tf_op jit(solution)/shard_map/ppermute | solution.py:1199
  105.3 41.4 %collective-permute-start.2 = (bf16[1024,256]{1,0:T(8,128)(2,1)}, bf16[1024,256]{1,0:T(8,128)(2,1)}, u32[]{:S(2)}, u32[]{:S(2)}) collective-permute-start(bf16[1024,256]{1,0:T(8,128)(2,1)} %get-tuple-element.46.rest_6_.rest_2_), channel_id=1, source_target_pairs={{0,1},{2,3},{4,5},{6,7},{8,9},{10,11},{12,13},{14,15},{16,17},{18,... | collective-permute-start | bytes 1572872 | tf_op jit(solution)/shard_map/ppermute | solution.py:1199
  147.7 20.4 %copy-start.33 = (bf16[4,2,2,2,32,1024]{5,4,3,2,1,0:T(8,128)(2,1)S(1)}, bf16[4,2,2,2,32,1024]{5,4,3,2,1,0:T(8,128)(2,1)}, u32[]{:S(2)}) copy-start(bf16[4,2,2,2,32,1024]{5,4,3,2,1,0:T(8,128)(2,1)} %get-tuple-element.49) | copy-start | bytes 6291460
  408.7 4.6 copy-start.2
  435.3 49.0 %collective-permute-start.4 = (bf16[1024,1024]{1,0:T(8,128)(2,1)}, bf16[1024,1024]{1,0:T(8,128)(2,1)}, u32[]{:S(2)}, u32[]{:S(2)}) collective-permute-start(bf16[1024,1024]{1,0:T(8,128)(2,1)} %get-tuple-element.58), channel_id=1, source_target_pairs={{1,0},{3,2},{5,4},{7,6},{9,8},{11,10},{13,12},{15,14},{17,16},{19,... | collective-permute-start | bytes 6291464 | tf_op jit(solution)/shard_map/ppermute | solution.py:1228
  472.4 4.0 copy-start.8
  472.4 4.0 copy-start.13
  472.4 4.0 copy-start.14
  484.9 100.5 %copy-start.29 = (f32[2,64]{1,0:T(2,128)S(1)}, f32[2,64]{1,0:T(2,128)}, u32[]{:S(2)}) copy-start(f32[2,64]{1,0:T(2,128)} %param.27) | copy-start | bytes 1540
  484.9 100.6 %copy-start.31 = (f32[2,64]{1,0:T(2,128)S(1)}, f32[2,64]{1,0:T(2,128)}, u32[]{:S(2)}) copy-start(f32[2,64]{1,0:T(2,128)} %param.28) | copy-start | bytes 1540
  484.9 100.6 %copy-start.32 = (f32[2,64]{1,0:T(2,128)S(1)}, f32[2,64]{1,0:T(2,128)}, u32[]{:S(2)}) copy-start(f32[2,64]{1,0:T(2,128)} %param.29) | copy-start | bytes 1540
  484.9 102.1 %copy-start.26 = (f32[2,1024]{1,0:T(2,128)S(1)}, f32[2,1024]{1,0:T(2,128)}, u32[]{:S(2)}) copy-start(f32[2,1024]{1,0:T(2,128)} %param.25) | copy-start | bytes 24580
  484.9 102.1 %copy-start.27 = (f32[2,1024]{1,0:T(2,128)S(1)}, f32[2,1024]{1,0:T(2,128)}, u32[]{:S(2)}) copy-start(f32[2,1024]{1,0:T(2,128)} %param.26) | copy-start | bytes 24580
  485.0 103.4 %copy-start.18 = (f32[32,1024]{1,0:T(8,128)S(1)}, f32[32,1024]{1,0:T(8,128)}, u32[]{:S(2)}) copy-start(f32[32,1024]{1,0:T(8,128)} %param.33) | copy-start | bytes 393220
  485.0 103.4 %copy-start.21 = (f32[32,1024]{1,0:T(8,128)S(1)}, f32[32,1024]{1,0:T(8,128)}, u32[]{:S(2)}) copy-start(f32[32,1024]{1,0:T(8,128)} %param.34) | copy-start | bytes 393220
  485.0 103.4 %copy-start.22 = (f32[32,1024]{1,0:T(8,128)S(1)}, f32[32,1024]{1,0:T(8,128)}, u32[]{:S(2)}) copy-start(f32[32,1024]{1,0:T(8,128)} %param.35) | copy-start | bytes 393220
  485.0 105.1 %copy-start.16 = (f32[32,2048]{1,0:T(8,128)S(1)}, f32[32,2048]{1,0:T(8,128)}, u32[]{:S(2)}) copy-start(f32[32,2048]{1,0:T(8,128)} %param.30) | copy-start | bytes 786436
  485.0 105.1 %copy-start.19 = (f32[32,2048]{1,0:T(8,128)S(1)}, f32[32,2048]{1,0:T(8,128)}, u32[]{:S(2)}) copy-start(f32[32,2048]{1,0:T(8,128)} %param.31) | copy-start | bytes 786436
  485.0 105.1 %copy-start.20 = (f32[32,2048]{1,0:T(8,128)S(1)}, f32[32,2048]{1,0:T(8,128)}, u32[]{:S(2)}) copy-start(f32[32,2048]{1,0:T(8,128)} %param.32) | copy-start | bytes 786436
  585.5 6.6 %copy-start.11 = (bf16[1024,1024]{1,0:T(8,128)(2,1)S(1)}, bf16[1024,1024]{1,0:T(8,128)(2,1)}, u32[]{:S(2)}) copy-start(bf16[1024,1024]{1,0:T(8,128)(2,1)} %get-tuple-element.59) | copy-start | bytes 6291460
  592.1 4.5 copy-start.10
  592.1 4.5 copy-start.17
  (10 other events, 26.6 us)
Sparse Core Ops, SparseCore 0:
  98.1 93.8 all-gather.1
  403.7 143.5 reduce-scatter.1

commit v6 on v5

--- a/solution.py
+++ b/solution.py
@@ -203,9 +203,11 @@
     )(low, first, q, *others, *own)
 
 
-def attend_back_kernel(start, low_ref, first_ref, q_ref, do_ref, mixed_ref, lse_ref, before_ref, *rest):
-    refs = rest[:PIECES]
-    d_ref, dq_ref, queries, rising, deltas, dqs, dkvs = rest[PIECES:]
+def attend_back_kernel(
+    start, pieces, count, low_ref, first_ref, q_ref, do_ref, mixed_ref, lse_ref, *rest
+):
+    befores, refs = rest[:count], rest[count : count + len(pieces)]
+    d_ref, dq_ref, queries, rising, deltas, dqs, dkvs = rest[count + len(pieces) :]
     turn = pl.program_id(0)
     block = q_ref.shape[0]
     rows = refs[0].shape[0]
@@ -219,12 +221,15 @@
 
     @pl.when(end <= begin)
     def _():
-        dq_ref[...] = before_ref[...]
+        if befores:
+            dq_ref[...] = jnp.concatenate([ref[...] for ref in befores], axis=1)
+        else:
+            dq_ref[...] = jnp.zeros_like(dq_ref)
 
     @pl.when(end > begin)
     def _():
-        for p in range(PIECES):
-            part = slice(p * 2 * LANES, (p + 1) * 2 * LANES)
+        for p, piece in enumerate(pieces):
+            part = slice(piece * 2 * LANES, (piece + 1) * 2 * LANES)
             queries[p] = stack_heads(q_ref[:, part])
             rising[p] = stack_heads(do_ref[:, part])
             across = jnp.transpose(do_ref[:, part].astype(F32) * mixed_ref[:, part].astype(F32))
@@ -249,9 +254,9 @@
             key_place = at * KEY_BLOCK + row
             allowed = (key_place >= first) & (key_place <= place)
             allowed = jnp.concatenate([allowed] * 4, axis=1)
-            for p in range(PIECES):
+            for p, piece in enumerate(pieces):
                 key, value = refs[p][span, :LANES], refs[p][span, LANES:]
-                logs = lse_ref[0:1, p * tall : (p + 1) * tall]
+                logs = lse_ref[0:1, piece * tall : (piece + 1) * tall]
                 probs = jnp.where(allowed, jnp.exp(dot_cols(key, queries[p]) - logs), 0.0)
                 dprobs = dot_cols(value, rising[p])
                 dscores = (probs * (dprobs - deltas[p, 0:1])).astype(BF16)
@@ -261,27 +266,35 @@
             return 0
 
         lax.fori_loop(begin, end, step, 0)
-        for p in range(PIECES):
+        for p in range(len(pieces)):
             part = slice(p * 2 * LANES, (p + 1) * 2 * LANES)
-            dq_ref[:, part] = before_ref[:, part] + unstack_heads(dqs[p])
+            total = unstack_heads(dqs[p])
+            if befores:
+                each = len(pieces) // count
+                at = p % each * 2 * LANES
+                total = total + befores[p // each][:, at : at + 2 * LANES]
+            dq_ref[:, part] = total
 
     @pl.when(turn == pl.num_programs(0) - 1)
     def _():
-        for p in range(PIECES):
+        for p in range(len(pieces)):
             for half in range(2):
-                part = slice(half * KEY_FEATURES + p * LANES, half * KEY_FEATURES + (p + 1) * LANES)
+                at = (half * len(pieces) + p) * LANES
+                part = slice(at, at + LANES)
                 d_ref[:, part] = dkvs[p, :, half * LANES : (half + 1) * LANES].astype(d_ref.dtype)
 
 
-def attend_back(start, q, d_mixed, mixed, lse, before, source, low, first_lane, kind):
+def attend_back(start, pieces, q, d_mixed, mixed, lse, befores, source, low, first_lane, kind):
     rows = q.shape[0]
     block = QUERY_BLOCK
     turns = rows // block
     count = source[0].shape[0]
-    whole = pl.BlockSpec((count, 2 * KEY_FEATURES), lambda t, low: (0, 0))
+    some = len(pieces)
+    whole = pl.BlockSpec((count, some * 2 * LANES), lambda t, low: (0, 0))
+    part = lambda width: pl.BlockSpec((block, width), lambda t, low: (t, 0))
     wide = pl.BlockSpec((block, QUERY_FEATURES), lambda t, low: (t, 0))
     d_keys, dq = pl.pallas_call(
-        functools.partial(attend_back_kernel, start),
+        functools.partial(attend_back_kernel, start, pieces, len(befores)),
         name="attend_back",
         grid_spec=pltpu.PrefetchScalarGridSpec(
             num_scalar_prefetch=1,
@@ -292,27 +305,27 @@
                 wide,
                 wide,
                 pl.BlockSpec((8, HQ * block), lambda t, low: (t, 0)),
-                wide,
             ]
-            + [pl.BlockSpec((count, 2 * LANES), lambda t, low: (0, 0))] * PIECES,
-            out_specs=[whole, wide],
+            + [part(v.shape[1]) for v in befores]
+            + [pl.BlockSpec((count, 2 * LANES), lambda t, low: (0, 0))] * some,
+            out_specs=[whole, part(some * 2 * LANES)],
             scratch_shapes=[
-                pltpu.VMEM((PIECES, 4 * block, LANES), BF16),
-                pltpu.VMEM((PIECES, 4 * block, LANES), BF16),
-                pltpu.VMEM((PIECES, 8, 4 * block), F32),
-                pltpu.VMEM((PIECES, 4 * block, LANES), F32),
-                pltpu.VMEM((PIECES, count, 2 * LANES), F32),
+                pltpu.VMEM((some, 4 * block, LANES), BF16),
+                pltpu.VMEM((some, 4 * block, LANES), BF16),
+                pltpu.VMEM((some, 8, 4 * block), F32),
+                pltpu.VMEM((some, 4 * block, LANES), F32),
+                pltpu.VMEM((some, count, 2 * LANES), F32),
             ],
         ),
         out_shape=[
-            jax.ShapeDtypeStruct((count, 2 * KEY_FEATURES), kind),
-            jax.ShapeDtypeStruct((rows, QUERY_FEATURES), F32),
+            jax.ShapeDtypeStruct((count, some * 2 * LANES), kind),
+            jax.ShapeDtypeStruct((rows, some * 2 * LANES), F32),
         ],
         compiler_params=params(),
         cost_estimate=pl.CostEstimate(
             flops=rows << 18, transcendentals=0, bytes_accessed=rows << 8
         ),
-    )(low, first_lane, q, d_mixed, mixed, lse, before, *source)
+    )(low, first_lane, q, d_mixed, mixed, lse, *befores, *[source[p] for p in pieces])
     return dq, d_keys
 
 
@@ -524,8 +537,10 @@
     return lax.optimization_barrier((values, earlier))[0]
 
 
-FIRST_PARTS = 3
-FEED_LEAD = 4
+FIRST_PARTS = 6
+SLACK = 2
+TERM_SLOTS = SLACK + 1
+FEED_LEAD = 3 * SLACK + 1
 
 
 def feed_kernel(
@@ -611,24 +626,24 @@
     def scatter_copies(p, stage):
         sems = (in_send, in_recv)
         if stage == 0:
-            return [remote(terms.at[lax.rem(p, 2), :, 1], got_c.at[p], sems, p, 0, "c", 1)]
+            return [remote(terms.at[lax.rem(p, TERM_SLOTS), :, 1], got_c.at[p], sems, p, 0, "c", 1)]
         copies = []
-        slot = 1
+        slot, slot_now = 1, lax.rem(p, 2)
         for which, order in enumerate(orders):
             for s in (1, 2):
                 k = order[s - 1]
                 for d in range(1, size[k]):
                     if s == 1:
-                        source = total_1.at[0, d] if k == "x" else total_1.at[1, :, d]
+                        source = total_1.at[slot_now, 0, d] if k == "x" else total_1.at[slot_now, 1, :, d]
                     else:
-                        source = total_2[which].at[d]
+                        source = total_2[which].at[slot_now, d]
                     target = (got_1, got_2)[s - 1][which].at[p, d - 1]
                     if s == stage:
                         copies.append(remote(source, target, sems, p, slot, k, d))
                     slot += 1
         if stage == 3:
             for d in range(1, size["z"]):
-                copies.append(remote(total_3.at[:, d], got_z.at[p, d - 1], sems, p, slot + d - 1, "z", d))
+                copies.append(remote(total_3.at[slot_now, :, d], got_z.at[p, d - 1], sems, p, slot + d - 1, "z", d))
         return copies
 
     def own_copy():
@@ -680,15 +695,15 @@
     def _():
         begin(step + FIRST_PARTS - 1)
 
-    on(3, arrived)
-    on(2, pass_on(3))
-    on(1, pass_on(2))
+    on(3 * SLACK, arrived)
+    on(2 * SLACK, pass_on(3))
+    on(SLACK, pass_on(2))
     on(0, pass_on(1))
 
     def finish(p):
         for copy in scatter_copies(p, 3):
             copy.wait()
-        total = total_3[:, 0].astype(F32)
+        total = total_3[lax.rem(p, 2), :, 0].astype(F32)
         for d in range(1, size["z"]):
             total = total + got_z[p, d - 1].astype(F32)
         for which in range(2):
@@ -698,10 +713,10 @@
         for copy in scatter_copies(p, 2):
             copy.wait()
         for which, order in enumerate(orders):
-            total = total_2[which][0].astype(F32)
+            total = total_2[which][lax.rem(p, 2), 0].astype(F32)
             for d in range(1, size[order[1]]):
                 total = total + got_2[which][p, d - 1].astype(F32)
-            total_3[which] = total.astype(BF16)
+            total_3[lax.rem(p, 2), which] = total.astype(BF16)
         for copy in scatter_copies(p, 3):
             copy.start()
 
@@ -709,26 +724,26 @@
         for copy in scatter_copies(p, 1):
             copy.wait()
         for which, order in enumerate(orders):
-            kept = total_1[0, 0] if order[0] == "x" else total_1[1, :, 0]
+            kept = total_1[lax.rem(p, 2), 0, 0] if order[0] == "x" else total_1[lax.rem(p, 2), 1, :, 0]
             total = kept.astype(F32)
             for d in range(1, size[order[0]]):
                 total = total + got_1[which][p, d - 1].astype(F32)
-            total_2[which][...] = total.astype(BF16)
+            total_2[which][lax.rem(p, 2)] = total.astype(BF16)
         for copy in scatter_copies(p, 2):
             copy.start()
 
     def first(p):
         for copy in scatter_copies(p, 0):
             copy.wait()
-        total = terms[lax.rem(p, 2), :, 0].astype(F32) + got_c[p].astype(F32)
-        total_1[...] = total.astype(BF16)
+        total = terms[lax.rem(p, TERM_SLOTS), :, 0].astype(F32) + got_c[p].astype(F32)
+        total_1[lax.rem(p, 2)] = total.astype(BF16)
         for copy in scatter_copies(p, 1):
             copy.start()
 
-    on(FEED_LEAD + 4, finish)
-    on(FEED_LEAD + 3, third)
-    on(FEED_LEAD + 2, second)
-    on(FEED_LEAD + 1, first)
+    on(FEED_LEAD + 4 * SLACK, finish)
+    on(FEED_LEAD + 3 * SLACK, third)
+    on(FEED_LEAD + 2 * SLACK, second)
+    on(FEED_LEAD + SLACK, first)
 
     def compute(p):
         load_copy(p).wait()
@@ -748,7 +763,8 @@
         y_ref[...] += dot(hidden, wd)
         b_ref[...] += dot_cols(d_gate, wg) + dot_cols(d_up, wu)
         at = at_ref[...]
-        shape = (2,) + total_1.shape[1:]
+        shape = (2,) + total_1.shape[2:]
+        slot = lax.rem(p, TERM_SLOTS)
         terms[slot, 0] = dot(at, d_gate).astype(BF16).reshape(shape)
         terms[slot, 1] = dot(at, d_up).astype(BF16).reshape(shape)
         gd_ref[...] = dot_rows(hidden, g).astype(BF16)
@@ -784,7 +800,7 @@
     _, y_sum, b_sum, grad_down, sums = pl.pallas_call(
         feed_kernel,
         name="feed",
-        grid=(parts + FEED_LEAD + 4,),
+        grid=(parts + FEED_LEAD + 4 * SLACK,),
         in_specs=[anywhere, whole, whole, whole, anywhere, row],
         out_specs=[anywhere, whole, whole, row, whole],
         out_shape=[
@@ -796,10 +812,10 @@
         ],
         scratch_shapes=[
             pltpu.VMEM((2, 2, *(size[k] for k in NAMES), shard_rows, FF_BLOCK), BF16),
-            pltpu.VMEM((2, 2, 2, x, y, *last), BF16),
-            pltpu.VMEM((2, x, y, *last), BF16),
-            [pltpu.VMEM((y, *last), BF16), pltpu.VMEM((x, *last), BF16)],
-            pltpu.VMEM((2, *last), BF16),
+            pltpu.VMEM((TERM_SLOTS, 2, 2, x, y, *last), BF16),
+            pltpu.VMEM((2, 2, x, y, *last), BF16),
+            [pltpu.VMEM((2, y, *last), BF16), pltpu.VMEM((2, x, *last), BF16)],
+            pltpu.VMEM((2, 2, *last), BF16),
             pltpu.VMEM((parts, 2, x, y, *last), BF16),
             [pltpu.VMEM((parts, x - 1, y, *last), BF16), pltpu.VMEM((parts, y - 1, x, *last), BF16)],
             [pltpu.VMEM((parts, y - 1, *last), BF16), pltpu.VMEM((parts, x - 1, *last), BF16)],
@@ -830,7 +846,19 @@
     raw_ref,
     dq_ref,
     near_ref,
-    back_ref,
+    w_ref,
+    attn_ref,
+    *rest,
+):
+    back_refs, rest = rest[:2], rest[2:]
+    run_leave(back_refs, raw_ref, dq_ref, near_ref, w_ref, attn_ref, *rest)
+
+
+def run_leave(
+    back_refs,
+    raw_ref,
+    dq_ref,
+    near_ref,
     w_ref,
     attn_ref,
     mixed_ref,
@@ -884,7 +912,7 @@
 
     def scatter_copies(p, stage):
         if stage == 0:
-            return [remote(terms.at[lax.rem(p, 2), :, 1], got_c.at[p], p, 0, "c", 1)]
+            return [remote(terms.at[lax.rem(p, 3), :, 1], got_c.at[p], p, 0, "c", 1)]
         copies = []
         slot = 1
         for which, order in enumerate(orders):
@@ -946,7 +974,7 @@
     def first(p):
         for copy in scatter_copies(p, 0):
             copy.wait()
-        total = terms[lax.rem(p, 2), :, 0].astype(F32) + got_c[p].astype(F32)
+        total = terms[lax.rem(p, 3), :, 0].astype(F32) + got_c[p].astype(F32)
         total_1[...] = total.astype(BF16)
         for copy in scatter_copies(p, 1):
             copy.start()
@@ -957,12 +985,16 @@
         first_ref[...] = jnp.zeros_like(first_ref)
         head_ref[...] = jnp.zeros_like(head_ref)
 
-    on(4, finish)
-    on(3, third)
-    on(2, second)
-    on(1, first)
+    on(5, finish)
+    on(4, third)
+    on(3, second)
+    on(2, first)
 
     block = 256
+
+    def back(half, j, rows_at):
+        at = (2 * half + j % 2) * LANES
+        return back_refs[j // 2][rows_at, at : at + LANES].astype(F32)
 
     def turn_back(which, scale):
         def some(i, sums):
@@ -974,7 +1006,7 @@
                 if which == 0:
                     d = dq_ref[at, part]
                 else:
-                    d = near_ref[at, part] + back_ref[at, part].astype(F32)
+                    d = near_ref[at, part] + back(0, j, at)
                 d = (d * cosine - swap_halves(d) * sine) * scale
                 r = lax.rsqrt(head_mean(u * u) + NORM_EPS)
                 w = d * gain_ref[which : which + 1]
@@ -996,11 +1028,13 @@
 
     @pl.when(step == OUT_PARTS + 3)
     def _():
-        part_ref[...] = (near_ref[...] + back_ref[...].astype(F32)).astype(BF16)
+        for j in range(4):
+            part = slice(j * LANES, (j + 1) * LANES)
+            part_ref[:, part] = (near_ref[:, part] + back(1, j, slice(None))).astype(BF16)
 
     def compute(p):
         shape = (2,) + total_1.shape[1:]
-        slot = lax.rem(p, 2)
+        slot = lax.rem(p, 3)
 
         @pl.when(p < OUT_PARTS)
         def _():
@@ -1082,16 +1116,15 @@
     return pl.pallas_call(
         exit_kernel,
         name="leave",
-        grid=(parts + 4,),
+        grid=(parts + 5,),
         in_specs=[
             block(rows, OUT_PARTS, 4),
             block(rows, OUT_PARTS, 2),
             block(rows, OUT_PARTS + 2, 2),
-            block(rows, OUT_PARTS + 2, 2),
             block(D, OUT_PARTS, 4),
             block(rows, 0, 2),
         ]
-        + [whole] * 8,
+        + [whole] * 10,
         out_specs=[whole] * 3,
         out_shape=[
             jax.ShapeDtypeStruct((rows, D), BF16),
@@ -1102,7 +1135,7 @@
             pltpu.VMEM((rows, 2 * width), BF16),
             pltpu.VMEM((rows, D), F32),
             pltpu.VMEM((8, LANES), F32),
-            pltpu.VMEM((2, 2, 2, xs, ys, *last), BF16),
+            pltpu.VMEM((3, 2, 2, xs, ys, *last), BF16),
             pltpu.VMEM((2, xs, ys, *last), BF16),
             [pltpu.VMEM((ys, *last), BF16), pltpu.VMEM((xs, *last), BF16)],
             pltpu.VMEM((2, *last), BF16),
@@ -1120,7 +1153,7 @@
             collective_id=number, has_side_effects=True, vmem_limit_bytes=56 << 20
         ),
         cost_estimate=pl.CostEstimate(flops=rows << 20, transcendentals=0, bytes_accessed=rows << 10),
-    )(raw, dq, near, back, w, d_attn, mixed_rows, at, gains, cosine, sine, x, norm_gains, second)
+    )(raw, dq, near, w, d_attn, *back, mixed_rows, at, gains, cosine, sine, x, norm_gains, second)
 
 
 def add_swapped(keep, send, direction):
@@ -1200,12 +1233,14 @@
     else:
         others = [lax.all_gather(p, "seq", axis=0, tiled=True) for p in own]
     w_down = gather(after(down_master.astype(BF16), others[3]))
+    hot_x = relative_rows("cxyz", D)
+    first_rows = transpose_in_order(hot_x, normed_first)
+    q = after(q, first_rows)
     mixed, lse = attend(q, others, own, low, first_wide)
     x_mid = x + jnp.dot(mixed, w_out, preferred_element_type=F32)
     scale_second = rms_scale(x_mid)
     normed_second = (x_mid * scale_second * norm_gains[1]).astype(BF16)
     g = cotangent[0]
-    hot_x = relative_rows("cxyz", D)
     shards = jnp.stack([gate_up_master[:, :FF], gate_up_master[:, FF:]]).astype(BF16)
     out_sum, d_b, grad_down, gate_up_sums = feed(
         after(shards, normed_second),
@@ -1222,14 +1257,17 @@
     d_mid = g.astype(F32) + d_norm
     d_attn = d_mid.astype(BF16)
     d_mixed = dot_cols(d_attn, w_out).astype(BF16)
-    zero = jnp.zeros((rows, QUERY_FEATURES), F32)
-    dq, far = attend_back(0, q, d_mixed, mixed, lse, zero, others, low, first_lane, BF16)
-    if seq_width == 2:
-        back = lax.ppermute(far, "seq", [(1, 0)])
-    else:
-        back = lax.psum_scatter(far, "seq", scatter_dimension=0, tiled=True)
+    far, back = [], []
+    for pieces in ((0, 1), (2, 3)):
+        far.append(attend_back(0, pieces, q, d_mixed, mixed, lse, [], others, low, first_lane, BF16))
+        d_keys = far[-1][1]
+        if seq_width == 2:
+            back.append(lax.ppermute(d_keys, "seq", [(1, 0)]))
+        else:
+            back.append(lax.psum_scatter(d_keys, "seq", scatter_dimension=0, tiled=True))
+    befores = [dq for dq, _ in far]
     dq, near = attend_back(
-        others[0].shape[0], q, d_mixed, mixed, lse, dq, own, low, first_lane, F32
+        others[0].shape[0], range(4), q, d_mixed, mixed, lse, befores, own, low, first_lane, F32
     )
     d_x, sums, gain_sums = leave(
         raw,
@@ -1238,8 +1276,8 @@
         back,
         w_qkv,
         d_attn,
-        transpose_in_order(hot_x, mixed),
-        transpose_in_order(hot_x, normed_first),
+        transpose_in_order(hot_x, after(mixed, befores)),
+        first_rows,
         gain_rows,
         cosine,
         sine,

time: 614 us -> 589 us (0.959)
  Pallas kernels: 433 us -> 419 us
  waiting for transfers between devices: 66.4 us -> 53.4 us
    pallas_call x4 -> x5, Pallas kernels: 359 us -> 340 us  [the longest x1 197 us: feed(): pl.pallas_call(feed_kernel, name='feed', grid=(parts + FEED_LEAD + 4 * SL...]
  transfers between devices with their start and end apart: 7 -> 8, of which waited for: 6 -> 5; matrix products, arithmetic and copies ran while one was open for 8% -> 9% of each run, Pallas kernels for 28% -> 29%
where the time goes in v6:
time: 589 us; the launch traced here: 579 us
  Pallas kernels  419 us (71%)
  waiting for transfers between devices  53.4 us (9%)
  other arithmetic  41.6 us (7%)
  matrix products  28.2 us (5%)
  between operations  14.9 us (3%)
  starting transfers between devices  13.8 us (2%)
  local copies, waits for them, and re-layouts  8.6 us (1%)
    pallas_call x1, Pallas kernels, feed(): pl.pallas_call(feed_kernel, name='feed', grid=(parts + FEED_LEAD + 4 * SL...  197 us
    pallas_call x1, Pallas kernels, leave(): pl.pallas_call(exit_kernel, name='leave', grid=(parts + 5,), in_specs=[bl...  76.2 us
    pallas_call x3, Pallas kernels, attend_back(): pl.pallas_call(functools.partial(attend_back_kernel, start, pieces, len(b...  66.2 us
    ppermute x4, waiting for transfers between devices, per_device(): others = [lax.ppermute(p, 'seq', [(0, 1)]) for p in own]  45 us
    pallas_call x1, Pallas kernels, gather_all(): pl.pallas_call(functools.partial(gather_kernel, plan), name='gather_all',...  44.6 us
    pallas_call x1, Pallas kernels, attend(): pl.pallas_call(attend_kernel, name='attend', grid_spec=pltpu.PrefetchScal...  26.1 us
    dot_general x4, matrix products, dot_cols(): lax.dot_general(a, b, (((1,), (1,)), ((), ())), preferred_element_type=F32)  15 us
    sub x6, other arithmetic, adam_update(): master - rate * (corrected + decay * master)  13.7 us
  transfers between devices with their start and end apart: 8, of which 5 were waited for; matrix products, arithmetic and copies ran while one was open for 9% of the time, Pallas kernels for 29%

profile of v6, /device:TPU:0, one launch (start us, length us, event | category | flops | bytes accessed | tf_op | source)
XLA Modules:
  0.0 579.2 jit_solution(893123219117567424)
XLA Ops:
  8.1 2.1 fusion
  12.0 3.0 fusion.26
  14.9 44.6 %gather_all.1 = (bf16[4,2,2,2,32,2048]{5,4,3,2,1,0:T(8,128)(2,1)}, bf16[4,2,2,2,32,1024]{5,4,3,2,1,0:T(8,128)(2,1)}) custom-call(bf16[32,2048]{1,0:T(8,128)(2,1)} %convert_element_type.70.refs_0_, bf16[32,1024]{1,0:T(8,128)(2,1)} %convert_element_type.71.refs_1_), custom_call_target="tpu_custom_call" | custom-call | tf_op jit(solution)/shard_map/gather_all/pallas_call | solution.py:517
  60.2 3.7 pad_maximum_fusion.1
  63.9 9.1 %fusion.7.raw_ref = f32[1024,2048]{1,0:T(8,128)} fusion(bf16[1024,2048]{1,0:T(8,128)(2,1)} %bitcast.40, bf16[1,1024,1024]{2,1,0:T(8,128)(2,1)S(1)} %copy-done.6, f32[1024]{0:T(1024)S(1)} %bitcast.46, f32[1024]{0:T(1024)S(1)} %add_rsqrt_fusion.1), kind=kOutput, calls=%fused_computation.18 | convolution fusion | flops 4299161600 | bytes 14688256 | tf_op jit(solution)/shard_map/dot_general | solution.py:1228
  73.0 8.2 %prep.1 = (bf16[1024,1024]{1,0:T(8,128)(2,1)}, bf16[1024,256]{1,0:T(8,128)(2,1)}, bf16[1024,256]{1,0:T(8,128)(2,1)}, bf16[1024,256]{1,0:T(8,128)(2,1)}, bf16[1024,256]{1,0:T(8,128)(2,1)}) custom-call(f32[1024,2048]{1,0:T(8,128)} %fusion.7.raw_ref, f32[8,128]{1,0:T(8,128)} %pad.8.gain_ref.rest_4_, f32[1024,128]{1,0:T(8,128)} %get-tuple-element.103.cos_ref.rest_5_, ...), custom_call_target="tpu_custom_call" | custom-call | flops 83886080 | bytes 12582912 | tf_op jit(solution)/shard_map/prep/pallas_call | solution.py:92
  81.2 1.9 collective-permute-start.3
  83.9 11.3 %collective-permute-done.3.rest_3_.rest_1_ = bf16[1024,256]{1,0:T(8,128)(2,1)S(1)} collective-permute-done((bf16[1024,256]{1,0:T(8,128)(2,1)}, bf16[1024,256]{1,0:T(8,128)(2,1)S(1)}, u32[]{:S(2)}, u32[]{:S(2)}) %collective-permute-start.3) | collective-permute-done | bytes 524320 | tf_op jit(solution)/shard_map/ppermute | solution.py:1232
  95.3 5.1 collective-permute-start
  100.4 2.1 collective-permute-start.1
  102.4 2.1 collective-permute-start.2
  104.6 3.9 fusion.17.rest_3_
  110.1 4.2 collective-permute-done.rest_0_
  114.3 11.3 %collective-permute-done.1.rest_1_ = bf16[1024,256]{1,0:T(8,128)(2,1)} collective-permute-done((bf16[1024,256]{1,0:T(8,128)(2,1)}, bf16[1024,256]{1,0:T(8,128)(2,1)}, u32[]{:S(2)}, u32[]{:S(2)}) %collective-permute-start.1) | collective-permute-done | bytes 524320 | tf_op jit(solution)/shard_map/ppermute | solution.py:1232
  125.7 18.2 %collective-permute-done.2.rest_2_.rest_0_ = bf16[1024,256]{1,0:T(8,128)(2,1)} collective-permute-done((bf16[1024,256]{1,0:T(8,128)(2,1)}, bf16[1024,256]{1,0:T(8,128)(2,1)}, u32[]{:S(2)}, u32[]{:S(2)}) %collective-permute-start.2) | collective-permute-done | bytes 524320 | tf_op jit(solution)/shard_map/ppermute | solution.py:1232
  144.9 26.1 %attend.1 = (bf16[1024,1024]{1,0:T(8,128)(2,1)}, f32[64,2048]{1,0:T(8,128)}) custom-call(s32[9]{0:T(128)} %pad_add_fusion.low_ref, s32[1024,128]{1,0:T(8,128)} %broadcast_in_dim.30.first_ref, bf16[1024,1024]{1,0:T(8,128)(2,1)} %get-tuple-element.48.q_ref, bf16[1024,256]{1,0:T(8,128)(2,1)} %collective-permute-done.rest_0_, ...), custom_call_target="tpu_custom_call" | custom-call | flops 25769803776 | bytes 16777216 | tf_op jit(solution)/shard_map/attend/pallas_call | solution.py:180
  171.0 4.1 multiply_reduce_fusion.2
  177.1 3.8 fusion.20.at_ref
  180.8 8.3 %all-gather.2.cloned.1.call-done.wd_ref = bf16[4608,1024]{1,0:T(8,128)(2,1)} async-done(((bf16[144,1024]{1,0:T(8,128)(2,1)}), bf16[4608,1024]{1,0:T(8,128)(2,1)}) %all-gather.2.cloned.1.call-update) | async-done | bytes 9437200 | tf_op jit(solution)/shard_map/all_gather | solution.py:370
  189.2 197.4 %feed.1 = (bf16[2,4,2,2,2,32,4608]{6,5,4,3,2,1,0:T(8,128)(2,1)}, f32[1024,1024]{1,0:T(8,128)}, f32[1024,1024]{1,0:T(8,128)}, bf16[4608,1024]{1,0:T(8,128)(2,1)}, f32[32,9216]{1,0:T(8,128)}) custom-call(bf16[2,32,4608]{2,1,0:T(8,128)(2,1)} %pad_maximum_fusion.shard_ref, bf16[1024,1024]{1,0:T(8,128)(2,1)} %copy-done.11, bf16[1024,1024]{1,0:T(8,128)(2,1)} %fusion.20.at_ref, ...), custom_call_target="tpu_custom_call" | custom-call | flops 86973087744 | bytes 56623104 | tf_op jit(solution)/shard_map/feed/pallas_call | solution.py:800
  387.9 4.9 multiply_reduce_fusion
  396.0 3.7 convolution_convert_fusion.do_ref
  400.3 8.6 %attend_back.4 = (bf16[1024,512]{1,0:T(8,128)(2,1)}, f32[1024,512]{1,0:T(8,128)}) custom-call(s32[9]{0:T(128)} %pad_add_fusion.low_ref, s32[8,1024]{1,0:T(8,128)} %broadcast_in_dim.56.first_ref, bf16[1024,1024]{1,0:T(8,128)(2,1)} %get-tuple-element.48.q_ref, bf16[1024,1024]{1,0:T(8,128)(2,1)} %convolution_convert_fusion.do_ref, ...), custom_call_target="tpu_custom_call" | custom-call | flops 268435456 | bytes 262144 | tf_op jit(solution)/shard_map/attend_back/pallas_call | solution.py:296
  410.2 8.6 %attend_back.3 = (bf16[1024,512]{1,0:T(8,128)(2,1)}, f32[1024,512]{1,0:T(8,128)}) custom-call(s32[9]{0:T(128)} %pad_add_fusion.low_ref, s32[8,1024]{1,0:T(8,128)} %broadcast_in_dim.56.first_ref, bf16[1024,1024]{1,0:T(8,128)(2,1)} %get-tuple-element.48.q_ref, bf16[1024,1024]{1,0:T(8,128)(2,1)} %convolution_convert_fusion.do_ref, ...), custom_call_target="tpu_custom_call" | custom-call | flops 268435456 | bytes 262144 | tf_op jit(solution)/shard_map/attend_back/pallas_call | solution.py:296
  420.1 4.5 multiply_subtract_fusion
  424.6 49.0 %attend_back.5 = (f32[1024,1024]{1,0:T(8,128)}, f32[1024,1024]{1,0:T(8,128)}) custom-call(s32[9]{0:T(128)} %pad_add_fusion.low_ref, s32[8,1024]{1,0:T(8,128)} %broadcast_in_dim.56.first_ref, bf16[1024,1024]{1,0:T(8,128)(2,1)} %get-tuple-element.48.q_ref, bf16[1024,1024]{1,0:T(8,128)(2,1)} %convolution_convert_fusion.do_ref, ...), custom_call_target="tpu_custom_call" | custom-call | flops 268435456 | bytes 262144 | tf_op jit(solution)/shard_map/attend_back/pallas_call | solution.py:296
  473.5 4.0 convert_bitcast_fusion
  477.5 3.7 fusion.21.rest_2_
  481.9 76.2 %leave.1 = (bf16[1024,1024]{1,0:T(8,128)(2,1)}, f32[32,3072]{1,0:T(8,128)}, f32[8,1024]{1,0:T(8,128)}) custom-call(f32[1024,2048]{1,0:T(8,128)} %fusion.7.raw_ref, f32[1024,1024]{1,0:T(8,128)} %get-tuple-element.62.dq_ref, f32[1024,1024]{1,0:T(8,128)} %get-tuple-element.63.near_ref, bf16[1024,2048]{1,0:T(8,128)(2,1)} %bitcast.41, ...), custom_call_target="tpu_custom_call" | custom-call | flops 1073741824 | bytes 1048576 | tf_op jit(solution)/shard_map/leave/pallas_call | solution.py:1116
  562.8 1.9 multiply_subtract_fusion.2
  564.7 4.5 add_bitcast_fusion
  569.3 2.7 multiply_subtract_fusion.1
  (105 shorter events, 21.6 us)
Async XLA Ops:
  7.2 4.5 copy-start.25
  7.2 181.9 %all-gather.2.cloned.1.call-start = ((), (), s32[]{:S(2)}) async-start(), calls=%async_computation.1 | async-start | bytes 9732096 | tf_op jit(solution)/shard_map/all_gather | solution.py:370
  11.9 51.9 %copy-start.6 = (bf16[1,1024,1024]{2,1,0:T(8,128)(2,1)S(1)}, bf16[1,1024,1024]{2,1,0:T(8,128)(2,1)}, u32[]{:S(2)}) copy-start(bf16[1,1024,1024]{2,1,0:T(8,128)(2,1)} %param.21) | copy-start | bytes 6291460
  73.0 10.1 %copy-start.8 = (f32[144,1024]{1,0:T(8,128)S(1)}, f32[144,1024]{1,0:T(8,128)}, u32[]{:S(2)}) copy-start(f32[144,1024]{1,0:T(8,128)} %param.39) | copy-start | bytes 1769476
  81.2 14.0 %collective-permute-start.3 = (bf16[1024,256]{1,0:T(8,128)(2,1)}, bf16[1024,256]{1,0:T(8,128)(2,1)S(1)}, u32[]{:S(2)}, u32[]{:S(2)}) collective-permute-start(bf16[1024,256]{1,0:T(8,128)(2,1)} %get-tuple-element.52.rest_7_.rest_5_), channel_id=1, source_target_pairs={{0,1},{2,3},{4,5},{6,7},{8,9},{10,11},{12,13},{14,15},{16,17},{18,... | collective-permute-start | bytes 1572872 | tf_op jit(solution)/shard_map/ppermute | solution.py:1232
  95.2 9.4 %copy-start.15 = (bf16[1024,256]{1,0:T(8,128)(2,1)}, bf16[1024,256]{1,0:T(8,128)(2,1)S(1)}, u32[]{:S(2)}) copy-start(bf16[1024,256]{1,0:T(8,128)(2,1)S(1)} %collective-permute-done.3.rest_3_.rest_1_) | copy-start | bytes 1572868
  95.2 474.0 %reduce-scatter.2.cloned.1.call-start = ((), (), s32[]{:S(2)}) async-start(), calls=%async_computation.2 | async-start | bytes 9732096 | tf_op jit(solution)/shard_map/reduce_scatter | solution.py:1255
  95.3 19.0 %collective-permute-start = (bf16[1024,256]{1,0:T(8,128)(2,1)}, bf16[1024,256]{1,0:T(8,128)(2,1)}, u32[]{:S(2)}, u32[]{:S(2)}) collective-permute-start(bf16[1024,256]{1,0:T(8,128)(2,1)} %get-tuple-element.49.rest_4_.rest_2_), channel_id=1, source_target_pairs={{0,1},{2,3},{4,5},{6,7},{8,9},{10,11},{12,13},{14,15},{16,17},{18,... | collective-permute-start | bytes 1572872 | tf_op jit(solution)/shard_map/ppermute | solution.py:1232
  100.4 25.3 %collective-permute-start.1 = (bf16[1024,256]{1,0:T(8,128)(2,1)}, bf16[1024,256]{1,0:T(8,128)(2,1)}, u32[]{:S(2)}, u32[]{:S(2)}) collective-permute-start(bf16[1024,256]{1,0:T(8,128)(2,1)} %get-tuple-element.50.rest_5_.rest_3_), channel_id=1, source_target_pairs={{0,1},{2,3},{4,5},{6,7},{8,9},{10,11},{12,13},{14,15},{16,17},{18,... | collective-permute-start | bytes 1572872 | tf_op jit(solution)/shard_map/ppermute | solution.py:1232
  102.4 41.4 %collective-permute-start.2 = (bf16[1024,256]{1,0:T(8,128)(2,1)}, bf16[1024,256]{1,0:T(8,128)(2,1)}, u32[]{:S(2)}, u32[]{:S(2)}) collective-permute-start(bf16[1024,256]{1,0:T(8,128)(2,1)} %get-tuple-element.51.rest_6_.rest_4_), channel_id=1, source_target_pairs={{0,1},{2,3},{4,5},{6,7},{8,9},{10,11},{12,13},{14,15},{16,17},{18,... | collective-permute-start | bytes 1572872 | tf_op jit(solution)/shard_map/ppermute | solution.py:1232
  104.6 4.0 copy-start.7
  144.9 26.1 %copy-start.30 = (bf16[4,2,2,2,32,1024]{5,4,3,2,1,0:T(8,128)(2,1)S(1)}, bf16[4,2,2,2,32,1024]{5,4,3,2,1,0:T(8,128)(2,1)}, u32[]{:S(2)}) copy-start(bf16[4,2,2,2,32,1024]{5,4,3,2,1,0:T(8,128)(2,1)} %get-tuple-element.54) | copy-start | bytes 6291460
  386.6 6.2 %copy-start.4 = (bf16[1,1024,1024]{2,1,0:T(8,128)(2,1)S(1)}, bf16[1,1024,1024]{2,1,0:T(8,128)(2,1)}, u32[]{:S(2)}) copy-start(bf16[1,1024,1024]{2,1,0:T(8,128)(2,1)} %param.22) | copy-start | bytes 6291460
  387.9 5.0 copy-start.1
  387.9 6.4 %copy-start.2 = (f32[1024,1024]{1,0:T(8,128)S(1)}, f32[1024,1024]{1,0:T(8,128)}, u32[]{:S(2)}) copy-start(f32[1024,1024]{1,0:T(8,128)} %get-tuple-element.58) | copy-start | bytes 12582916
  408.9 72.4 %collective-permute-start.5 = (bf16[1024,512]{1,0:T(8,128)(2,1)}, bf16[1024,512]{1,0:T(8,128)(2,1)}, u32[]{:S(2)}, u32[]{:S(2)}) collective-permute-start(bf16[1024,512]{1,0:T(8,128)(2,1)} %get-tuple-element.65), channel_id=1, source_target_pairs={{1,0},{3,2},{5,4},{7,6},{9,8},{11,10},{13,12},{15,14},{17,16},{19,... | collective-permute-start | bytes 3145736 | tf_op jit(solution)/shard_map/ppermute | solution.py:1265
  418.8 62.4 %collective-permute-start.4 = (bf16[1024,512]{1,0:T(8,128)(2,1)}, bf16[1024,512]{1,0:T(8,128)(2,1)}, u32[]{:S(2)}, u32[]{:S(2)}) collective-permute-start(bf16[1024,512]{1,0:T(8,128)(2,1)} %get-tuple-element.64), channel_id=1, source_target_pairs={{1,0},{3,2},{5,4},{7,6},{9,8},{11,10},{13,12},{15,14},{17,16},{19,... | collective-permute-start | bytes 3145736 | tf_op jit(solution)/shard_map/ppermute | solution.py:1265
  473.5 4.0 copy-start.3
  481.8 76.3 %copy-start.26 = (f32[2,64]{1,0:T(2,128)S(1)}, f32[2,64]{1,0:T(2,128)}, u32[]{:S(2)}) copy-start(f32[2,64]{1,0:T(2,128)} %param.27) | copy-start | bytes 1540
  481.8 76.3 %copy-start.28 = (f32[2,64]{1,0:T(2,128)S(1)}, f32[2,64]{1,0:T(2,128)}, u32[]{:S(2)}) copy-start(f32[2,64]{1,0:T(2,128)} %param.28) | copy-start | bytes 1540
  481.9 76.3 %copy-start.29 = (f32[2,64]{1,0:T(2,128)S(1)}, f32[2,64]{1,0:T(2,128)}, u32[]{:S(2)}) copy-start(f32[2,64]{1,0:T(2,128)} %param.29) | copy-start | bytes 1540
  481.9 77.8 %copy-start.23 = (f32[2,1024]{1,0:T(2,128)S(1)}, f32[2,1024]{1,0:T(2,128)}, u32[]{:S(2)}) copy-start(f32[2,1024]{1,0:T(2,128)} %param.25) | copy-start | bytes 24580
  481.9 77.8 %copy-start.24 = (f32[2,1024]{1,0:T(2,128)S(1)}, f32[2,1024]{1,0:T(2,128)}, u32[]{:S(2)}) copy-start(f32[2,1024]{1,0:T(2,128)} %param.26) | copy-start | bytes 24580
  481.9 79.2 %copy-start.17 = (f32[32,1024]{1,0:T(8,128)S(1)}, f32[32,1024]{1,0:T(8,128)}, u32[]{:S(2)}) copy-start(f32[32,1024]{1,0:T(8,128)} %param.33) | copy-start | bytes 393220
  481.9 79.2 %copy-start.20 = (f32[32,1024]{1,0:T(8,128)S(1)}, f32[32,1024]{1,0:T(8,128)}, u32[]{:S(2)}) copy-start(f32[32,1024]{1,0:T(8,128)} %param.34) | copy-start | bytes 393220
  481.9 79.2 %copy-start.21 = (f32[32,1024]{1,0:T(8,128)S(1)}, f32[32,1024]{1,0:T(8,128)}, u32[]{:S(2)}) copy-start(f32[32,1024]{1,0:T(8,128)} %param.35) | copy-start | bytes 393220
  481.9 80.9 %copy-start.13 = (f32[32,2048]{1,0:T(8,128)S(1)}, f32[32,2048]{1,0:T(8,128)}, u32[]{:S(2)}) copy-start(f32[32,2048]{1,0:T(8,128)} %param.30) | copy-start | bytes 786436
  481.9 80.9 %copy-start.18 = (f32[32,2048]{1,0:T(8,128)S(1)}, f32[32,2048]{1,0:T(8,128)}, u32[]{:S(2)}) copy-start(f32[32,2048]{1,0:T(8,128)} %param.31) | copy-start | bytes 786436
  481.9 80.9 %copy-start.19 = (f32[32,2048]{1,0:T(8,128)S(1)}, f32[32,2048]{1,0:T(8,128)}, u32[]{:S(2)}) copy-start(f32[32,2048]{1,0:T(8,128)} %param.32) | copy-start | bytes 786436
  558.2 6.6 %copy-start.10 = (bf16[1024,1024]{1,0:T(8,128)(2,1)S(1)}, bf16[1024,1024]{1,0:T(8,128)(2,1)}, u32[]{:S(2)}) copy-start(bf16[1024,1024]{1,0:T(8,128)(2,1)} %get-tuple-element.67) | copy-start | bytes 6291460
  564.7 4.5 copy-start.9
  564.7 4.5 copy-start.14
  (8 other events, 22.0 us)
Sparse Core Ops, SparseCore 0:
  95.3 93.7 all-gather.1
  386.8 145.1 reduce-scatter.1

commit v7 on v6

--- a/solution.py
+++ b/solution.py
@@ -133,21 +133,24 @@
     return jnp.clip(begin, first, last), jnp.clip(end, first, last)
 
 
-def attend_kernel(low_ref, first_ref, q_ref, *rest):
-    sources = (rest[:PIECES], rest[PIECES : 2 * PIECES])
-    out_ref, lse_ref, queries, totals = rest[2 * PIECES :]
+def attend_kernel(start, last, low_ref, first_ref, q_ref, *rest):
+    befores, rest = (rest[:2], rest[2:]) if last else ((), rest)
+    refs = rest[:PIECES]
+    first_out, second_out, queries, totals = rest[PIECES:]
     turn = pl.program_id(0)
     block = q_ref.shape[0]
-    for p in range(PIECES):
-        queries[p] = stack_heads(q_ref[:, p * 2 * LANES : (p + 1) * 2 * LANES])
+    rows = refs[0].shape[0]
+    begin, end = key_range(low_ref, turn, block, start, rows)
     totals[...] = jnp.zeros_like(totals)
-    place = low_ref[0] + turn * block + lax.broadcasted_iota(jnp.int32, (block, KEY_BLOCK), 0)
-    first = jnp.concatenate([first_ref[...]] * (KEY_BLOCK // LANES), axis=1)
-    column = lax.broadcasted_iota(jnp.int32, (block, KEY_BLOCK), 1)
-    ones = jnp.ones((KEY_BLOCK, LANES), BF16)
-    start = 0
-    for refs in sources:
-        rows = refs[0].shape[0]
+
+    @pl.when(end > begin)
+    def _():
+        for p in range(PIECES):
+            queries[p] = stack_heads(q_ref[:, p * 2 * LANES : (p + 1) * 2 * LANES])
+        place = low_ref[0] + turn * block + lax.broadcasted_iota(jnp.int32, (block, KEY_BLOCK), 0)
+        first = jnp.concatenate([first_ref[...]] * (KEY_BLOCK // LANES), axis=1)
+        column = lax.broadcasted_iota(jnp.int32, (block, KEY_BLOCK), 1)
+        ones = jnp.ones((KEY_BLOCK, LANES), BF16)
 
         def step(at, _):
             span = pl.ds(pl.multiple_of(at * KEY_BLOCK - start, KEY_BLOCK), KEY_BLOCK)
@@ -161,46 +164,60 @@
                 totals[p] += dot(powers.reshape(4 * block, KEY_BLOCK), values)
             return 0
 
-        begin, end = key_range(low_ref, turn, block, start, rows)
         lax.fori_loop(begin, end, step, 0)
-        start += rows
+
     for p in range(PIECES):
-        mass = totals[p, :, LANES:]
-        mixed = totals[p, :, :LANES] / mass
-        out_ref[:, p * 2 * LANES : (p + 1) * 2 * LANES] = unstack_heads(mixed).astype(BF16)
-        lse_ref[:, p * 4 * block : (p + 1) * 4 * block] = jnp.transpose(jnp.log(mass))[0:8, :]
-
-
-def attend(q, others, own, low, first):
+        part = slice(p * 2 * LANES, (p + 1) * 2 * LANES)
+        mixed = unstack_heads(totals[p, :, :LANES])
+        mass = unstack_heads(totals[p, :, LANES:])
+        if not last:
+            first_out[:, part] = mixed
+            second_out[:, part] = mass
+            continue
+        mixed = mixed + befores[0][:, part]
+        mass = mass + befores[1][:, part]
+        first_out[:, part] = (mixed / mass).astype(BF16)
+        logs = jnp.transpose(jnp.log(mass))
+        heads = [logs[i * HEAD_SIZE : i * HEAD_SIZE + 8] for i in range(4)]
+        second_out[:, p * 4 * block : (p + 1) * 4 * block] = jnp.concatenate(heads, axis=1)
+
+
+def attend(start, q, befores, source, low, first):
     rows = q.shape[0]
     block = QUERY_BLOCK
     turns = rows // block
-    whole = lambda size: pl.BlockSpec((size, 2 * LANES), lambda t, low: (0, 0))
+    last = len(befores) > 0
     wide = pl.BlockSpec((block, QUERY_FEATURES), lambda t, low: (t, 0))
+    if last:
+        second = pl.BlockSpec((8, HQ * block), lambda t, low: (t, 0))
+        shapes = [
+            jax.ShapeDtypeStruct((rows, QUERY_FEATURES), BF16),
+            jax.ShapeDtypeStruct((8 * turns, HQ * block), F32),
+        ]
+    else:
+        second = wide
+        shapes = [jax.ShapeDtypeStruct((rows, QUERY_FEATURES), F32)] * 2
     return pl.pallas_call(
-        attend_kernel,
+        functools.partial(attend_kernel, start, last),
         name="attend",
         grid_spec=pltpu.PrefetchScalarGridSpec(
             num_scalar_prefetch=1,
             grid=(turns,),
             in_specs=[pl.BlockSpec((block, LANES), lambda t, low: (t, 0)), wide]
-            + [whole(others[0].shape[0])] * PIECES
-            + [whole(rows)] * PIECES,
-            out_specs=[wide, pl.BlockSpec((8, HQ * block), lambda t, low: (t, 0))],
+            + [wide] * len(befores)
+            + [pl.BlockSpec((source[0].shape[0], 2 * LANES), lambda t, low: (0, 0))] * PIECES,
+            out_specs=[wide, second],
             scratch_shapes=[
                 pltpu.VMEM((PIECES, 4 * block, LANES), BF16),
                 pltpu.VMEM((PIECES, 4 * block, 2 * LANES), F32),
             ],
         ),
-        out_shape=[
-            jax.ShapeDtypeStruct((rows, QUERY_FEATURES), BF16),
-            jax.ShapeDtypeStruct((8 * turns, HQ * block), F32),
-        ],
+        out_shape=shapes,
         compiler_params=params(),
         cost_estimate=pl.CostEstimate(
-            flops=rows * 1024 * 1024 * 24, transcendentals=rows * 1024 * 16, bytes_accessed=16 << 20
+            flops=rows * 1024 * 1024 * 12, transcendentals=rows * 1024 * 8, bytes_accessed=16 << 20
         ),
-    )(low, first, q, *others, *own)
+    )(low, first, q, *befores, *source)
 
 
 def attend_back_kernel(
@@ -1226,17 +1243,18 @@
     scale_first = rms_scale(x)
     normed_first = (x * scale_first * norm_gains[0]).astype(BF16)
     raw = jnp.dot(normed_first, w_qkv, preferred_element_type=F32)
+    w_down = gather(after(down_master.astype(BF16), raw))
     gain_rows = jnp.pad(jnp.tile(qk_gains, (1, 2)), ((0, 6), (0, 0)))
     q, *own = prep(raw, gain_rows, cosine, sine)
     if seq_width == 2:
         others = [lax.ppermute(p, "seq", [(0, 1)]) for p in own]
     else:
         others = [lax.all_gather(p, "seq", axis=0, tiled=True) for p in own]
-    w_down = gather(after(down_master.astype(BF16), others[3]))
     hot_x = relative_rows("cxyz", D)
     first_rows = transpose_in_order(hot_x, normed_first)
     q = after(q, first_rows)
-    mixed, lse = attend(q, others, own, low, first_wide)
+    sums = attend(others[0].shape[0], q, [], own, low, first_wide)
+    mixed, lse = attend(0, q, sums, others, low, first_wide)
     x_mid = x + jnp.dot(mixed, w_out, preferred_element_type=F32)
     scale_second = rms_scale(x_mid)
     normed_second = (x_mid * scale_second * norm_gains[1]).astype(BF16)

time: 589 us -> 579 us (0.983)
    ppermute x2, waiting for transfers between devices: 0.01 us -> 16.1 us  [per_device(): back.append(lax.ppermute(d_keys, 'seq', [(1, 0)]))]
    pallas_call x3, Pallas kernels: 66.2 us -> 51.2 us  [attend_back(): pl.pallas_call(functools.partial(attend_back_kernel, start, pieces, len(b...]
    ppermute x4, waiting for transfers between devices: 45 us -> 33.3 us  [per_device(): others = [lax.ppermute(p, 'seq', [(0, 1)]) for p in own]]
    pallas_call x1, Pallas kernels: 197 us -> 209 us  [feed(): pl.pallas_call(feed_kernel, name='feed', grid=(parts + FEED_LEAD + 4 * SL...]
    all_gather x1, waiting for transfers between devices: 8.34 us -> 0.01 us  [gather(): return lax.all_gather(shard, ALL, axis=0, tiled=True)]
    pallas_call x1 -> x2, Pallas kernels: 26.1 us -> 29.3 us  [attend(): pl.pallas_call(functools.partial(attend_kernel, start, last), name='atten...]
  transfers between devices with their start and end apart: 8 -> 8, of which waited for: 5 -> 3; matrix products, arithmetic and copies ran while one was open for 9% -> 10% of each run, Pallas kernels for 29% -> 29%
where the time goes in v7:
time: 579 us; the launch traced here: 573 us
  Pallas kernels  419 us (72%)
  waiting for transfers between devices  49.4 us (9%)
  other arithmetic  40.6 us (7%)
  matrix products  28.2 us (5%)
  between operations  14.6 us (3%)
  starting transfers between devices  11.9 us (2%)
  local copies, waits for them, and re-layouts  8.75 us (2%)
    pallas_call x1, Pallas kernels, feed(): pl.pallas_call(feed_kernel, name='feed', grid=(parts + FEED_LEAD + 4 * SL...  209 us
    pallas_call x1, Pallas kernels, leave(): pl.pallas_call(exit_kernel, name='leave', grid=(parts + 5,), in_specs=[bl...  77.4 us
    pallas_call x3, Pallas kernels, attend_back(): pl.pallas_call(functools.partial(attend_back_kernel, start, pieces, len(b...  51.2 us
    pallas_call x1, Pallas kernels, gather_all(): pl.pallas_call(functools.partial(gather_kernel, plan), name='gather_all',...  44.6 us
    ppermute x4, waiting for transfers between devices, per_device(): others = [lax.ppermute(p, 'seq', [(0, 1)]) for p in own]  33.3 us
    pallas_call x2, Pallas kernels, attend(): pl.pallas_call(functools.partial(attend_kernel, start, last), name='atten...  29.3 us
    ppermute x2, waiting for transfers between devices, per_device(): back.append(lax.ppermute(d_keys, 'seq', [(1, 0)]))  16.1 us
    dot_general x4, matrix products, dot_cols(): lax.dot_general(a, b, (((1,), (1,)), ((), ())), preferred_element_type=F32)  15 us
  transfers between devices with their start and end apart: 8, of which 3 were waited for; matrix products, arithmetic and copies ran while one was open for 10% of the time, Pallas kernels for 29%

profile of v7, /device:TPU:0, one launch (start us, length us, event | category | flops | bytes accessed | tf_op | source)
XLA Modules:
  0.0 572.9 jit_solution(15186991719483365729)
XLA Ops:
  8.2 2.1 fusion
  14.2 44.6 %gather_all.1 = (bf16[4,2,2,2,32,2048]{5,4,3,2,1,0:T(8,128)(2,1)}, bf16[4,2,2,2,32,1024]{5,4,3,2,1,0:T(8,128)(2,1)}) custom-call(bf16[32,2048]{1,0:T(8,128)(2,1)} %convert_element_type.70.refs_0_, bf16[32,1024]{1,0:T(8,128)(2,1)} %convert_element_type.71.refs_1_), custom_call_target="tpu_custom_call" | custom-call | tf_op jit(solution)/shard_map/gather_all/pallas_call | solution.py:534
  58.9 9.1 %fusion.7.raw_ref = f32[1024,2048]{1,0:T(8,128)} fusion(bf16[1024,2048]{1,0:T(8,128)(2,1)} %bitcast.40, bf16[1,1024,1024]{2,1,0:T(8,128)(2,1)S(1)} %copy-done.6, f32[1024]{0:T(1024)S(1)} %bitcast.46, f32[1024]{0:T(1024)S(1)} %add_rsqrt_fusion.1), kind=kOutput, calls=%fused_computation.18 | convolution fusion | flops 4299161600 | bytes 14688256 | tf_op jit(solution)/shard_map/dot_general | solution.py:1245
  69.1 1.9 fusion.26
  71.0 1.9 pad_maximum_fusion.1
  72.9 8.2 %prep.1 = (bf16[1024,1024]{1,0:T(8,128)(2,1)}, bf16[1024,256]{1,0:T(8,128)(2,1)}, bf16[1024,256]{1,0:T(8,128)(2,1)}, bf16[1024,256]{1,0:T(8,128)(2,1)}, bf16[1024,256]{1,0:T(8,128)(2,1)}) custom-call(f32[1024,2048]{1,0:T(8,128)} %fusion.7.raw_ref, f32[8,128]{1,0:T(8,128)} %pad.8.gain_ref.rest_4_, f32[1024,128]{1,0:T(8,128)} %get-tuple-element.107.cos_ref.rest_5_, ...), custom_call_target="tpu_custom_call" | custom-call | flops 83886080 | bytes 12582912 | tf_op jit(solution)/shard_map/prep/pallas_call | solution.py:92
  81.1 2.7 collective-permute-start
  83.8 2.1 collective-permute-start.1
  85.9 2.1 collective-permute-start.2
  88.0 2.3 collective-permute-start.3
  90.4 3.9 fusion.17.rest_3_
  96.0 18.3 %attend.2 = (f32[1024,1024]{1,0:T(8,128)}, f32[1024,1024]{1,0:T(8,128)}) custom-call(s32[9]{0:T(128)} %pad_add_fusion.low_ref, s32[1024,128]{1,0:T(8,128)} %broadcast_in_dim.30.first_ref, bf16[1024,1024]{1,0:T(8,128)(2,1)} %get-tuple-element.50.q_ref, bf16[1024,256]{1,0:T(8,128)(2,1)} %get-tuple-element.51.rest_0_.rest_2_, ...), custom_call_target="tpu_custom_call" | custom-call | flops 12884901888 | bytes 16777216 | tf_op jit(solution)/shard_map/attend/pallas_call | solution.py:200
  115.2 11.3 %collective-permute-done.2.rest_4_.rest_0_ = bf16[1024,256]{1,0:T(8,128)(2,1)} collective-permute-done((bf16[1024,256]{1,0:T(8,128)(2,1)}, bf16[1024,256]{1,0:T(8,128)(2,1)}, u32[]{:S(2)}, u32[]{:S(2)}) %collective-permute-start.2) | collective-permute-done | bytes 524320 | tf_op jit(solution)/shard_map/ppermute | solution.py:1250
  126.5 22.1 %collective-permute-done.3.rest_5_.rest_1_ = bf16[1024,256]{1,0:T(8,128)(2,1)} collective-permute-done((bf16[1024,256]{1,0:T(8,128)(2,1)}, bf16[1024,256]{1,0:T(8,128)(2,1)}, u32[]{:S(2)}, u32[]{:S(2)}) %collective-permute-start.3) | collective-permute-done | bytes 524320 | tf_op jit(solution)/shard_map/ppermute | solution.py:1250
  148.5 11.0 %attend.3 = (bf16[1024,1024]{1,0:T(8,128)(2,1)}, f32[64,2048]{1,0:T(8,128)}) custom-call(s32[9]{0:T(128)} %pad_add_fusion.low_ref, s32[1024,128]{1,0:T(8,128)} %broadcast_in_dim.30.first_ref, bf16[1024,1024]{1,0:T(8,128)(2,1)} %get-tuple-element.50.q_ref, f32[1024,1024]{1,0:T(8,128)} %get-tuple-element.55.rest_0_, f32[1024,1024]{1,0:T(8,128)} %get-tuple-element.56.rest_1_, ...), custom_call_target="tpu_custom_call" | custom-call | flops 12884901888 | bytes 16777216 | tf_op jit(solution)/shard_map/attend/pallas_call | solution.py:200
  159.5 4.1 multiply_reduce_fusion.2
  165.6 3.8 fusion.20.at_ref
  169.4 208.8 %feed.1 = (bf16[2,4,2,2,2,32,4608]{6,5,4,3,2,1,0:T(8,128)(2,1)}, f32[1024,1024]{1,0:T(8,128)}, f32[1024,1024]{1,0:T(8,128)}, bf16[4608,1024]{1,0:T(8,128)(2,1)}, f32[32,9216]{1,0:T(8,128)}) custom-call(bf16[2,32,4608]{2,1,0:T(8,128)(2,1)} %pad_maximum_fusion.shard_ref, bf16[1024,1024]{1,0:T(8,128)(2,1)} %copy-done.11, bf16[1024,1024]{1,0:T(8,128)(2,1)} %fusion.20.at_ref, ...), custom_call_target="tpu_custom_call" | custom-call | flops 86973087744 | bytes 56623104 | tf_op jit(solution)/shard_map/feed/pallas_call | solution.py:817
  379.5 4.9 multiply_reduce_fusion
  387.6 3.7 convolution_convert_fusion.do_ref
  391.9 8.5 %attend_back.4 = (bf16[1024,512]{1,0:T(8,128)(2,1)}, f32[1024,512]{1,0:T(8,128)}) custom-call(s32[9]{0:T(128)} %pad_add_fusion.low_ref, s32[8,1024]{1,0:T(8,128)} %broadcast_in_dim.56.first_ref, bf16[1024,1024]{1,0:T(8,128)(2,1)} %get-tuple-element.50.q_ref, bf16[1024,1024]{1,0:T(8,128)(2,1)} %convolution_convert_fusion.do_ref, ...), custom_call_target="tpu_custom_call" | custom-call | flops 268435456 | bytes 262144 | tf_op jit(solution)/shard_map/attend_back/pallas_call | solution.py:313
  401.7 8.6 %attend_back.3 = (bf16[1024,512]{1,0:T(8,128)(2,1)}, f32[1024,512]{1,0:T(8,128)}) custom-call(s32[9]{0:T(128)} %pad_add_fusion.low_ref, s32[8,1024]{1,0:T(8,128)} %broadcast_in_dim.56.first_ref, bf16[1024,1024]{1,0:T(8,128)(2,1)} %get-tuple-element.50.q_ref, bf16[1024,1024]{1,0:T(8,128)(2,1)} %convolution_convert_fusion.do_ref, ...), custom_call_target="tpu_custom_call" | custom-call | flops 268435456 | bytes 262144 | tf_op jit(solution)/shard_map/attend_back/pallas_call | solution.py:313
  411.6 4.5 multiply_subtract_fusion
  416.1 34.1 %attend_back.5 = (f32[1024,1024]{1,0:T(8,128)}, f32[1024,1024]{1,0:T(8,128)}) custom-call(s32[9]{0:T(128)} %pad_add_fusion.low_ref, s32[8,1024]{1,0:T(8,128)} %broadcast_in_dim.56.first_ref, bf16[1024,1024]{1,0:T(8,128)(2,1)} %get-tuple-element.50.q_ref, bf16[1024,1024]{1,0:T(8,128)(2,1)} %convolution_convert_fusion.do_ref, ...), custom_call_target="tpu_custom_call" | custom-call | flops 268435456 | bytes 262144 | tf_op jit(solution)/shard_map/attend_back/pallas_call | solution.py:313
  450.2 4.1 convert_bitcast_fusion
  454.3 3.7 fusion.21.rest_2_
  458.0 16.1 %collective-permute-done.4.rest_0_ = bf16[1024,512]{1,0:T(8,128)(2,1)} collective-permute-done((bf16[1024,512]{1,0:T(8,128)(2,1)}, bf16[1024,512]{1,0:T(8,128)(2,1)}, u32[]{:S(2)}, u32[]{:S(2)}) %collective-permute-start.4) | collective-permute-done | bytes 1048608 | tf_op jit(solution)/shard_map/ppermute | solution.py:1283
  474.8 77.4 %leave.1 = (bf16[1024,1024]{1,0:T(8,128)(2,1)}, f32[32,3072]{1,0:T(8,128)}, f32[8,1024]{1,0:T(8,128)}) custom-call(f32[1024,2048]{1,0:T(8,128)} %fusion.7.raw_ref, f32[1024,1024]{1,0:T(8,128)} %get-tuple-element.66.dq_ref, f32[1024,1024]{1,0:T(8,128)} %get-tuple-element.67.near_ref, bf16[1024,2048]{1,0:T(8,128)(2,1)} %bitcast.41, ...), custom_call_target="tpu_custom_call" | custom-call | flops 1073741824 | bytes 1048576 | tf_op jit(solution)/shard_map/leave/pallas_call | solution.py:1133
  555.1 1.7 multiply_subtract_fusion.3
  556.8 1.9 multiply_subtract_fusion.2
  558.7 4.5 add_bitcast_fusion
  563.3 2.7 multiply_subtract_fusion.1
  (100 shorter events, 22.0 us)
Async XLA Ops:
  7.2 51.6 %copy-start.6 = (bf16[1,1024,1024]{2,1,0:T(8,128)(2,1)S(1)}, bf16[1,1024,1024]{2,1,0:T(8,128)(2,1)}, u32[]{:S(2)}) copy-start(bf16[1,1024,1024]{2,1,0:T(8,128)(2,1)} %param.21) | copy-start | bytes 6291460
  7.2 6.2 %copy-start.8 = (f32[144,1024]{1,0:T(8,128)S(1)}, f32[144,1024]{1,0:T(8,128)}, u32[]{:S(2)}) copy-start(f32[144,1024]{1,0:T(8,128)} %param.39) | copy-start | bytes 1769476
  7.2 162.2 %all-gather.2.cloned.1.call-start = ((), (), s32[]{:S(2)}) async-start(), calls=%async_computation.1 | async-start | bytes 9732096 | tf_op jit(solution)/shard_map/all_gather | solution.py:387
  58.8 9.2 %copy-start.24 = (s32[1,16]{1,0:T(1,128)S(1)}, s32[1,16]{1,0:T(1,128)}, u32[]{:S(2)}) copy-start(s32[1,16]{1,0:T(1,128)} %param.23) | copy-start | bytes 196
  58.8 9.5 %copy-start.22 = (f32[2,64]{1,0:T(2,128)S(1)}, f32[2,64]{1,0:T(2,128)}, u32[]{:S(2)}) copy-start(f32[2,64]{1,0:T(2,128)} %param.27) | copy-start | bytes 1540
  68.0 495.2 %reduce-scatter.2.cloned.1.call-start = ((), (), s32[]{:S(2)}) async-start(), calls=%async_computation.2 | async-start | bytes 9732096 | tf_op jit(solution)/shard_map/reduce_scatter | solution.py:1273
  81.1 34.1 %collective-permute-start = (bf16[1024,256]{1,0:T(8,128)(2,1)}, bf16[1024,256]{1,0:T(8,128)(2,1)}, u32[]{:S(2)}, u32[]{:S(2)}) collective-permute-start(bf16[1024,256]{1,0:T(8,128)(2,1)} %get-tuple-element.51.rest_0_.rest_2_), channel_id=1, source_target_pairs={{0,1},{2,3},{4,5},{6,7},{8,9},{10,11},{12,13},{14,15},{16,17},{18,... | collective-permute-start | bytes 1572872 | tf_op jit(solution)/shard_map/ppermute | solution.py:1250
  83.8 31.4 %collective-permute-start.1 = (bf16[1024,256]{1,0:T(8,128)(2,1)}, bf16[1024,256]{1,0:T(8,128)(2,1)}, u32[]{:S(2)}, u32[]{:S(2)}) collective-permute-start(bf16[1024,256]{1,0:T(8,128)(2,1)} %get-tuple-element.52.rest_1_.rest_3_), channel_id=1, source_target_pairs={{0,1},{2,3},{4,5},{6,7},{8,9},{10,11},{12,13},{14,15},{16,17},{18,... | collective-permute-start | bytes 1572872 | tf_op jit(solution)/shard_map/ppermute | solution.py:1250
  85.9 40.6 %collective-permute-start.2 = (bf16[1024,256]{1,0:T(8,128)(2,1)}, bf16[1024,256]{1,0:T(8,128)(2,1)}, u32[]{:S(2)}, u32[]{:S(2)}) collective-permute-start(bf16[1024,256]{1,0:T(8,128)(2,1)} %get-tuple-element.53.rest_2_.rest_4_), channel_id=1, source_target_pairs={{0,1},{2,3},{4,5},{6,7},{8,9},{10,11},{12,13},{14,15},{16,17},{18,... | collective-permute-start | bytes 1572872 | tf_op jit(solution)/shard_map/ppermute | solution.py:1250
  88.0 60.5 %collective-permute-start.3 = (bf16[1024,256]{1,0:T(8,128)(2,1)}, bf16[1024,256]{1,0:T(8,128)(2,1)}, u32[]{:S(2)}, u32[]{:S(2)}) collective-permute-start(bf16[1024,256]{1,0:T(8,128)(2,1)} %get-tuple-element.54.rest_3_.rest_5_), channel_id=1, source_target_pairs={{0,1},{2,3},{4,5},{6,7},{8,9},{10,11},{12,13},{14,15},{16,17},{18,... | collective-permute-start | bytes 1572872 | tf_op jit(solution)/shard_map/ppermute | solution.py:1250
  90.4 4.0 copy-start.7
  148.5 11.0 %copy-start.27 = (bf16[4,2,2,2,32,1024]{5,4,3,2,1,0:T(8,128)(2,1)S(1)}, bf16[4,2,2,2,32,1024]{5,4,3,2,1,0:T(8,128)(2,1)}, u32[]{:S(2)}) copy-start(bf16[4,2,2,2,32,1024]{5,4,3,2,1,0:T(8,128)(2,1)} %get-tuple-element.58) | copy-start | bytes 6291460
  378.2 6.2 %copy-start.4 = (bf16[1,1024,1024]{2,1,0:T(8,128)(2,1)S(1)}, bf16[1,1024,1024]{2,1,0:T(8,128)(2,1)}, u32[]{:S(2)}) copy-start(bf16[1,1024,1024]{2,1,0:T(8,128)(2,1)} %param.22) | copy-start | bytes 6291460
  379.5 5.0 copy-start.1
  379.5 6.4 %copy-start.2 = (f32[1024,1024]{1,0:T(8,128)S(1)}, f32[1024,1024]{1,0:T(8,128)}, u32[]{:S(2)}) copy-start(f32[1024,1024]{1,0:T(8,128)} %get-tuple-element.62) | copy-start | bytes 12582916
  400.5 57.5 %collective-permute-start.5 = (bf16[1024,512]{1,0:T(8,128)(2,1)}, bf16[1024,512]{1,0:T(8,128)(2,1)}, u32[]{:S(2)}, u32[]{:S(2)}) collective-permute-start(bf16[1024,512]{1,0:T(8,128)(2,1)} %get-tuple-element.69), channel_id=1, source_target_pairs={{1,0},{3,2},{5,4},{7,6},{9,8},{11,10},{13,12},{15,14},{17,16},{19,... | collective-permute-start | bytes 3145736 | tf_op jit(solution)/shard_map/ppermute | solution.py:1283
  410.3 63.7 %collective-permute-start.4 = (bf16[1024,512]{1,0:T(8,128)(2,1)}, bf16[1024,512]{1,0:T(8,128)(2,1)}, u32[]{:S(2)}, u32[]{:S(2)}) collective-permute-start(bf16[1024,512]{1,0:T(8,128)(2,1)} %get-tuple-element.68), channel_id=1, source_target_pairs={{1,0},{3,2},{5,4},{7,6},{9,8},{11,10},{13,12},{15,14},{17,16},{19,... | collective-permute-start | bytes 3145736 | tf_op jit(solution)/shard_map/ppermute | solution.py:1283
  450.2 4.1 copy-start.3
  474.7 77.5 %copy-start.23 = (f32[2,64]{1,0:T(2,128)S(1)}, f32[2,64]{1,0:T(2,128)}, u32[]{:S(2)}) copy-start(f32[2,64]{1,0:T(2,128)} %param.27) | copy-start | bytes 1540
  474.7 77.5 %copy-start.25 = (f32[2,64]{1,0:T(2,128)S(1)}, f32[2,64]{1,0:T(2,128)}, u32[]{:S(2)}) copy-start(f32[2,64]{1,0:T(2,128)} %param.28) | copy-start | bytes 1540
  474.7 77.5 %copy-start.26 = (f32[2,64]{1,0:T(2,128)S(1)}, f32[2,64]{1,0:T(2,128)}, u32[]{:S(2)}) copy-start(f32[2,64]{1,0:T(2,128)} %param.29) | copy-start | bytes 1540
  474.7 79.0 %copy-start.20 = (f32[2,1024]{1,0:T(2,128)S(1)}, f32[2,1024]{1,0:T(2,128)}, u32[]{:S(2)}) copy-start(f32[2,1024]{1,0:T(2,128)} %param.25) | copy-start | bytes 24580
  474.7 79.0 %copy-start.21 = (f32[2,1024]{1,0:T(2,128)S(1)}, f32[2,1024]{1,0:T(2,128)}, u32[]{:S(2)}) copy-start(f32[2,1024]{1,0:T(2,128)} %param.26) | copy-start | bytes 24580
  474.7 80.4 %copy-start.14 = (f32[32,1024]{1,0:T(8,128)S(1)}, f32[32,1024]{1,0:T(8,128)}, u32[]{:S(2)}) copy-start(f32[32,1024]{1,0:T(8,128)} %param.33) | copy-start | bytes 393220
  474.7 80.4 %copy-start.17 = (f32[32,1024]{1,0:T(8,128)S(1)}, f32[32,1024]{1,0:T(8,128)}, u32[]{:S(2)}) copy-start(f32[32,1024]{1,0:T(8,128)} %param.34) | copy-start | bytes 393220
  474.7 80.4 %copy-start.18 = (f32[32,1024]{1,0:T(8,128)S(1)}, f32[32,1024]{1,0:T(8,128)}, u32[]{:S(2)}) copy-start(f32[32,1024]{1,0:T(8,128)} %param.35) | copy-start | bytes 393220
  474.7 82.1 %copy-start.12 = (f32[32,2048]{1,0:T(8,128)S(1)}, f32[32,2048]{1,0:T(8,128)}, u32[]{:S(2)}) copy-start(f32[32,2048]{1,0:T(8,128)} %param.30) | copy-start | bytes 786436
  474.7 82.1 %copy-start.15 = (f32[32,2048]{1,0:T(8,128)S(1)}, f32[32,2048]{1,0:T(8,128)}, u32[]{:S(2)}) copy-start(f32[32,2048]{1,0:T(8,128)} %param.31) | copy-start | bytes 786436
  474.7 82.0 %copy-start.16 = (f32[32,2048]{1,0:T(8,128)S(1)}, f32[32,2048]{1,0:T(8,128)}, u32[]{:S(2)}) copy-start(f32[32,2048]{1,0:T(8,128)} %param.32) | copy-start | bytes 786436
  552.1 6.6 %copy-start.10 = (bf16[1024,1024]{1,0:T(8,128)(2,1)S(1)}, bf16[1024,1024]{1,0:T(8,128)(2,1)}, u32[]{:S(2)}) copy-start(bf16[1024,1024]{1,0:T(8,128)(2,1)} %get-tuple-element.71) | copy-start | bytes 6291460
  558.7 4.5 copy-start.9
  558.7 4.5 copy-start.13
  (5 other events, 11.9 us)
Sparse Core Ops, SparseCore 0:
  68.1 90.8 all-gather.1
  378.3 143.9 reduce-scatter.1
